TPU v7x, 32 devices: a whole 2x2x4 slice. The times are simulated.
32 devices in a mesh: dp: 8 (over z, y), inner: 4 (over x, core).
Axes of the slice: x: 2, y: 2, z: 4, core: 2. Of those that a mesh axis runs over, the one named last changes fastest.
Arguments:
- tokens: bfloat16 [32768, 512], P(('dp', 'inner')), may hold values from -6 to 6
- segments: int32 [32768], P(('dp', 'inner')), may hold values from 0 to 32767, as said below
- positions: int32 [32768], P(('dp', 'inner')), may hold values from 0 to 1023, as said below
- cotangent: bfloat16 [32768, 512], P(('dp', 'inner')), may hold values from -6 to 6
- attn_weight: float32 [4, 512, 512], P(None, ('dp', 'inner')), may hold values from -0.53033009 to 0.53033009
- attn_m: float32 [4, 512, 512], P(None, ('dp', 'inner')), may hold values from -0.0007324219 to 0.0007324219
- attn_v: float32 [4, 512, 512], P(None, ('dp', 'inner')), may hold values from 1.0882435e-09 to 4.352974e-09
- gate_weight: float32 [2, 512, 512], P(None, ('dp', 'inner')), may hold values from -0.25 to 0.25
- gate_m: float32 [2, 512, 512], P(None, ('dp', 'inner')), may hold values from -0.00036621094 to 0.00036621094
- gate_v: float32 [2, 512, 512], P(None, ('dp', 'inner')), may hold values from 2.7206087e-10 to 1.0882435e-09
- in_weight: float32 [512, 2048], P(('dp', 'inner')), may hold values from -0.25 to 0.25
- in_m: float32 [512, 2048], P(('dp', 'inner')), may hold values from -0.00036621094 to 0.00036621094
- in_v: float32 [512, 2048], P(('dp', 'inner')), may hold values from 2.7206087e-10 to 1.0882435e-09
- out_weight: float32 [2048, 512], P(('dp', 'inner')), may hold values from -0.125 to 0.125
- out_m: float32 [2048, 512], P(('dp', 'inner')), may hold values from -0.00036621094 to 0.00036621094
- out_v: float32 [2048, 512], P(('dp', 'inner')), may hold values from 2.7206087e-10 to 1.0882435e-09
- norm_params: float32 [7, 512], P(None, ('dp', 'inner'))
- norm_m: float32 [7, 512], P(None, ('dp', 'inner')), may hold values from -0.0014648438 to 0.0014648438
- norm_v: float32 [7, 512], P(None, ('dp', 'inner')), may hold values from 4.352974e-09 to 1.7411896e-08
- in_bias: float32 [2048], P(('dp', 'inner')), may hold values from -1.75 to 1.75
- bias_m: float32 [2048], P(('dp', 'inner')), may hold values from -0.00024414062 to 0.00024414062
- bias_v: float32 [2048], P(('dp', 'inner')), may hold values from 1.7411896e-10 to 7.073583e-10
Outputs:
- layer_out: bfloat16 [32768, 512], P(('dp', 'inner'))
- input_grad: bfloat16 [32768, 512], P(('dp', 'inner'))
- grad_norm: float32 [], replicated
- attn_new: float32 [4, 512, 512], P(None, ('dp', 'inner'))
- attn_m_new: float32 [4, 512, 512], P(None, ('dp', 'inner'))
- attn_v_new: float32 [4, 512, 512], P(None, ('dp', 'inner'))
- gate_new: float32 [2, 512, 512], P(None, ('dp', 'inner'))
- gate_m_new: float32 [2, 512, 512], P(None, ('dp', 'inner'))
- gate_v_new: float32 [2, 512, 512], P(None, ('dp', 'inner'))
- in_new: float32 [512, 2048], P(('dp', 'inner'))
- in_m_new: float32 [512, 2048], P(('dp', 'inner'))
- in_v_new: float32 [512, 2048], P(('dp', 'inner'))
- out_new: float32 [2048, 512], P(('dp', 'inner'))
- out_m_new: float32 [2048, 512], P(('dp', 'inner'))
- out_v_new: float32 [2048, 512], P(('dp', 'inner'))
- norm_new: float32 [7, 512], P(None, ('dp', 'inner'))
- norm_m_new: float32 [7, 512], P(None, ('dp', 'inner'))
- norm_v_new: float32 [7, 512], P(None, ('dp', 'inner'))
- bias_new: float32 [2048], P(('dp', 'inner'))
- bias_m_new: float32 [2048], P(('dp', 'inner'))
- bias_v_new: float32 [2048], P(('dp', 'inner'))
Inputs may be any that keep to these rules, and one draw needn't show every extreme that they name: `segments`: a token's segment number is the index of its document's first token, so segment numbers never fall; a new document begins at every sequence start (every 1024 tokens); the first sequence is one document; the last token forms a document of its own. positions restart at 0 with every new segment number.
All inputs are finite; a program needn't handle non-finite values.
Results may differ from a plain program's by a relative error of at most 0.033.
The roundings to bfloat16 on the way count: a program that leaves them out, or rounds other values in their place, can miss the bound.
Values may be sent and summed in bfloat16 or wider, within the bound.
No kernel may reach another device: no remote copies, remote signals or barrier semaphores. Data moves between devices by JAX's collectives and lax.ppermute only.
A program may use at most 192 MiB of HBM per device.

v0:
```python
import functools
import jax
import jax.numpy as jnp
from jax import lax
from jax.experimental import pallas as pl
from jax.experimental.pallas import tpu as pltpu
from jax.sharding import PartitionSpec as P

AXES = ("dp", "inner")
HEADS = 8
HEAD = 64
STEP = 10
LOG2E = 1.4426950408889634
BLOCK = 256


norm_eps = 1e-05
first_decay = 0.9
second_decay = 0.999
adam_eps = 1e-08
learn_rate = 0.05
vector_rate = 0.8
weight_decay = 0.1
clip_norm = 1.0
masked_score = -1e30


def normalize_parts(values, gain_row, bias_row):
    centred = values - jnp.mean(values, -1, keepdims=True)
    spread = jnp.mean(centred * centred, -1, keepdims=True)
    scale_row = lax.rsqrt(spread + norm_eps)
    unit_rows = centred * scale_row
    return (unit_rows * gain_row + bias_row, unit_rows, scale_row)


def normalize_back(grad_rows, unit_rows, scale_row, gain_row):
    grad_unit = grad_rows * gain_row
    return scale_row * (
        grad_unit
        - jnp.mean(grad_unit, -1, keepdims=True)
        - unit_rows * jnp.mean(grad_unit * unit_rows, -1, keepdims=True)
    )


def bit_groups(sizes):
    dp_bits = sizes["dp"].bit_length() - 1
    inner_bits = sizes["inner"].bit_length() - 1
    y_bits = dp_bits // 2
    plane_bits = (inner_bits - 1) + y_bits
    return (1, plane_bits, dp_bits - y_bits)


def swap_with(array, offset, count):
    return lax.ppermute(array, AXES, [(source, source ^ offset) for source in range(count)])


def stage_bits(groups):
    return ((0, groups[0]), (groups[0], groups[1]), (groups[0] + groups[1], groups[2]))


def gather_z(shard, groups):
    count = 2 ** sum(groups)
    first_bit, bits = stage_bits(groups)[2]
    return jnp.stack([shard] + [swap_with(shard, offset << first_bit, count) for offset in range(1, 2**bits)])


def gather_plane(column, groups):
    count = 2 ** sum(groups)
    first_bit, bits = stage_bits(groups)[1]
    return [swap_with(column, offset << first_bit, count) for offset in range(1, 2**bits)]


def gather_core(column, planes, groups):
    return swap_with(jnp.concatenate([column] + planes), 1, 2 ** sum(groups))


def offsets_of(groups):
    (_, _), (plane_bit, plane_bits), (z_bit, z_bits) = stage_bits(groups)
    table = [
        [(plane << plane_bit) | (z << z_bit) for z in range(2**z_bits)] for plane in range(2**plane_bits)
    ]
    return table + [[offset | 1 for row in table for offset in row]]


def plane_orders(groups):
    _, (first_bit, bits), _ = stage_bits(groups)
    order = list(range(first_bit, first_bit + bits))
    return order, order[bits // 2 :] + order[: bits // 2]


def z_offsets(groups):
    _, _, (first_bit, bits) = stage_bits(groups)
    return [z << first_bit for z in range(2**bits)]


def send_halves(arrays, orders, position, groups):
    count = 2 ** sum(groups)
    return [swap_with(array, 1 << order[position], count) for array, order in zip(arrays, orders)]


def join_halves(arrays, received, tables, orders, position):
    arrays = [jnp.concatenate(pair) for pair in zip(arrays, received)]
    tables = [
        table + [offset | (1 << order[position]) for offset in table] for table, order in zip(tables, orders)
    ]
    return arrays, tables


def vmem_spec():
    return pl.BlockSpec(memory_space=pltpu.VMEM)


def smem_spec():
    return pl.BlockSpec(memory_space=pltpu.SMEM)


def matrix_shape(kind, pieces, count, step, width):
    if kind == "stack":
        return (pieces, count, step, width)
    if kind == "rows":
        return (count, pieces, step, width)
    return (count, step, pieces * width)


def place_kernel(tables, layout, own_ref, *refs):
    parts = refs[: len(tables)]
    outs = refs[len(tables) :]
    own = own_ref[0]
    total = None
    where_to = [
        (index, kind, piece) for index, (kind, _, pieces) in enumerate(layout) for piece in range(pieces)
    ]
    for part, (row, first) in zip(parts, tables):
        width = part.shape[3]
        for entry, offset in enumerate(row):
            owner = own ^ offset
            for source in range(part.shape[1]):
                index, kind, piece = where_to[first + source]
                block = part[entry, source]
                if kind == "sum":
                    block = block.astype(jnp.float32)
                    total = block if total is None else total + block
                elif kind == "stack":
                    outs[index][piece, owner] = block
                elif kind == "rows":
                    outs[index][owner, piece] = block
                else:
                    outs[index][owner, :, piece * width : (piece + 1) * width] = block
    for index, (kind, _, _) in enumerate(layout):
        if kind == "sum":
            outs[index][...] = total


def place(own, parts, tables, layout, groups):
    count = 2 ** sum(groups)
    step, width = parts[0].shape[2:]
    if step % 16:
        firsts = sorted({first for _, first in tables})
        groups_of = []
        for first in firsts:
            chosen = [(part, row) for part, (row, base) in zip(parts, tables) if base == first]
            order = jnp.argsort(jnp.array([o for _, row in chosen for o in row]) ^ own)
            groups_of.append(jnp.concatenate([part for part, _ in chosen])[order])
        full = jnp.concatenate(groups_of, 1)
        result = []
        for kind, first, pieces in layout:
            chosen = full[:, first : first + pieces]
            if kind == "sum":
                result.append(jnp.sum(chosen.astype(jnp.float32), 0).reshape(pieces * step, width))
            elif kind == "stack":
                result.append(jnp.moveaxis(chosen, 0, 1))
            elif kind == "rows":
                result.append(chosen)
            else:
                result.append(jnp.moveaxis(chosen, 1, 2).reshape(count, step, pieces * width))
        return result
    shapes = [
        jax.ShapeDtypeStruct((step, width), jnp.float32)
        if kind == "sum"
        else jax.ShapeDtypeStruct(matrix_shape(kind, pieces, count, step, width), jnp.bfloat16)
        for kind, _, pieces in layout
    ]
    return pl.pallas_call(
        functools.partial(place_kernel, tables, layout),
        in_specs=[smem_spec()] + [vmem_spec() for _ in parts],
        out_specs=[vmem_spec() for _ in layout],
        out_shape=shapes,
        name="place",
    )(own[None].astype(jnp.int32), *parts)


def split_kernel(offsets, layout, own_ref, *refs):
    ins = refs[: len(layout)]
    kept, sent = refs[len(layout) :]
    own = own_ref[0]
    for entry, offset in enumerate(offsets):
        for side, target in enumerate((kept, sent)):
            owner = own ^ (offset | side)
            for index, (kind, first, pieces) in enumerate(layout):
                width = target.shape[3]
                for piece in range(pieces):
                    if kind == "sum":
                        block = ins[index][...]
                    elif kind == "stack":
                        block = ins[index][piece, owner]
                    elif kind == "rows":
                        block = ins[index][owner, piece]
                    else:
                        block = ins[index][owner, :, piece * width : (piece + 1) * width]
                    target[entry, first + piece] = block


def split(own, grads, layout, groups):
    count = 2 ** sum(groups)
    width = 512
    total = sum(pieces for _, _, pieces in layout)
    step = grads[0].shape[-2]
    offsets = [offset for row in offsets_of(groups)[:-1] for offset in row]
    if step % 16:
        pieces_of = []
        for grad, (kind, _, pieces) in zip(grads, layout):
            if kind == "sum":
                grad = jnp.broadcast_to(grad.reshape(1, pieces, step, width), (count, pieces, step, width))
            elif kind == "stack":
                grad = jnp.moveaxis(grad, 1, 0)
            elif kind == "columns":
                grad = jnp.moveaxis(grad.reshape(count, step, pieces, width), 2, 1)
            pieces_of.append(grad)
        full = jnp.concatenate(pieces_of, 1)
        order = jnp.array(offsets) ^ own
        return full[order], full[order ^ 1]
    shape = jax.ShapeDtypeStruct((len(offsets), total, step, width), jnp.bfloat16)
    return pl.pallas_call(
        functools.partial(split_kernel, offsets, layout),
        in_specs=[smem_spec()] + [vmem_spec() for _ in grads],
        out_specs=[vmem_spec(), vmem_spec()],
        out_shape=[shape, shape],
        name="split",
    )(own[None].astype(jnp.int32), *grads)


def plane_sums(kept, received, groups):
    _, (_, bits), (_, z_bits) = stage_bits(groups)
    shape = (2**bits, 2**z_bits) + kept.shape[1:]
    kept = kept.reshape(shape)
    received = received.reshape(shape)
    total = lambda offset: kept[offset].astype(jnp.float32) + received[offset].astype(jnp.float32)
    return total(0), [total(offset).astype(jnp.bfloat16) for offset in range(1, 2**bits)]


def plane_send(parts, groups):
    first_bit = stage_bits(groups)[1][0]
    return [swap_with(part, offset << first_bit, 2 ** sum(groups)) for offset, part in enumerate(parts, 1)]


def reduce_z(own_part, arrived, groups):
    count = 2 ** sum(groups)
    first_bit, bits = stage_bits(groups)[2]
    total = lambda z: own_part[z] + sum(part[z].astype(jnp.float32) for part in arrived)
    return total(0), [
        swap_with(total(z).astype(jnp.bfloat16), z << first_bit, count) for z in range(1, 2**bits)
    ]


def reduce_end(own_part, arrived):
    return own_part + sum(part.astype(jnp.float32) for part in arrived)


def sum_all(value, groups):
    for bit in range(sum(groups)):
        value = value + swap_with(value, 1 << bit, 2 ** sum(groups))
    return value


def tie(*values):
    return lax.optimization_barrier(values)


def small_shard(vec, bias, own, count, width):
    step = vec.shape[1]
    lane = lax.broadcasted_iota(jnp.int32, (7, width), 1)
    rows = jnp.where(lane // step == own, jnp.tile(vec, (1, count)), 0.0)
    place_of = lax.broadcasted_iota(jnp.int32, (4, width), 0) * width + lax.broadcasted_iota(
        jnp.int32, (4, width), 1
    )
    tiled = jnp.tile(bias, width // bias.shape[0])[None]
    bias_rows = jnp.where(place_of // bias.shape[0] == own, tiled, 0.0)
    return jnp.concatenate([rows, bias_rows])


def pad_rows(rows, step):
    pieces = -(-rows.shape[0] // step)
    rows = jnp.pad(rows.astype(jnp.bfloat16), ((0, pieces * step - rows.shape[0]), (0, 0)))
    return rows.reshape(pieces, step, rows.shape[1])


def mat(a,b,dims):
    return lax.dot_general(a,b,(dims,((),())),preferred_element_type=jnp.float32)

def fill_bias(bias_ref, seg_col, pos_col, seg_row, pos_row):
    rows=bias_ref.shape[0]
    step=min(BLOCK,rows)
    for first in range(0,rows,step):
        sc=seg_col[first:first+step,:]; pc=pos_col[first:first+step,:]
        sr=seg_row[:,first:]; pr=pos_row[:,first:]
        allowed=(sc==sr)&(pc<=pr)
        bias_ref[first:first+step,first:]=jnp.where(allowed,0.0,masked_score)

def head_lanes(shape, which):
    lane=lax.broadcasted_iota(jnp.int32,shape,1)
    return (lane//HEAD)==which

def attn_fwd_kernel(segc,posc,segr,posr,q_ref,k_ref,v_ref,o_ref,lse_ref,bias_ref):
    @pl.when(pl.program_id(0)==0)
    def _():
        fill_bias(bias_ref,segc,posc,segr,posr)
    rows=q_ref.shape[0]; step=min(BLOCK,rows)
    pair=q_ref.shape[1]//HEAD
    const=HEAD**-0.5*LOG2E
    for first in range(0,rows,step):
        keys=first+step
        q=q_ref[first:keys,:]
        mixed=None
        for which in range(pair):
            own=head_lanes(q.shape,which)
            qh=jnp.where(own,q,jnp.zeros_like(q))
            s=mat(k_ref[:keys,:],qh,((1,),(1,)))*const+bias_ref[:keys,first:keys]
            m=jnp.max(s,0,keepdims=True)
            w=jnp.exp2(s-m)
            total=jnp.sum(w,0,keepdims=True)
            p=(w*(1.0/total)).astype(jnp.bfloat16)
            o=mat(p,v_ref[:keys,:],((0,),(0,)))
            mixed=o if mixed is None else jnp.where(own,o,mixed)
            lse_ref[0,which:which+1,first:keys]=m+jnp.log2(total)
        o_ref[first:keys,:]=mixed.astype(jnp.bfloat16)

def attn_bwd_kernel(
    offsets, own_ref, segc, posc, segr, posr, q_ref, k_ref, v_ref, do_ref, lse_ref, h_ref, w_ref, start_ref, *refs
):
    *outs, dh_ref, bias_ref, dk_acc, dv_acc, ht_ref, dw_ref = refs
    rows = q_ref.shape[0]

    @pl.when(pl.program_id(0) == 0)
    def _():
        fill_bias(bias_ref, segc, posc, segr, posr)
        ht_ref[...] = h_ref[...].T
        dh_ref[...] = start_ref[...]

    step = min(BLOCK, rows)
    pair = q_ref.shape[1] // HEAD
    const = HEAD**-0.5 * LOG2E
    scale = HEAD**-0.5
    dk_acc[...] = jnp.zeros_like(dk_acc)
    dv_acc[...] = jnp.zeros_like(dv_acc)
    dq_parts = []
    for first in range(0, rows, step):
        keys = first + step
        q = q_ref[first:keys, :]
        do = do_ref[first:keys, :]
        dq = None
        for which in range(pair):
            own = head_lanes(q.shape, which)
            qh = jnp.where(own, q, jnp.zeros_like(q))
            doh = jnp.where(own, do, jnp.zeros_like(do))
            s = mat(k_ref[:keys, :], qh, ((1,), (1,)))
            p = jnp.exp2(s * const + (bias_ref[:keys, first:keys] - lse_ref[0, which : which + 1, first:keys]))
            dp = mat(v_ref[:keys, :], doh, ((1,), (1,)))
            inner = jnp.sum(p * dp, 0, keepdims=True)
            ds = (p * (dp - inner)).astype(jnp.bfloat16)
            dv_acc[:keys, :] += mat(p.astype(jnp.bfloat16), doh, ((1,), (0,)))
            dk_acc[:keys, :] += mat(ds, qh, ((1,), (0,)))
            d = mat(ds, k_ref[:keys, :], ((0,), (0,)))
            dq = d if dq is None else jnp.where(own, d, dq)
        dq_parts.append((dq * scale).astype(jnp.bfloat16))
    grads = jnp.concatenate(
        [
            jnp.concatenate(dq_parts, 0),
            (dk_acc[...] * scale).astype(jnp.bfloat16),
            dv_acc[...].astype(jnp.bfloat16),
        ],
        1,
    )
    weights = jnp.concatenate([w_ref[0], w_ref[1], w_ref[2]], 1)
    dh_ref[...] += mat(grads, weights, ((1,), (1,)))
    dw = mat(ht_ref[...], grads, ((1,), (0,))).astype(jnp.bfloat16)
    lanes = q_ref.shape[1]
    if offsets is None:
        for j in range(3):
            outs[0][j] = dw[:, j * lanes : (j + 1) * lanes]
    else:
        dw_ref[...] = dw.reshape(dw_ref.shape)
        for entry, offset in enumerate(offsets):
            for side in range(2):
                owner = own_ref[0] ^ (offset | side)
                for j in range(3):
                    outs[side][entry, j] = dw_ref[owner, :, j * lanes : (j + 1) * lanes]


def const_map(*_): return (0,0)

def seg_args(segments,positions):
    return (segments[:,None],positions[:,None],segments[None],positions[None])

def attend(q,k,v,segments,positions):
    rows,width=q.shape
    pairs=width//128
    blk=pl.BlockSpec((rows,128),lambda j:(0,j))
    col=pl.BlockSpec((rows,1),const_map); row=pl.BlockSpec((1,rows),const_map)
    return pl.pallas_call(attn_fwd_kernel,grid=(pairs,),
        in_specs=[col,col,row,row,blk,blk,blk],
        out_specs=[blk,pl.BlockSpec((1,2,rows),lambda j:(j,0,0))],
        out_shape=[jax.ShapeDtypeStruct((rows,width),jnp.bfloat16),jax.ShapeDtypeStruct((pairs,2,rows),jnp.float32)],
        scratch_shapes=[pltpu.VMEM((rows,rows),jnp.float32)],
        name="attn_fwd",
    )(*seg_args(segments,positions),q,k,v)

def attend_back(own, q, k, v, do, lse, segments, positions, normed, w_qkv, start, groups):
    rows, width = q.shape
    lanes = 2 * HEAD
    count = 2 ** sum(groups)
    inputs = w_qkv.shape[1]
    step = inputs // count
    blk = pl.BlockSpec((rows, lanes), lambda j: (0, j))
    col = pl.BlockSpec((rows, 1), const_map)
    row = pl.BlockSpec((1, rows), const_map)
    offsets = None
    if step % 16 == 0:
        offsets = [offset for table in offsets_of(groups)[:-1] for offset in table]
        shape = (len(offsets), 3, step, width)
        out_specs = [pl.BlockSpec(shape[:3] + (lanes,), lambda j: (0, 0, 0, j)) for _ in range(2)]
        out_shape = [jax.ShapeDtypeStruct(shape, jnp.bfloat16) for _ in range(2)]
        dw_scratch = pltpu.VMEM((count, step, 3 * lanes), jnp.bfloat16)
    else:
        out_specs = [pl.BlockSpec((3, inputs, lanes), lambda j: (0, 0, j))]
        out_shape = [jax.ShapeDtypeStruct((3, inputs, width), jnp.bfloat16)]
        dw_scratch = pltpu.VMEM((16, lanes), jnp.bfloat16)
    *grads, dh = pl.pallas_call(
        functools.partial(attn_bwd_kernel, offsets),
        grid=(width // lanes,),
        in_specs=[smem_spec(), col, col, row, row, blk, blk, blk, blk]
        + [
            pl.BlockSpec((1, 2, rows), lambda j: (j, 0, 0)),
            pl.BlockSpec((rows, inputs), const_map),
            pl.BlockSpec((3, inputs, lanes), lambda j: (0, 0, j)),
            pl.BlockSpec((rows, inputs), const_map),
        ],
        out_specs=out_specs + [pl.BlockSpec((rows, inputs), const_map)],
        out_shape=out_shape + [jax.ShapeDtypeStruct((rows, inputs), jnp.float32)],
        scratch_shapes=[
            pltpu.VMEM((rows, rows), jnp.float32),
            pltpu.VMEM((rows, lanes), jnp.float32),
            pltpu.VMEM((rows, lanes), jnp.float32),
            pltpu.VMEM((inputs, rows), jnp.bfloat16),
            dw_scratch,
        ],
        name="attn_bwd",
    )(own[None].astype(jnp.int32), *seg_args(segments, positions), q, k, v, do, lse, normed, w_qkv, start)
    if offsets is None:
        grads = split(own, [grads[0].reshape(3, count, step, width)], [("stack", 0, 3)], groups)
    return grads[0], grads[1], dh


def copy_parts(tables, layout, own, parts, outs):
    where_to = [
        (index, kind, piece) for index, (kind, _, pieces) in enumerate(layout) for piece in range(pieces)
    ]
    for part, (row, first) in zip(parts, tables):
        width = part.shape[3]
        for entry, offset in enumerate(row):
            owner = own ^ offset
            for source in range(part.shape[1]):
                index, kind, piece = where_to[first + source]
                if kind == "stack":
                    outs[index][owner] = part[entry, source]
                elif kind == "rows":
                    outs[index][owner, piece] = part[entry, source]
                else:
                    outs[index][owner, :, piece * width : (piece + 1) * width] = part[entry, source]


def copy_blocks(offsets, layout, own, ins, kept, sent):
    width = kept.shape[3]
    for entry, offset in enumerate(offsets):
        for side, target in enumerate((kept, sent)):
            owner = own ^ (offset | side)
            for index, (kind, first, pieces) in enumerate(layout):
                for piece in range(pieces):
                    if kind == "stack":
                        block = ins[index][owner]
                    elif kind == "rows":
                        block = ins[index][owner, piece]
                    else:
                        block = ins[index][owner, :, piece * width : (piece + 1) * width]
                    target[entry, first + piece] = block


def ffn_kernel(direct, part_count, tables, offsets, layout, own_ref, x_ref, cot_ref, h_ref, o_ref, vec_ref, bias_ref, *refs):
    low = lambda value: value.astype(jnp.bfloat16)
    parts = refs[:part_count]
    out_count = 6 + (2 if direct else 5)
    outs = refs[part_count : part_count + out_count]
    scratch = refs[part_count + out_count :]
    y_ref, do_ref, dh_ref, dx_ref, dvec_ref, dbias_ref = outs[:6]
    r_ref, dz_ref, h2_ref, df_ref, dzf_ref, da_ref, dza_ref = scratch[:7]
    tile = pl.program_id(0)
    if direct:
        weights = targets = scratch[7:]

        @pl.when(tile == 0)
        def _():
            copy_parts(tables, layout, own_ref[0], parts, weights)

    else:
        weights, targets = parts, outs[6:]
    width = x_ref.shape[1]
    size = x_ref.shape[0]
    chunks = r_ref.shape[0]
    load = lambda index: weights[index][...].reshape(-1, weights[index].shape[-1])
    rows = pl.ds(tile * size, size)

    @pl.when(tile == 0)
    def _():
        dvec_ref[...] = jnp.zeros_like(dvec_ref)
        dbias_ref[...] = jnp.zeros_like(dbias_ref)

    forward = ((1,), (0,))
    backward = ((1,), (1,))
    x = x_ref[...].astype(jnp.float32)
    a = mat(o_ref[rows, :], load(0), forward)
    ga = jax.nn.sigmoid(mat(h_ref[rows, :], load(1), forward) + vec_ref[4:5, :])
    x1 = ga * a + (1.0 - ga) * x
    gain = vec_ref[2:3, :]
    h2_full, n2, s2 = normalize_parts(x1, gain, vec_ref[3:4, :])
    h2 = low(h2_full)
    z = mat(h2, load(3), forward) + bias_ref[...]
    r = low(jnp.maximum(z, 0.0))
    f = mat(r, load(4), forward) + vec_ref[6:7, :]
    gf = jax.nn.sigmoid(mat(h2, load(2), forward) + vec_ref[5:6, :])
    y_ref[...] = low(gf * f + (1.0 - gf) * x1)
    dy = cot_ref[...].astype(jnp.float32)
    df = dy * gf
    dzf = dy * (f - x1) * gf * (1.0 - gf)
    dx1 = dy * (1.0 - gf)
    dfb = low(df)
    dzfb = low(dzf)
    dz = jnp.where(z > 0.0, mat(dfb, load(4), backward), 0.0)
    dzb = low(dz)
    dh2 = mat(dzb, load(3), backward) + mat(dzfb, load(2), backward)
    dx1 = dx1 + normalize_back(dh2, n2, s2, gain)
    da = low(dx1 * ga)
    dza = dx1 * (a - x) * ga * (1.0 - ga)
    dzab = low(dza)
    dx_ref[...] = dx1 * (1.0 - ga)
    do_ref[...] = low(mat(da, load(0), backward))
    dh_ref[...] = mat(dzab, load(1), backward)
    total = lambda value: jnp.sum(value, 0, keepdims=True)
    dvec_ref[0:1, :] += total(dh2 * n2)
    dvec_ref[1:2, :] += total(dh2)
    dvec_ref[2:3, :] += total(dza)
    dvec_ref[3:4, :] += total(dzf)
    dvec_ref[4:5, :] += total(df)
    dbias_ref[...] += total(dz)
    for chunk in range(chunks):
        r_ref[chunk, rows, :] = r[:, chunk * width : (chunk + 1) * width]
        dz_ref[chunk, rows, :] = dzb[:, chunk * width : (chunk + 1) * width]
    h2_ref[rows, :] = h2
    df_ref[rows, :] = dfb
    dzf_ref[rows, :] = dzfb
    da_ref[rows, :] = da
    dza_ref[rows, :] = dzab

    @pl.when(tile == pl.num_programs(0) - 1)
    def _():
        across = lambda left, right: low(mat(left, right, forward))
        targets[0][...] = across(o_ref[...].T, da_ref[...]).reshape(targets[0].shape)
        targets[1][...] = across(h_ref[...].T, dza_ref[...]).reshape(targets[1].shape)
        h2_turned = h2_ref[...].T
        targets[2][...] = across(h2_turned, dzf_ref[...]).reshape(targets[2].shape)
        for chunk in range(chunks):
            lanes = slice(chunk * width, (chunk + 1) * width)
            grad_in = across(h2_turned, dz_ref[chunk])
            grad_out = across(r_ref[chunk].T, df_ref[...])
            if direct:
                owners = targets[4].shape[0] // chunks
                targets[3][:, :, lanes] = grad_in.reshape(targets[3].shape[:2] + (width,))
                targets[4][chunk * owners : (chunk + 1) * owners] = grad_out.reshape(
                    (owners,) + targets[4].shape[1:]
                )
            else:
                targets[3][:, lanes] = grad_in
                targets[4][lanes, :] = grad_out
        if direct:
            copy_blocks(offsets, layout, own_ref[0], targets, *outs[6:])


FFN_LAYOUT = [("stack", 0, 1), ("stack", 1, 1), ("stack", 2, 1), ("columns", 3, 4), ("rows", 7, 4)]


def ffn(own, tokens, cotangent, normed, mixed_heads, vectors, bias, parts, tables, groups):
    rows, width = tokens.shape
    count = 2 ** sum(groups)
    step = parts[0].shape[2]
    hidden = bias.shape[0]
    chunks = hidden // width
    tile = min(256, rows)
    direct = step % 16 == 0
    offsets = [offset for row in offsets_of(groups)[:-1] for offset in row]
    matrices = [(width, width)] * 3 + [(width, hidden), (hidden, width)]
    low = jnp.bfloat16
    once = dict(pipeline_mode=pl.Buffered(1))
    block = pl.BlockSpec((tile, width), lambda i: (i, 0))
    whole = lambda shape: pl.BlockSpec(shape, lambda i: (0,) * len(shape), **once)
    scratch = [pltpu.VMEM((chunks, rows, width), low)] * 2 + [pltpu.VMEM((rows, width), low)] * 5
    if direct:
        shape = (len(offsets), 3 + 2 * chunks, step, width)
        grads = [jax.ShapeDtypeStruct(shape, low)] * 2
        scratch += [pltpu.VMEM((count, step, width), low)] * 3
        scratch += [pltpu.VMEM((count, step, hidden), low), pltpu.VMEM((count, chunks, step, width), low)]
    else:
        placed = place(own, parts, tables, FFN_LAYOUT, groups)
        parts = [weight.reshape(shape) for weight, shape in zip(placed, matrices)]
        grads = [jax.ShapeDtypeStruct(shape, low) for shape in matrices]
    full = jax.ShapeDtypeStruct((rows, width), jnp.float32)
    half = jax.ShapeDtypeStruct((rows, width), low)
    small = [jax.ShapeDtypeStruct((8, width), jnp.float32), jax.ShapeDtypeStruct((1, hidden), jnp.float32)]
    result = pl.pallas_call(
        functools.partial(ffn_kernel, direct, len(parts), tables, offsets, FFN_LAYOUT),
        grid=(rows // tile,),
        in_specs=[smem_spec(), block, block, whole((rows, width)), whole((rows, width))]
        + [whole(vectors.shape), whole((1, hidden))]
        + [whole(part.shape) for part in parts],
        out_specs=[block] * 4 + [whole(item.shape) for item in small + grads],
        out_shape=[half, half, full, full] + small + grads,
        scratch_shapes=scratch,
        name="ffn",
    )(own[None].astype(jnp.int32), tokens, cotangent, normed, mixed_heads, vectors, bias[None], *parts)
    if not direct:
        blocks = [grad.reshape(1, count, step, width) for grad in result[6:9]]
        blocks += [result[9].reshape(count, step, hidden), result[10].reshape(count, chunks, step, width)]
        result = list(result[:6]) + list(split(own, blocks, FFN_LAYOUT, groups))
    return result


def adam_update(weight, first_moment, second_moment, gradient, factor, step_rate):
    clipped = gradient * factor
    first_new = first_decay * first_moment + (1.0 - first_decay) * clipped
    second_new = second_decay * second_moment + (1.0 - second_decay) * clipped * clipped
    corrected = first_new / (1.0 - first_decay**STEP)
    spread = second_new / (1.0 - second_decay**STEP)
    weight_new = weight - step_rate * (
        corrected / (jnp.sqrt(spread) + adam_eps) + weight_decay * weight
    )
    return (weight_new, first_new, second_new)


def body(
    groups,
    tokens,
    segments,
    positions,
    cotangent,
    attn_weight,
    attn_m,
    attn_v,
    gate_weight,
    gate_m,
    gate_v,
    in_weight,
    in_m,
    in_v,
    out_weight,
    out_m,
    out_v,
    norm_params,
    norm_m,
    norm_v,
    in_bias,
    bias_m,
    bias_v,
):
    count = 2 ** sum(groups)
    own = lax.axis_index(AXES)
    width = 512
    step = attn_weight.shape[1]
    low = lambda value: value.astype(jnp.bfloat16)
    dot = functools.partial(jnp.einsum, preferred_element_type=jnp.float32)
    columns = lambda value: [value[:, width * j : width * (j + 1)] for j in range(4)]
    small = pad_rows(small_shard(norm_params, in_bias, own, count, width), step)
    extra = small.shape[0]
    first_shard = jnp.concatenate([low(attn_weight[:3]), small])
    second_shard = jnp.concatenate(
        [
            low(attn_weight[3:]),
            low(gate_weight),
            jnp.stack(columns(low(in_weight))),
            low(out_weight).reshape(4, step, width),
        ]
    )
    cut = 6
    orders = plane_orders(groups)
    plane_steps = range(len(orders[0]))
    z_first = gather_z(first_shard, groups)
    z_first, second_shard = tie(z_first, second_shard)
    plane_first = gather_plane(z_first, groups)
    z_second = gather_z(second_shard, groups)
    halves = [z_second[:, :cut], z_second[:, cut:]]
    tied = tie(*halves, z_first, *plane_first)
    halves, z_first, plane_first = tied[:2], tied[2], list(tied[3:])
    core_first = gather_core(z_first, plane_first, groups)
    received = send_halves(halves, orders, 0, groups)
    w_qkv, vectors = place(
        own,
        [z_first] + plane_first + [core_first],
        [(row, 0) for row in offsets_of(groups)],
        [("stack", 0, 3), ("sum", 3, extra)],
        groups,
    )
    w_qkv = w_qkv.reshape(3, count * step, width)
    bias = vectors[7:11].reshape(-1)
    inputs = tokens.astype(jnp.float32)
    normed_full, unit_one, scale_one = normalize_parts(inputs, vectors[0], vectors[1])
    normed = low(normed_full)
    queries, keys, values = [low(dot("td,de->te", normed, w_qkv[j])) for j in range(3)]
    queries, keys, values, *received = tie(queries, keys, values, *received)
    tables = [z_offsets(groups)] * 2
    for position in plane_steps[1:]:
        halves, tables = join_halves(halves, received, tables, orders, position - 1)
        received = send_halves(halves, orders, position, groups)
    mixed_heads, log_total = attend(queries, keys, values, segments, positions)
    mixed_heads, *received = tie(mixed_heads, *received)
    second_step, tables = join_halves(halves, received, tables, orders, plane_steps[-1])
    others = [swap_with(half, 1, count) for half in second_step]
    layer_out, grad_mixed, grad_normed, grad_inputs, sums, grad_bias, kept_b, sent_b = ffn(
        own,
        tokens,
        cotangent,
        normed,
        mixed_heads,
        vectors,
        bias,
        list(second_step) + others,
        [(tables[0], 0), (tables[1], cut)]
        + [([offset | 1 for offset in table], first) for table, first in zip(tables, (0, cut))],
        groups,
    )
    core_b = swap_with(sent_b, 1, count)
    core_b, kept_b, grad_mixed = tie(core_b, kept_b, grad_mixed)
    own_b, parts_b = plane_sums(kept_b, core_b, groups)
    own_b, log_total, *parts_b = tie(own_b, log_total, *parts_b)
    plane_b = plane_send(parts_b, groups)
    kept_a, sent_a, grad_normed = attend_back(
        own, queries, keys, values, grad_mixed, log_total, segments, positions, normed, w_qkv, grad_normed, groups
    )
    kept_a, sent_a, grad_normed, own_b, *plane_b = tie(kept_a, sent_a, grad_normed, own_b, *plane_b)
    core_a = swap_with(sent_a, 1, count)
    own_b, z_b = reduce_z(own_b, plane_b, groups)
    grad_gain_one = jnp.sum(grad_normed * unit_one, 0)
    grad_shift_one = jnp.sum(grad_normed, 0)
    grad_inputs = grad_inputs + normalize_back(grad_normed, unit_one, scale_one, vectors[0])
    input_grad = low(grad_inputs)
    own_a, parts_a = plane_sums(kept_a, core_a, groups)
    plane_a = plane_send(parts_a, groups)
    own_a, z_a = reduce_z(own_a, plane_a, groups)
    total_b = reduce_end(own_b, z_b)
    total_a = reduce_end(own_a, z_a)
    local_squares = jnp.sum(total_b * total_b) + jnp.sum(total_a * total_a)
    payload = jnp.concatenate(
        [
            grad_gain_one[None],
            grad_shift_one[None],
            sums[:5],
            grad_bias.reshape(4, width),
            jnp.full((1, width), local_squares),
        ]
    )
    payload = sum_all(payload, groups)
    own_small = payload[:11]
    own_vec = lax.dynamic_slice(own_small[:7], (0, own * step), (7, step))
    own_bias = lax.dynamic_slice(own_small[7:11].reshape(-1), (own * 4 * step,), (4 * step,))
    owned = (
        jnp.concatenate([total_a, total_b[:1]]),
        total_b[1:3],
        jnp.concatenate(list(total_b[3:7]), 1),
        total_b[7:].reshape(4 * step, width),
        own_vec,
        own_bias,
    )
    grad_norm = jnp.sqrt(payload[11, 0] + jnp.sum(own_small * own_small))
    factor = jnp.minimum(1.0, clip_norm / (grad_norm + 1e-06))
    states = (
        (attn_weight, attn_m, attn_v),
        (gate_weight, gate_m, gate_v),
        (in_weight, in_m, in_v),
        (out_weight, out_m, out_v),
        (norm_params, norm_m, norm_v),
        (in_bias, bias_m, bias_v),
    )
    step_rates = (learn_rate, learn_rate, learn_rate, learn_rate, vector_rate, vector_rate)
    updated = [
        adam_update(state[0], state[1], state[2], gradient, factor, step_rate)
        for state, gradient, step_rate in zip(states, owned, step_rates)
    ]
    return (
        layer_out,
        input_grad,
        grad_norm,
        updated[0][0],
        updated[0][1],
        updated[0][2],
        updated[1][0],
        updated[1][1],
        updated[1][2],
        updated[2][0],
        updated[2][1],
        updated[2][2],
        updated[3][0],
        updated[3][1],
        updated[3][2],
        updated[4][0],
        updated[4][1],
        updated[4][2],
        updated[5][0],
        updated[5][1],
        updated[5][2],
    )


def solution(mesh):
    return jax.shard_map(
        functools.partial(body, bit_groups(mesh.shape)),
        mesh=mesh,
        in_specs=(
            P(("dp", "inner"), None),
            P(("dp", "inner")),
            P(("dp", "inner")),
            P(("dp", "inner"), None),
            P(None, ("dp", "inner"), None),
            P(None, ("dp", "inner"), None),
            P(None, ("dp", "inner"), None),
            P(None, ("dp", "inner"), None),
            P(None, ("dp", "inner"), None),
            P(None, ("dp", "inner"), None),
            P(("dp", "inner"), None),
            P(("dp", "inner"), None),
            P(("dp", "inner"), None),
            P(("dp", "inner"), None),
            P(("dp", "inner"), None),
            P(("dp", "inner"), None),
            P(None, ("dp", "inner")),
            P(None, ("dp", "inner")),
            P(None, ("dp", "inner")),
            P(("dp", "inner")),
            P(("dp", "inner")),
            P(("dp", "inner")),
        ),
        out_specs=(
            P(("dp", "inner"), None),
            P(("dp", "inner"), None),
            P(),
            P(None, ("dp", "inner"), None),
            P(None, ("dp", "inner"), None),
            P(None, ("dp", "inner"), None),
            P(None, ("dp", "inner"), None),
            P(None, ("dp", "inner"), None),
            P(None, ("dp", "inner"), None),
            P(("dp", "inner"), None),
            P(("dp", "inner"), None),
            P(("dp", "inner"), None),
            P(("dp", "inner"), None),
            P(("dp", "inner"), None),
            P(("dp", "inner"), None),
            P(None, ("dp", "inner")),
            P(None, ("dp", "inner")),
            P(None, ("dp", "inner")),
            P(("dp", "inner")),
            P(("dp", "inner")),
            P(("dp", "inner")),
        ),
        check_vma=False,
    )
```

profile of v0, /device:TPU:0, one launch (start us, length us, event | category | flops | bytes accessed | tf_op | source)
XLA Modules:
  0.0 216.0 jit_solution(13375919421946850249)
XLA Ops:
  3.4 3.1 %collective-permute-start = (bf16[4,16,512]{2,1,0:T(8,128)(2,1)S(1)}, bf16[4,16,512]{2,1,0:T(8,128)(2,1)S(1)}, u32[]{:S(2)}, u32[]{:S(2)}) collective-permute-start(bf16[4,16,512]{2,1,0:T(8,128)(2,1)S(1)} %get-tuple-element.162), channel_id=1, source_target_pairs={{0,8},{1,9},{2,10},{3,11},{4,12},{5,13},{6,14},{7,15},{8,0},{9,1},... | collective-permute-start | bytes 196616 | tf_op jit(solution)/shard_map/ppermute | solution.py:54
  6.5 2.6 %collective-permute-start.1 = (bf16[4,16,512]{2,1,0:T(8,128)(2,1)S(1)}, bf16[4,16,512]{2,1,0:T(8,128)(2,1)S(1)}, u32[]{:S(2)}, u32[]{:S(2)}) collective-permute-start(bf16[4,16,512]{2,1,0:T(8,128)(2,1)S(1)} %get-tuple-element.162), channel_id=1, source_target_pairs={{0,16},{1,17},{2,18},{3,19},{4,20},{5,21},{6,22},{7,23},{8,24},{9,... | collective-permute-start | bytes 196616 | tf_op jit(solution)/shard_map/ppermute | solution.py:54
  11.8 1.9 collective-permute-done.1
  13.7 1.4 collective-permute-done.2
  15.3 2.3 %collective-permute-start.4 = (bf16[11,16,512]{2,1,0:T(8,128)(2,1)S(1)}, bf16[11,16,512]{2,1,0:T(8,128)(2,1)S(1)}, u32[]{:S(2)}, u32[]{:S(2)}) collective-permute-start(bf16[11,16,512]{2,1,0:T(8,128)(2,1)S(1)} %constant_dynamic-update-slice_fusion), channel_id=1, source_target_pairs={{0,16},{1,17},{2,18},{3,19},{4,20},{5,21},{6,22},{7,23},{8,24},{9,... | collective-permute-start | bytes 540680 | tf_op jit(solution)/shard_map/ppermute | solution.py:54
  17.6 2.0 collective-permute-start.5
  19.6 1.5 collective-permute-start.6
  21.1 1.5 collective-permute-start.7
  22.7 2.3 %collective-permute-start.8 = (bf16[4,4,16,512]{3,2,1,0:T(8,128)(2,1)S(1)}, bf16[4,4,16,512]{3,2,1,0:T(8,128)(2,1)S(1)}, u32[]{:S(2)}, u32[]{:S(2)}) collective-permute-start(bf16[4,4,16,512]{3,2,1,0:T(8,128)(2,1)S(1)} %pad_maximum_fusion.5.refs_0_), channel_id=1, source_target_pairs={{0,6},{1,7},{2,4},{3,5},{4,2},{5,3},{6,0},{7,1},{8,14},{9,15},{10,... | collective-permute-start | bytes 786440 | tf_op jit(solution)/shard_map/ppermute | solution.py:54
  24.9 6.0 %collective-permute-done.4 = bf16[11,16,512]{2,1,0:T(8,128)(2,1)S(1)} collective-permute-done((bf16[11,16,512]{2,1,0:T(8,128)(2,1)S(1)}, bf16[11,16,512]{2,1,0:T(8,128)(2,1)S(1)}, u32[]{:S(2)}, u32[]{:S(2)}) %collective-permute-start.4) | collective-permute-done | bytes 180256 | tf_op jit(solution)/shard_map/ppermute | solution.py:54
  31.2 1.7 collective-permute-done.7.refs_2_
  33.9 1.3 collective-permute-start.10
  35.2 1.1 collective-permute-start.11
  36.3 2.8 %place.1 = (bf16[3,32,16,512]{3,2,1,0:T(8,128)(2,1)}, f32[16,512]{1,0:T(8,128)}) custom-call(s32[1]{0:T(128)} %bitcast.own_ref, bf16[4,4,16,512]{3,2,1,0:T(8,128)(2,1)} %copy-done.5, bf16[4,4,16,512]{3,2,1,0:T(8,128)(2,1)} %copy-done.9, bf16[4,4,16,512]{3,2,1,0:T(8,128)(2,1)} %copy-done.10, bf16[4,4,16,512]{3,2,1,0:T(8,128)(2,1)} %copy-done.11, ...), custom_call_target="tpu_custom_call" | custom-call | tf_op jit(solution)/shard_map/place/pallas_call | solution.py:183
  39.1 1.5 fusion.54
  41.8 1.7 convolution_convert_fusion.v_ref
  43.5 1.7 convolution_convert_fusion.1.k_ref
  45.2 1.7 convolution_convert_fusion.2.q_ref
  46.9 0.9 pad_maximum_fusion.1
  47.8 1.1 collective-permute-start.12
  48.9 0.9 pad_maximum_fusion.3
  50.6 1.0 copy.43.segc
  51.7 1.0 copy.44.posc
  52.7 14.2 %attn_fwd.1 = (bf16[1024,512]{1,0:T(8,128)(2,1)}, f32[4,2,1024]{2,1,0:T(2,128)}) custom-call(s32[1024,1]{1,0:T(8,128)} %copy.43.segc, s32[1024,1]{1,0:T(8,128)} %copy.44.posc, s32[1,1024]{1,0:T(1,128)} %bitcast.107, s32[1,1024]{1,0:T(1,128)} %bitcast.110, bf16[1024,512]{1,0:T(8,128)(2,1)} %convolution_convert_fusion.2.q_ref, ...), custom_call_target="tpu_custom_call" | custom-call | tf_op jit(solution)/shard_map/attn_fwd/pallas_call | solution.py:409
  67.5 1.2 constant_dynamic-update-slice_fusion.6.refs_0_
  68.9 1.6 constant_dynamic-update-slice_fusion.9.refs_1_
  72.0 2.1 collective-permute-done.15.refs_3_
  74.1 1.1 copy-done.8
  75.2 1.1 copy-done.7
  76.3 30.7 %ffn.1 = (bf16[1024,512]{1,0:T(8,128)(2,1)}, bf16[1024,512]{1,0:T(8,128)(2,1)}, f32[1024,512]{1,0:T(8,128)}, f32[1024,512]{1,0:T(8,128)}, f32[8,512]{1,0:T(8,128...) custom-call(s32[1]{0:T(128)} %bitcast.own_ref, ...), custom_call_target="tpu_custom_call" | custom-call | tf_op jit(solution)/shard_map/ffn/pallas_call | solution.py:626
  107.3 5.4 %collective-permute-done.16 = bf16[16,11,16,512]{3,2,1,0:T(8,128)(2,1)S(1)} collective-permute-done((bf16[16,11,16,512]{3,2,1,0:T(8,128)(2,1)}, bf16[16,11,16,512]{3,2,1,0:T(8,128)(2,1)S(1)}, u32[]{:S(2)}, u32[]{:S(2)}) %collective-permute-start.16) | collective-permute-done | bytes 2883616 | tf_op jit(solution)/shard_map/ppermute | solution.py:54
  112.6 4.3 %add_convert_fusion = (bf16[4,11,16,512]{3,2,1,0:T(8,128)(2,1)S(1)}, bf16[4,11,16,512]{3,2,1,0:T(8,128)(2,1)}, bf16[4,11,16,512]{3,2,1,0:T(8,128)(2,1)}, f32[4,11,16,512]{3,2,1,0:T(8,128)}) fusion(bf16[16,11,16,512]{3,2,1,0:T(8,128)(2,1)S(1)} %collective-permute-done.16, bf16[16,11,16,512]{3,2,1,0:T(8,128)(2,1)} %get-tuple-element.92), kind=kLoop, calls=%fused_computation.21 | loop fusion | flops 5406720 | bytes 9371648 | tf_op jit(solution)/shard_map/convert_element_type | solution.py:248
  117.0 1.2 collective-permute-start.17
  119.1 1.4 collective-permute-start.19
  120.5 29.5 %attn_bwd.1 = (bf16[16,3,16,512]{3,2,1,0:T(8,128)(2,1)}, bf16[16,3,16,512]{3,2,1,0:T(8,128)(2,1)}, f32[1024,512]{1,0:T(8,128)}) custom-call(s32[1]{0:T(128)} %bitcast.own_ref, s32[1024,1]{1,0:T(8,128)} %copy.43.segc, s32[1024,1]{1,0:T(8,128)} %copy.44.posc, s32[1,1024]{1,0:T(1,128)} %bitcast.108, s32[1,1024]{1,0:T(1,128)} %bitcast.111, ...), custom_call_target="tpu_custom_call" | custom-call | tf_op jit(solution)/shard_map/attn_bwd/pallas_call | solution.py:437
  150.0 1.8 collective-permute-done.18
  153.2 2.2 %fusion.15 = (bf16[11,16,512]{2,1,0:T(8,128)(2,1)S(1)}, bf16[11,16,512]{2,1,0:T(8,128)(2,1)S(1)}, bf16[11,16,512]{2,1,0:T(8,128)(2,1)S(1)}) fusion(f32[4,11,16,512]{3,2,1,0:T(8,128)} %get-tuple-element.107, bf16[4,11,16,512]{3,2,1,0:T(8,128)(2,1)} %copy-done.14, bf16[4,11,16,512]{3,2,1,0:T(8,128)(2,1)} %copy-done.13, bf16[4,11,16,512]{3,2,1,0:T(8,128)(2,1)} %copy-done.12), kind=kLoop, calls=%fused_computation.43 | loop fusion | flops 1892352 | bytes 3244032 | tf_op jit(solution)/shard_map/add | solution.py:259
  155.4 1.6 collective-permute-start.20
  157.0 1.4 collective-permute-start.21
  158.4 1.7 add_convert_fusion.5
  160.1 1.2 collective-permute-start.24
  161.3 1.0 collective-permute-start.25
  162.2 1.4 collective-permute-start.26
  163.7 1.7 fusion.13
  165.4 2.6 %collective-permute-done.24 = bf16[4,3,16,512]{3,2,1,0:T(8,128)(2,1)S(1)} collective-permute-done((bf16[4,3,16,512]{3,2,1,0:T(8,128)(2,1)S(1)}, bf16[4,3,16,512]{3,2,1,0:T(8,128)(2,1)S(1)}, u32[]{:S(2)}, u32[]{:S(2)}) %collective-permute-start.24) | collective-permute-done | bytes 196640 | tf_op jit(solution)/shard_map/ppermute | solution.py:54
  168.0 1.5 collective-permute-start.22
  169.5 1.2 collective-permute-done.25
  170.7 1.6 collective-permute-done.26
  172.4 1.7 collective-permute-start.27
  174.4 2.4 %collective-permute-start.29 = (bf16[3,16,512]{2,1,0:T(8,128)(2,1)S(1)}, bf16[3,16,512]{2,1,0:T(8,128)(2,1)S(1)}, u32[]{:S(2)}, u32[]{:S(2)}) collective-permute-start(bf16[3,16,512]{2,1,0:T(8,128)(2,1)S(1)} %get-tuple-element.154), channel_id=1, source_target_pairs={{0,24},{1,25},{2,26},{3,27},{4,28},{5,29},{6,30},{7,31},{8,16},{9,... | collective-permute-start | bytes 147464 | tf_op jit(solution)/shard_map/ppermute | solution.py:54
  176.8 2.0 multiply_reduce_fusion.1
  178.9 2.4 %collective-permute-done.28 = bf16[3,16,512]{2,1,0:T(8,128)(2,1)S(1)} collective-permute-done((bf16[3,16,512]{2,1,0:T(8,128)(2,1)S(1)}, bf16[3,16,512]{2,1,0:T(8,128)(2,1)S(1)}, u32[]{:S(2)}, u32[]{:S(2)}) %collective-permute-start.28) | collective-permute-done | bytes 49184 | tf_op jit(solution)/shard_map/ppermute | solution.py:54
  181.2 1.3 multiply_reduce_fusion.2
  184.4 1.6 concatenate.44
  186.0 1.3 collective-permute-done.30
  188.1 1.2 collective-permute-start.31
  190.0 2.0 collective-permute-done.31
  192.0 1.5 collective-permute-start.32
  194.2 1.7 collective-permute-done.32
  195.9 2.1 collective-permute-start.33
  198.0 2.9 %fusion.12 = bf16[1024,512]{1,0:T(8,128)(2,1)} fusion(f32[1024,512]{1,0:T(8,128)} %get-tuple-element.87, bf16[1024,512]{1,0:T(8,128)(2,1)S(1)} %copy-done.1, f32[1024,512]{1,0:T(8,128)S(1)} %copy-done.3, f32[1024]{0:T(1024)S(1)} %broadcast_multiply_fusion, f32[1024]{0:T(1024)S(1)} %broadcast_multiply_fusion.1, f32[512]{0:T(512)} %bitcast.115, ...), kind=kLoop, calls=%fused_computation.14 | loop fusion | flops 5242880 | bytes 6309888 | tf_op jit(solution)/shard_map/convert_element_type | solution.py:685
  201.2 4.7 %collective-permute-done.34 = f32[12,512]{1,0:T(8,128)S(1)} collective-permute-done((f32[12,512]{1,0:T(8,128)S(1)}, f32[12,512]{1,0:T(8,128)S(1)}, u32[]{:S(2)}, u32[]{:S(2)}) %collective-permute-start.34) | collective-permute-done | bytes 24608 | tf_op jit(solution)/shard_map/ppermute | solution.py:54
  208.5 1.6 multiply_subtract_fusion.3
  210.1 1.8 multiply_subtract_fusion
  (156 shorter events, 20.8 us)
Async XLA Ops:
  3.4 8.4 %collective-permute-start = (bf16[4,16,512]{2,1,0:T(8,128)(2,1)S(1)}, bf16[4,16,512]{2,1,0:T(8,128)(2,1)S(1)}, u32[]{:S(2)}, u32[]{:S(2)}) collective-permute-start(bf16[4,16,512]{2,1,0:T(8,128)(2,1)S(1)} %get-tuple-element.162), channel_id=1, source_target_pairs={{0,8},{1,9},{2,10},{3,11},{4,12},{5,13},{6,14},{7,15},{8,0},{9,1},... | collective-permute-start | bytes 196616 | tf_op jit(solution)/shard_map/ppermute | solution.py:54
  6.5 7.3 %collective-permute-start.1 = (bf16[4,16,512]{2,1,0:T(8,128)(2,1)S(1)}, bf16[4,16,512]{2,1,0:T(8,128)(2,1)S(1)}, u32[]{:S(2)}, u32[]{:S(2)}) collective-permute-start(bf16[4,16,512]{2,1,0:T(8,128)(2,1)S(1)} %get-tuple-element.162), channel_id=1, source_target_pairs={{0,16},{1,17},{2,18},{3,19},{4,20},{5,21},{6,22},{7,23},{8,24},{9,... | collective-permute-start | bytes 196616 | tf_op jit(solution)/shard_map/ppermute | solution.py:54
  9.1 6.1 %collective-permute-start.2 = (bf16[4,16,512]{2,1,0:T(8,128)(2,1)S(1)}, bf16[4,16,512]{2,1,0:T(8,128)(2,1)S(1)}, u32[]{:S(2)}, u32[]{:S(2)}) collective-permute-start(bf16[4,16,512]{2,1,0:T(8,128)(2,1)S(1)} %get-tuple-element.162), channel_id=1, source_target_pairs={{0,24},{1,25},{2,26},{3,27},{4,28},{5,29},{6,30},{7,31},{8,16},{9,... | collective-permute-start | bytes 196616 | tf_op jit(solution)/shard_map/ppermute | solution.py:54
  15.2 17.8 %copy-start.5 = (bf16[4,4,16,512]{3,2,1,0:T(8,128)(2,1)}, bf16[4,4,16,512]{3,2,1,0:T(8,128)(2,1)S(1)}, u32[]{:S(2)}) copy-start(bf16[4,4,16,512]{3,2,1,0:T(8,128)(2,1)S(1)} %pad_maximum_fusion.5.refs_0_) | copy-start | bytes 786436
  15.2 7.5 %collective-permute-start.3 = (bf16[11,16,512]{2,1,0:T(8,128)(2,1)S(1)}, bf16[11,16,512]{2,1,0:T(8,128)(2,1)S(1)}, u32[]{:S(2)}, u32[]{:S(2)}) collective-permute-start(bf16[11,16,512]{2,1,0:T(8,128)(2,1)S(1)} %constant_dynamic-update-slice_fusion), channel_id=1, source_target_pairs={{0,8},{1,9},{2,10},{3,11},{4,12},{5,13},{6,14},{7,15},{8,0},{9,1},... | collective-permute-start | bytes 540680 | tf_op jit(solution)/shard_map/ppermute | solution.py:54
  15.3 15.7 %collective-permute-start.4 = (bf16[11,16,512]{2,1,0:T(8,128)(2,1)S(1)}, bf16[11,16,512]{2,1,0:T(8,128)(2,1)S(1)}, u32[]{:S(2)}, u32[]{:S(2)}) collective-permute-start(bf16[11,16,512]{2,1,0:T(8,128)(2,1)S(1)} %constant_dynamic-update-slice_fusion), channel_id=1, source_target_pairs={{0,16},{1,17},{2,18},{3,19},{4,20},{5,21},{6,22},{7,23},{8,24},{9,... | collective-permute-start | bytes 540680 | tf_op jit(solution)/shard_map/ppermute | solution.py:54
  17.6 13.4 %collective-permute-start.5 = (bf16[11,16,512]{2,1,0:T(8,128)(2,1)S(1)}, bf16[11,16,512]{2,1,0:T(8,128)(2,1)S(1)}, u32[]{:S(2)}, u32[]{:S(2)}) collective-permute-start(bf16[11,16,512]{2,1,0:T(8,128)(2,1)S(1)} %constant_dynamic-update-slice_fusion), channel_id=1, source_target_pairs={{0,24},{1,25},{2,26},{3,27},{4,28},{5,29},{6,30},{7,31},{8,16},{9,... | collective-permute-start | bytes 540680 | tf_op jit(solution)/shard_map/ppermute | solution.py:54
  19.6 11.5 %collective-permute-start.6 = (bf16[4,4,16,512]{3,2,1,0:T(8,128)(2,1)S(1)}, bf16[4,4,16,512]{3,2,1,0:T(8,128)(2,1)S(1)}, u32[]{:S(2)}, u32[]{:S(2)}) collective-permute-start(bf16[4,4,16,512]{3,2,1,0:T(8,128)(2,1)S(1)} %pad_maximum_fusion.5.refs_0_), channel_id=1, source_target_pairs={{0,2},{1,3},{2,0},{3,1},{4,6},{5,7},{6,4},{7,5},{8,10},{9,11},{10,... | collective-permute-start | bytes 786440 | tf_op jit(solution)/shard_map/ppermute | solution.py:54
  21.1 11.7 %collective-permute-start.7 = (bf16[4,4,16,512]{3,2,1,0:T(8,128)(2,1)S(1)}, bf16[4,4,16,512]{3,2,1,0:T(8,128)(2,1)S(1)}, u32[]{:S(2)}, u32[]{:S(2)}) collective-permute-start(bf16[4,4,16,512]{3,2,1,0:T(8,128)(2,1)S(1)} %pad_maximum_fusion.5.refs_0_), channel_id=1, source_target_pairs={{0,4},{1,5},{2,6},{3,7},{4,0},{5,1},{6,2},{7,3},{8,12},{9,13},{10,... | collective-permute-start | bytes 786440 | tf_op jit(solution)/shard_map/ppermute | solution.py:54
  22.7 10.2 %collective-permute-start.8 = (bf16[4,4,16,512]{3,2,1,0:T(8,128)(2,1)S(1)}, bf16[4,4,16,512]{3,2,1,0:T(8,128)(2,1)S(1)}, u32[]{:S(2)}, u32[]{:S(2)}) collective-permute-start(bf16[4,4,16,512]{3,2,1,0:T(8,128)(2,1)S(1)} %pad_maximum_fusion.5.refs_0_), channel_id=1, source_target_pairs={{0,6},{1,7},{2,4},{3,5},{4,2},{5,3},{6,0},{7,1},{8,14},{9,15},{10,... | collective-permute-start | bytes 786440 | tf_op jit(solution)/shard_map/ppermute | solution.py:54
  31.1 2.0 copy-start
  31.2 2.7 %copy-start.9 = (bf16[4,4,16,512]{3,2,1,0:T(8,128)(2,1)}, bf16[4,4,16,512]{3,2,1,0:T(8,128)(2,1)S(1)}, u32[]{:S(2)}) copy-start(bf16[4,4,16,512]{3,2,1,0:T(8,128)(2,1)S(1)} %collective-permute-done.6.refs_1_) | copy-start | bytes 786436
  33.0 3.3 %collective-permute-start.9 = (bf16[16,4,16,512]{3,2,1,0:T(8,128)(2,1)S(1)}, bf16[16,4,16,512]{3,2,1,0:T(8,128)(2,1)}, u32[]{:S(2)}, u32[]{:S(2)}) collective-permute-start(bf16[16,4,16,512]{3,2,1,0:T(8,128)(2,1)S(1)} %pad_maximum_fusion), channel_id=1, source_target_pairs={{0,1},{1,0},{2,3},{3,2},{4,5},{5,4},{6,7},{7,6},{8,9},{9,8},{10,11... | collective-permute-start | bytes 3145736 | tf_op jit(solution)/shard_map/ppermute | solution.py:54
  33.9 13.0 %collective-permute-start.10 = (bf16[4,6,16,512]{3,2,1,0:T(8,128)(2,1)S(1)}, bf16[4,6,16,512]{3,2,1,0:T(8,128)(2,1)S(1)}, u32[]{:S(2)}, u32[]{:S(2)}) collective-permute-start(bf16[4,6,16,512]{3,2,1,0:T(8,128)(2,1)S(1)} %slice.315), channel_id=1, source_target_pairs={{0,2},{1,3},{2,0},{3,1},{4,6},{5,7},{6,4},{7,5},{8,10},{9,11},{10,... | collective-permute-start | bytes 1179656 | tf_op jit(solution)/shard_map/ppermute | solution.py:54
  35.2 11.7 %collective-permute-start.11 = (bf16[4,5,16,512]{3,2,1,0:T(8,128)(2,1)S(1)}, bf16[4,5,16,512]{3,2,1,0:T(8,128)(2,1)S(1)}, u32[]{:S(2)}, u32[]{:S(2)}) collective-permute-start(bf16[4,5,16,512]{3,2,1,0:T(8,128)(2,1)S(1)} %pad_maximum_fusion.4), channel_id=1, source_target_pairs={{0,4},{1,5},{2,6},{3,7},{4,0},{5,1},{6,2},{7,3},{8,12},{9,13},{10,... | collective-permute-start | bytes 983048 | tf_op jit(solution)/shard_map/ppermute | solution.py:54
  41.4 122.3 %copy-start.24 = (f32[1,512]{1,0:T(1,128)}, f32[1,512]{1,0:T(1,128)S(1)}, u32[]{:S(2)}) copy-start(f32[1,512]{1,0:T(1,128)S(1)} %get-tuple-element.163) | copy-start | bytes 6148
  41.8 3.4 %copy-start.2 = (bf16[1024,512]{1,0:T(8,128)(2,1)}, bf16[1024,512]{1,0:T(8,128)(2,1)S(1)}, u32[]{:S(2)}) copy-start(bf16[1024,512]{1,0:T(8,128)(2,1)S(1)} %fusion.7.h_ref) | copy-start | bytes 3145732
  46.9 3.8 %copy-start.22 = (s32[1024]{0:T(1024)S(1)}, s32[1024]{0:T(1024)}, u32[]{:S(2)}) copy-start(s32[1024]{0:T(1024)} %param.23) | copy-start | bytes 12292
  46.9 4.8 %copy-start.23 = (s32[1024]{0:T(1024)S(1)}, s32[1024]{0:T(1024)}, u32[]{:S(2)}) copy-start(s32[1024]{0:T(1024)} %param.24) | copy-start | bytes 12292
  47.8 19.7 %collective-permute-start.12 = (bf16[8,6,16,512]{3,2,1,0:T(8,128)(2,1)}, bf16[8,6,16,512]{3,2,1,0:T(8,128)(2,1)}, u32[]{:S(2)}, u32[]{:S(2)}) collective-permute-start(bf16[8,6,16,512]{3,2,1,0:T(8,128)(2,1)} %pad_maximum_fusion.1), channel_id=1, source_target_pairs={{0,4},{1,5},{2,6},{3,7},{4,0},{5,1},{6,2},{7,3},{8,12},{9,13},{10,... | collective-permute-start | bytes 2359304 | tf_op jit(solution)/shard_map/ppermute | solution.py:54
  49.8 17.1 %collective-permute-start.13 = (bf16[8,5,16,512]{3,2,1,0:T(8,128)(2,1)}, bf16[8,5,16,512]{3,2,1,0:T(8,128)(2,1)}, u32[]{:S(2)}, u32[]{:S(2)}) collective-permute-start(bf16[8,5,16,512]{3,2,1,0:T(8,128)(2,1)} %pad_maximum_fusion.3), channel_id=1, source_target_pairs={{0,2},{1,3},{2,0},{3,1},{4,6},{5,7},{6,4},{7,5},{8,10},{9,11},{10,... | collective-permute-start | bytes 1966088 | tf_op jit(solution)/shard_map/ppermute | solution.py:54
  68.7 7.6 %copy-start.4 = (bf16[16,6,16,512]{3,2,1,0:T(8,128)(2,1)}, bf16[16,6,16,512]{3,2,1,0:T(8,128)(2,1)S(1)}, u32[]{:S(2)}) copy-start(bf16[16,6,16,512]{3,2,1,0:T(8,128)(2,1)S(1)} %constant_dynamic-update-slice_fusion.6.refs_0_) | copy-start | bytes 4718596
  68.7 5.4 %collective-permute-start.14 = (bf16[16,6,16,512]{3,2,1,0:T(8,128)(2,1)S(1)}, bf16[16,6,16,512]{3,2,1,0:T(8,128)(2,1)S(1)}, u32[]{:S(2)}, u32[]{:S(2)}) collective-permute-start(bf16[16,6,16,512]{3,2,1,0:T(8,128)(2,1)S(1)} %constant_dynamic-update-slice_fusion.6.refs_0_), channel_id=1, source_target_pairs={{0,1},{1,0},{2,3},{3,2},{4,5},{5,4},{6,7},{7,6},{8,9},{9,8},{10,11... | collective-permute-start | bytes 4718600 | tf_op jit(solution)/shard_map/ppermute | solution.py:54
  70.4 3.7 %copy-start.6 = (bf16[16,5,16,512]{3,2,1,0:T(8,128)(2,1)}, bf16[16,5,16,512]{3,2,1,0:T(8,128)(2,1)S(1)}, u32[]{:S(2)}) copy-start(bf16[16,5,16,512]{3,2,1,0:T(8,128)(2,1)S(1)} %constant_dynamic-update-slice_fusion.9.refs_1_) | copy-start | bytes 3932164
  70.4 3.6 %collective-permute-start.15 = (bf16[16,5,16,512]{3,2,1,0:T(8,128)(2,1)S(1)}, bf16[16,5,16,512]{3,2,1,0:T(8,128)(2,1)S(1)}, u32[]{:S(2)}, u32[]{:S(2)}) collective-permute-start(bf16[16,5,16,512]{3,2,1,0:T(8,128)(2,1)S(1)} %constant_dynamic-update-slice_fusion.9.refs_1_), channel_id=1, source_target_pairs={{0,1},{1,0},{2,3},{3,2},{4,5},{5,4},{6,7},{7,6},{8,9},{9,8},{10,11... | collective-permute-start | bytes 3932168 | tf_op jit(solution)/shard_map/ppermute | solution.py:54
  75.2 1.1 copy-start.7
  107.1 5.6 %collective-permute-start.16 = (bf16[16,11,16,512]{3,2,1,0:T(8,128)(2,1)}, bf16[16,11,16,512]{3,2,1,0:T(8,128)(2,1)S(1)}, u32[]{:S(2)}, u32[]{:S(2)}) collective-permute-start(bf16[16,11,16,512]{3,2,1,0:T(8,128)(2,1)} %get-tuple-element.88), channel_id=1, source_target_pairs={{0,1},{1,0},{2,3},{3,2},{4,5},{5,4},{6,7},{7,6},{8,9},{9,8},{10,11... | collective-permute-start | bytes 8650760 | tf_op jit(solution)/shard_map/ppermute | solution.py:54
  117.0 33.0 %collective-permute-start.17 = (bf16[4,11,16,512]{3,2,1,0:T(8,128)(2,1)}, bf16[4,11,16,512]{3,2,1,0:T(8,128)(2,1)S(1)}, u32[]{:S(2)}, u32[]{:S(2)}) collective-permute-start(bf16[4,11,16,512]{3,2,1,0:T(8,128)(2,1)} %get-tuple-element.101), channel_id=1, source_target_pairs={{0,2},{1,3},{2,0},{3,1},{4,6},{5,7},{6,4},{7,5},{8,10},{9,11},{10,... | collective-permute-start | bytes 2162696 | tf_op jit(solution)/shard_map/ppermute | solution.py:54
  118.2 33.6 %collective-permute-start.18 = (bf16[4,11,16,512]{3,2,1,0:T(8,128)(2,1)}, bf16[4,11,16,512]{3,2,1,0:T(8,128)(2,1)S(1)}, u32[]{:S(2)}, u32[]{:S(2)}) collective-permute-start(bf16[4,11,16,512]{3,2,1,0:T(8,128)(2,1)} %get-tuple-element.102), channel_id=1, source_target_pairs={{0,4},{1,5},{2,6},{3,7},{4,0},{5,1},{6,2},{7,3},{8,12},{9,13},{10,... | collective-permute-start | bytes 2162696 | tf_op jit(solution)/shard_map/ppermute | solution.py:54
  119.1 32.7 %collective-permute-start.19 = (bf16[4,11,16,512]{3,2,1,0:T(8,128)(2,1)S(1)}, bf16[4,11,16,512]{3,2,1,0:T(8,128)(2,1)S(1)}, u32[]{:S(2)}, u32[]{:S(2)}) collective-permute-start(bf16[4,11,16,512]{3,2,1,0:T(8,128)(2,1)S(1)} %get-tuple-element.103), channel_id=1, source_target_pairs={{0,6},{1,7},{2,4},{3,5},{4,2},{5,3},{6,0},{7,1},{8,14},{9,15},{10,... | collective-permute-start | bytes 2162696 | tf_op jit(solution)/shard_map/ppermute | solution.py:54
  120.5 32.0 %copy-start.26 = (f32[1,2048]{1,0:T(1,128)S(1)}, f32[1,2048]{1,0:T(1,128)}, u32[]{:S(2)}) copy-start(f32[1,2048]{1,0:T(1,128)} %get-tuple-element.106) | copy-start | bytes 24580
  150.0 3.1 %copy-start.12 = (bf16[4,11,16,512]{3,2,1,0:T(8,128)(2,1)}, bf16[4,11,16,512]{3,2,1,0:T(8,128)(2,1)S(1)}, u32[]{:S(2)}) copy-start(bf16[4,11,16,512]{3,2,1,0:T(8,128)(2,1)S(1)} %collective-permute-done.17) | copy-start | bytes 2162692
  151.8 1.4 copy-start.13
  151.8 1.4 copy-start.14
  151.8 6.6 %collective-permute-start.23 = (bf16[16,3,16,512]{3,2,1,0:T(8,128)(2,1)}, bf16[16,3,16,512]{3,2,1,0:T(8,128)(2,1)}, u32[]{:S(2)}, u32[]{:S(2)}) collective-permute-start(bf16[16,3,16,512]{3,2,1,0:T(8,128)(2,1)} %get-tuple-element.112), channel_id=1, source_target_pairs={{0,1},{1,0},{2,3},{3,2},{4,5},{5,4},{6,7},{7,6},{8,9},{9,8},{10,11... | collective-permute-start | bytes 2359304 | tf_op jit(solution)/shard_map/ppermute | solution.py:54
  153.2 10.5 %copy-start.1 = (bf16[1024,512]{1,0:T(8,128)(2,1)S(1)}, bf16[1024,512]{1,0:T(8,128)(2,1)}, u32[]{:S(2)}) copy-start(bf16[1024,512]{1,0:T(8,128)(2,1)} %x_ref.1) | copy-start | bytes 3145732
  153.2 10.5 %copy-start.3 = (f32[1024,512]{1,0:T(8,128)S(1)}, f32[1024,512]{1,0:T(8,128)}, u32[]{:S(2)}) copy-start(f32[1024,512]{1,0:T(8,128)} %get-tuple-element.104) | copy-start | bytes 6291460
  155.4 19.0 %collective-permute-start.20 = (bf16[11,16,512]{2,1,0:T(8,128)(2,1)S(1)}, bf16[11,16,512]{2,1,0:T(8,128)(2,1)S(1)}, u32[]{:S(2)}, u32[]{:S(2)}) collective-permute-start(bf16[11,16,512]{2,1,0:T(8,128)(2,1)S(1)} %get-tuple-element.143), channel_id=1, source_target_pairs={{0,8},{1,9},{2,10},{3,11},{4,12},{5,13},{6,14},{7,15},{8,0},{9,1},... | collective-permute-start | bytes 540680 | tf_op jit(solution)/shard_map/ppermute | solution.py:54
  157.0 19.8 %collective-permute-start.21 = (bf16[11,16,512]{2,1,0:T(8,128)(2,1)S(1)}, bf16[11,16,512]{2,1,0:T(8,128)(2,1)S(1)}, u32[]{:S(2)}, u32[]{:S(2)}) collective-permute-start(bf16[11,16,512]{2,1,0:T(8,128)(2,1)S(1)} %get-tuple-element.145), channel_id=1, source_target_pairs={{0,16},{1,17},{2,18},{3,19},{4,20},{5,21},{6,22},{7,23},{8,24},{9,... | collective-permute-start | bytes 540680 | tf_op jit(solution)/shard_map/ppermute | solution.py:54
  160.1 7.8 %collective-permute-start.24 = (bf16[4,3,16,512]{3,2,1,0:T(8,128)(2,1)S(1)}, bf16[4,3,16,512]{3,2,1,0:T(8,128)(2,1)S(1)}, u32[]{:S(2)}, u32[]{:S(2)}) collective-permute-start(bf16[4,3,16,512]{3,2,1,0:T(8,128)(2,1)S(1)} %get-tuple-element.146), channel_id=1, source_target_pairs={{0,2},{1,3},{2,0},{3,1},{4,6},{5,7},{6,4},{7,5},{8,10},{9,11},{10,... | collective-permute-start | bytes 589832 | tf_op jit(solution)/shard_map/ppermute | solution.py:54
  161.3 9.4 %collective-permute-start.25 = (bf16[4,3,16,512]{3,2,1,0:T(8,128)(2,1)S(1)}, bf16[4,3,16,512]{3,2,1,0:T(8,128)(2,1)S(1)}, u32[]{:S(2)}, u32[]{:S(2)}) collective-permute-start(bf16[4,3,16,512]{3,2,1,0:T(8,128)(2,1)S(1)} %get-tuple-element.148), channel_id=1, source_target_pairs={{0,4},{1,5},{2,6},{3,7},{4,0},{5,1},{6,2},{7,3},{8,12},{9,13},{10,... | collective-permute-start | bytes 589832 | tf_op jit(solution)/shard_map/ppermute | solution.py:54
  162.2 10.0 %collective-permute-start.26 = (bf16[4,3,16,512]{3,2,1,0:T(8,128)(2,1)S(1)}, bf16[4,3,16,512]{3,2,1,0:T(8,128)(2,1)S(1)}, u32[]{:S(2)}, u32[]{:S(2)}) collective-permute-start(bf16[4,3,16,512]{3,2,1,0:T(8,128)(2,1)S(1)} %get-tuple-element.147), channel_id=1, source_target_pairs={{0,6},{1,7},{2,4},{3,5},{4,2},{5,3},{6,0},{7,1},{8,14},{9,15},{10,... | collective-permute-start | bytes 589832 | tf_op jit(solution)/shard_map/ppermute | solution.py:54
  168.0 8.9 %collective-permute-start.22 = (bf16[11,16,512]{2,1,0:T(8,128)(2,1)S(1)}, bf16[11,16,512]{2,1,0:T(8,128)(2,1)S(1)}, u32[]{:S(2)}, u32[]{:S(2)}) collective-permute-start(bf16[11,16,512]{2,1,0:T(8,128)(2,1)S(1)} %get-tuple-element.144), channel_id=1, source_target_pairs={{0,24},{1,25},{2,26},{3,27},{4,28},{5,29},{6,30},{7,31},{8,16},{9,... | collective-permute-start | bytes 540680 | tf_op jit(solution)/shard_map/ppermute | solution.py:54
  172.4 6.5 %collective-permute-start.27 = (bf16[3,16,512]{2,1,0:T(8,128)(2,1)S(1)}, bf16[3,16,512]{2,1,0:T(8,128)(2,1)S(1)}, u32[]{:S(2)}, u32[]{:S(2)}) collective-permute-start(bf16[3,16,512]{2,1,0:T(8,128)(2,1)S(1)} %get-tuple-element.153), channel_id=1, source_target_pairs={{0,8},{1,9},{2,10},{3,11},{4,12},{5,13},{6,14},{7,15},{8,0},{9,1},... | collective-permute-start | bytes 147464 | tf_op jit(solution)/shard_map/ppermute | solution.py:54
  174.1 7.1 %collective-permute-start.28 = (bf16[3,16,512]{2,1,0:T(8,128)(2,1)S(1)}, bf16[3,16,512]{2,1,0:T(8,128)(2,1)S(1)}, u32[]{:S(2)}, u32[]{:S(2)}) collective-permute-start(bf16[3,16,512]{2,1,0:T(8,128)(2,1)S(1)} %get-tuple-element.155), channel_id=1, source_target_pairs={{0,16},{1,17},{2,18},{3,19},{4,20},{5,21},{6,22},{7,23},{8,24},{9,... | collective-permute-start | bytes 147464 | tf_op jit(solution)/shard_map/ppermute | solution.py:54
  174.4 6.8 %collective-permute-start.29 = (bf16[3,16,512]{2,1,0:T(8,128)(2,1)S(1)}, bf16[3,16,512]{2,1,0:T(8,128)(2,1)S(1)}, u32[]{:S(2)}, u32[]{:S(2)}) collective-permute-start(bf16[3,16,512]{2,1,0:T(8,128)(2,1)S(1)} %get-tuple-element.154), channel_id=1, source_target_pairs={{0,24},{1,25},{2,26},{3,27},{4,28},{5,29},{6,30},{7,31},{8,16},{9,... | collective-permute-start | bytes 147464 | tf_op jit(solution)/shard_map/ppermute | solution.py:54
  186.0 1.3 collective-permute-start.30
  188.1 3.9 %collective-permute-start.31 = (f32[12,512]{1,0:T(8,128)S(1)}, f32[12,512]{1,0:T(8,128)S(1)}, u32[]{:S(2)}, u32[]{:S(2)}) collective-permute-start(f32[12,512]{1,0:T(8,128)S(1)} %add.364), channel_id=1, source_target_pairs={{0,2},{1,3},{2,0},{3,1},{4,6},{5,7},{6,4},{7,5},{8,10},{9,11},{10,... | collective-permute-start | bytes 73736 | tf_op jit(solution)/shard_map/ppermute | solution.py:54
  192.0 3.9 %collective-permute-start.32 = (f32[12,512]{1,0:T(8,128)S(1)}, f32[12,512]{1,0:T(8,128)S(1)}, u32[]{:S(2)}, u32[]{:S(2)}) collective-permute-start(f32[12,512]{1,0:T(8,128)S(1)} %add.365), channel_id=1, source_target_pairs={{0,4},{1,5},{2,6},{3,7},{4,0},{5,1},{6,2},{7,3},{8,12},{9,13},{10,... | collective-permute-start | bytes 73736 | tf_op jit(solution)/shard_map/ppermute | solution.py:54
  195.9 5.1 %collective-permute-start.33 = (f32[12,512]{1,0:T(8,128)S(1)}, f32[12,512]{1,0:T(8,128)S(1)}, u32[]{:S(2)}, u32[]{:S(2)}) collective-permute-start(f32[12,512]{1,0:T(8,128)S(1)} %add.366), channel_id=1, source_target_pairs={{0,8},{1,9},{2,10},{3,11},{4,12},{5,13},{6,14},{7,15},{8,0},{9,1},... | collective-permute-start | bytes 73736 | tf_op jit(solution)/shard_map/ppermute | solution.py:54
  200.9 11.0 %copy-start.29 = (f32[64]{0:T(128)S(1)}, f32[64]{0:T(128)}, u32[]{:S(2)}) copy-start(f32[64]{0:T(128)} %param.41) | copy-start | bytes 772
  200.9 11.0 %copy-start.30 = (f32[64]{0:T(128)S(1)}, f32[64]{0:T(128)}, u32[]{:S(2)}) copy-start(f32[64]{0:T(128)} %param.42) | copy-start | bytes 772
  200.9 11.0 %copy-start.31 = (f32[64]{0:T(128)S(1)}, f32[64]{0:T(128)}, u32[]{:S(2)}) copy-start(f32[64]{0:T(128)} %param.43) | copy-start | bytes 772
  200.9 11.6 %copy-start.25 = (f32[7,16]{1,0:T(8,128)S(1)}, f32[7,16]{1,0:T(8,128)}, u32[]{:S(2)}) copy-start(f32[7,16]{1,0:T(8,128)} %param.38) | copy-start | bytes 1348
  200.9 11.6 %copy-start.27 = (f32[7,16]{1,0:T(8,128)S(1)}, f32[7,16]{1,0:T(8,128)}, u32[]{:S(2)}) copy-start(f32[7,16]{1,0:T(8,128)} %param.39) | copy-start | bytes 1348
  200.9 11.6 %copy-start.28 = (f32[7,16]{1,0:T(8,128)S(1)}, f32[7,16]{1,0:T(8,128)}, u32[]{:S(2)}) copy-start(f32[7,16]{1,0:T(8,128)} %param.40) | copy-start | bytes 1348
  201.0 12.3 %copy-start.15 = (f32[4,16,512]{2,1,0:T(8,128)S(1)}, f32[4,16,512]{2,1,0:T(8,128)}, u32[]{:S(2)}) copy-start(f32[4,16,512]{2,1,0:T(8,128)} %param.26) | copy-start | bytes 393220
  201.0 12.3 %copy-start.17 = (f32[3,16,512]{2,1,0:T(8,128)S(1)}, f32[3,16,512]{2,1,0:T(8,128)}, u32[]{:S(2)}) copy-start(f32[3,16,512]{2,1,0:T(8,128)} %get-tuple-element.136) | copy-start | bytes 294916
  201.0 12.3 %copy-start.18 = (f32[4,16,512]{2,1,0:T(8,128)S(1)}, f32[4,16,512]{2,1,0:T(8,128)}, u32[]{:S(2)}) copy-start(f32[4,16,512]{2,1,0:T(8,128)} %param.27) | copy-start | bytes 393220
  201.0 12.3 %copy-start.19 = (f32[4,16,512]{2,1,0:T(8,128)S(1)}, f32[4,16,512]{2,1,0:T(8,128)}, u32[]{:S(2)}) copy-start(f32[4,16,512]{2,1,0:T(8,128)} %param.28) | copy-start | bytes 393220
  201.0 13.1 %copy-start.16 = (f32[16,2048]{1,0:T(8,128)S(1)}, f32[16,2048]{1,0:T(8,128)}, u32[]{:S(2)}) copy-start(f32[16,2048]{1,0:T(8,128)} %param.32) | copy-start | bytes 393220
  201.0 13.1 %copy-start.20 = (f32[16,2048]{1,0:T(8,128)S(1)}, f32[16,2048]{1,0:T(8,128)}, u32[]{:S(2)}) copy-start(f32[16,2048]{1,0:T(8,128)} %param.33) | copy-start | bytes 393220
  201.0 13.1 %copy-start.21 = (f32[16,2048]{1,0:T(8,128)S(1)}, f32[16,2048]{1,0:T(8,128)}, u32[]{:S(2)}) copy-start(f32[16,2048]{1,0:T(8,128)} %param.34) | copy-start | bytes 393220
  201.1 4.9 %collective-permute-start.34 = (f32[12,512]{1,0:T(8,128)S(1)}, f32[12,512]{1,0:T(8,128)S(1)}, u32[]{:S(2)}, u32[]{:S(2)}) collective-permute-start(f32[12,512]{1,0:T(8,128)S(1)} %add.367), channel_id=1, source_target_pairs={{0,16},{1,17},{2,18},{3,19},{4,20},{5,21},{6,22},{7,23},{8,24},{9,... | collective-permute-start | bytes 73736 | tf_op jit(solution)/shard_map/ppermute | solution.py:54
  (3 other events, 3.1 us)
where the time goes:
time: 217 us; the launch traced here: 216 us
  Pallas kernels  77.2 us (36%)
  starting transfers between devices  41.1 us (19%)
  waiting for transfers between devices  38.4 us (18%)
  other arithmetic  33.2 us (15%)
  local copies, waits for them, and re-layouts  15.9 us (7%)
  between operations  5.11 us (2%)
  matrix products  5.04 us (2%)
    ppermute x35, starting transfers between devices, swap_with(): lax.ppermute(array, AXES, [(source, source ^ offset) for source in range(...  41.1 us
    ppermute x35, waiting for transfers between devices, swap_with(): lax.ppermute(array, AXES, [(source, source ^ offset) for source in range(...  38.4 us
    pallas_call x1, Pallas kernels, ffn(): pl.pallas_call(functools.partial(ffn_kernel, direct, len(parts), tables,...  30.7 us
    pallas_call x1, Pallas kernels, attend_back(): pl.pallas_call(functools.partial(attn_bwd_kernel, offsets), grid=(width /...  29.5 us
    pallas_call x1, Pallas kernels, attend(): pl.pallas_call(attn_fwd_kernel, grid=(pairs,), in_specs=[col, col, row, r...  14.2 us
    sub x6, other arithmetic, adam_update(): weight - step_rate * (corrected / (jnp.sqrt(spread) + adam_eps) + weight_...  6.36 us
    convert_element_type x2, other arithmetic, plane_sums(): total(offset).astype(jnp.bfloat16)  6.08 us
    convert_element_type x4, other arithmetic, body(): low = lambda value: value.astype(jnp.bfloat16)  5.21 us
  transfers between devices with their start and end apart: 35, of which 16 were waited for; matrix products, arithmetic and copies ran while one was open for 14% of the time, Pallas kernels for 22%

commit v1 on v0

--- a/solution.py
+++ b/solution.py
@@ -653,6 +653,62 @@
     return (weight_new, first_new, second_new)
 
 
+def own_lanes(rows, first, lanes):
+    width = rows.shape[1]
+    return pltpu.roll(rows, (width - first) % width, 1)[:, :lanes]
+
+
+def update_kernel(own_ref, payload_ref, a_ref, b_ref, *refs):
+    states = [refs[3 * index : 3 * index + 3] for index in range(6)]
+    norm_ref = refs[18]
+    news = [refs[19 + 3 * index : 22 + 3 * index] for index in range(6)]
+    squares = payload_ref[:11, :] * payload_ref[:11, :]
+    total = jnp.sum(jnp.sum(squares, 1, keepdims=True), 0, keepdims=True)
+    norm = jnp.sqrt(total + payload_ref[11:12, 0:1])
+    norm_ref[...] = norm
+    factor = jnp.minimum(1.0, clip_norm / (norm + 1e-06))
+
+    def update(index, where, gradient):
+        rate = vector_rate if index > 3 else learn_rate
+        values = adam_update(*[ref[where] for ref in states[index]], gradient, factor, rate)
+        for ref, value in zip(news[index], values):
+            ref[where] = value
+
+    width = a_ref.shape[2]
+    for piece in range(3):
+        update(0, piece, a_ref[piece])
+    update(0, 3, b_ref[0])
+    for piece in range(2):
+        update(1, piece, b_ref[1 + piece])
+    chunks = (b_ref.shape[0] - 3) // 2
+    step = b_ref.shape[1]
+    for chunk in range(chunks):
+        update(2, (slice(None), slice(chunk * width, (chunk + 1) * width)), b_ref[3 + chunk])
+        update(3, slice(chunk * step, (chunk + 1) * step), b_ref[3 + chunks + chunk])
+    own = own_ref[0]
+    vec_lanes = states[4][0].shape[1]
+    update(4, Ellipsis, own_lanes(payload_ref[0:8, :], own * vec_lanes, vec_lanes)[:7])
+    bias_lanes = states[5][0].shape[1]
+    first = own * bias_lanes
+    line = lax.broadcasted_iota(jnp.int32, (5, width), 0)
+    picked = jnp.sum(jnp.where(line == first // width, payload_ref[7:12, :], 0.0), 0, keepdims=True)
+    picked = own_lanes(jnp.broadcast_to(picked, (8, width)), first % width, bias_lanes)
+    update(5, Ellipsis, picked[0:1])
+
+
+def update_all(own, payload, total_a, total_b, states):
+    flat = [value for state in states for value in state]
+    shapes = [jax.ShapeDtypeStruct(value.shape, jnp.float32) for value in flat]
+    norm, *news = pl.pallas_call(
+        update_kernel,
+        in_specs=[smem_spec()] + [vmem_spec() for _ in range(3 + len(flat))],
+        out_specs=[vmem_spec() for _ in range(1 + len(flat))],
+        out_shape=[jax.ShapeDtypeStruct((1, 1), jnp.float32)] + shapes,
+        name="update",
+    )(own[None].astype(jnp.int32), payload, total_a, total_b, *flat)
+    return norm[0, 0], [news[3 * index : 3 * index + 3] for index in range(len(states))]
+
+
 def body(
     groups,
     tokens,
@@ -754,12 +810,17 @@
     kept_a, sent_a, grad_normed, own_b, *plane_b = tie(kept_a, sent_a, grad_normed, own_b, *plane_b)
     core_a = swap_with(sent_a, 1, count)
     own_b, z_b = reduce_z(own_b, plane_b, groups)
+    own_a, parts_a = plane_sums(kept_a, core_a, groups)
+    grad_normed, own_a, *parts_a = tie(grad_normed, own_a, *parts_a)
     grad_gain_one = jnp.sum(grad_normed * unit_one, 0)
     grad_shift_one = jnp.sum(grad_normed, 0)
     grad_inputs = grad_inputs + normalize_back(grad_normed, unit_one, scale_one, vectors[0])
     input_grad = low(grad_inputs)
-    own_a, parts_a = plane_sums(kept_a, core_a, groups)
     plane_a = plane_send(parts_a, groups)
+    input_grad, grad_gain_one, grad_shift_one, *arrived = tie(
+        input_grad, grad_gain_one, grad_shift_one, *z_b, *plane_a
+    )
+    z_b, plane_a = arrived[: len(z_b)], arrived[len(z_b) :]
     own_a, z_a = reduce_z(own_a, plane_a, groups)
     total_b = reduce_end(own_b, z_b)
     total_a = reduce_end(own_a, z_a)
@@ -774,32 +835,15 @@
         ]
     )
     payload = sum_all(payload, groups)
-    own_small = payload[:11]
-    own_vec = lax.dynamic_slice(own_small[:7], (0, own * step), (7, step))
-    own_bias = lax.dynamic_slice(own_small[7:11].reshape(-1), (own * 4 * step,), (4 * step,))
-    owned = (
-        jnp.concatenate([total_a, total_b[:1]]),
-        total_b[1:3],
-        jnp.concatenate(list(total_b[3:7]), 1),
-        total_b[7:].reshape(4 * step, width),
-        own_vec,
-        own_bias,
-    )
-    grad_norm = jnp.sqrt(payload[11, 0] + jnp.sum(own_small * own_small))
-    factor = jnp.minimum(1.0, clip_norm / (grad_norm + 1e-06))
     states = (
         (attn_weight, attn_m, attn_v),
         (gate_weight, gate_m, gate_v),
         (in_weight, in_m, in_v),
         (out_weight, out_m, out_v),
         (norm_params, norm_m, norm_v),
-        (in_bias, bias_m, bias_v),
-    )
-    step_rates = (learn_rate, learn_rate, learn_rate, learn_rate, vector_rate, vector_rate)
-    updated = [
-        adam_update(state[0], state[1], state[2], gradient, factor, step_rate)
-        for state, gradient, step_rate in zip(states, owned, step_rates)
-    ]
+        (in_bias[None], bias_m[None], bias_v[None]),
+    )
+    grad_norm, updated = update_all(own, payload, total_a, total_b, states)
     return (
         layer_out,
         input_grad,
@@ -819,9 +863,9 @@
         updated[4][0],
         updated[4][1],
         updated[4][2],
-        updated[5][0],
-        updated[5][1],
-        updated[5][2],
+        updated[5][0][0],
+        updated[5][1][0],
+        updated[5][2][0],
     )
 
 

time: 217 us -> 209 us (0.963)
  other arithmetic: 33.2 us -> 21.7 us
  waiting for transfers between devices: 38.4 us -> 42.9 us
  Pallas kernels: 77.2 us -> 80.2 us
  local copies, waits for them, and re-layouts: 15.9 us -> 13.2 us
  between operations: 5.11 us -> 2.68 us
    sub x6 -> x0, other arithmetic: 6.36 us -> none  [adam_update(): weight - step_rate * (corrected / (jnp.sqrt(spread) + adam_eps) + weight_...]
    ppermute x35, waiting for transfers between devices: 38.4 us -> 42.9 us  [swap_with(): lax.ppermute(array, AXES, [(source, source ^ offset) for source in range(...]
    pallas_call x0 -> x1, Pallas kernels: none -> 2.97 us  [update_all(): pl.pallas_call(update_kernel, in_specs=[smem_spec()] + [vmem_spec() for _...]
  transfers between devices with their start and end apart: 35 -> 35, of which waited for: 16 -> 18; matrix products, arithmetic and copies ran while one was open for 14% -> 13% of each run, Pallas kernels for 22% -> 22%
where the time goes in v1:
time: 209 us
  Pallas kernels  80.2 us (38%)
  waiting for transfers between devices  42.9 us (21%)
  starting transfers between devices  42.8 us (20%)
  other arithmetic  21.7 us (10%)
  local copies, waits for them, and re-layouts  13.2 us (6%)
  matrix products  5.11 us (2%)
  between operations  2.68 us (1%)
    ppermute x35, waiting for transfers between devices, swap_with(): lax.ppermute(array, AXES, [(source, source ^ offset) for source in range(...  42.9 us
    ppermute x35, starting transfers between devices, swap_with(): lax.ppermute(array, AXES, [(source, source ^ offset) for source in range(...  42.8 us
    pallas_call x1, Pallas kernels, ffn(): pl.pallas_call(functools.partial(ffn_kernel, direct, len(parts), tables,...  30.7 us
    pallas_call x1, Pallas kernels, attend_back(): pl.pallas_call(functools.partial(attn_bwd_kernel, offsets), grid=(width /...  29.5 us
    pallas_call x1, Pallas kernels, attend(): pl.pallas_call(attn_fwd_kernel, grid=(pairs,), in_specs=[col, col, row, r...  14.2 us
    dot_general x3, matrix products, body(): dot('td,de->te', normed, w_qkv[j])  5.11 us
    convert_element_type x2, other arithmetic, plane_sums(): total(offset).astype(jnp.bfloat16)  4.4 us
  transfers between devices with their start and end apart: 35, of which 18 were waited for; matrix products, arithmetic and copies ran while one was open for 13% of the time, Pallas kernels for 22%

profile of v1, /device:TPU:0, one launch (start us, length us, event | category | flops | bytes accessed | tf_op | source)
XLA Modules:
  0.0 208.5 jit_solution(8539662003221389384)
XLA Ops:
  2.3 0.9 convert.28
  3.4 3.1 %collective-permute-start = (bf16[4,16,512]{2,1,0:T(8,128)(2,1)S(1)}, bf16[4,16,512]{2,1,0:T(8,128)(2,1)S(1)}, u32[]{:S(2)}, u32[]{:S(2)}) collective-permute-start(bf16[4,16,512]{2,1,0:T(8,128)(2,1)S(1)} %get-tuple-element.205), channel_id=1, source_target_pairs={{0,8},{1,9},{2,10},{3,11},{4,12},{5,13},{6,14},{7,15},{8,0},{9,1},... | collective-permute-start | bytes 196616 | tf_op jit(solution)/shard_map/ppermute | solution.py:54
  6.5 2.6 %collective-permute-start.1 = (bf16[4,16,512]{2,1,0:T(8,128)(2,1)S(1)}, bf16[4,16,512]{2,1,0:T(8,128)(2,1)S(1)}, u32[]{:S(2)}, u32[]{:S(2)}) collective-permute-start(bf16[4,16,512]{2,1,0:T(8,128)(2,1)S(1)} %get-tuple-element.205), channel_id=1, source_target_pairs={{0,16},{1,17},{2,18},{3,19},{4,20},{5,21},{6,22},{7,23},{8,24},{9,... | collective-permute-start | bytes 196616 | tf_op jit(solution)/shard_map/ppermute | solution.py:54
  9.1 0.9 convert_element_type.220
  10.9 0.9 convert_element_type.221
  11.8 1.9 collective-permute-done.1
  13.7 1.4 collective-permute-done.2
  15.3 2.3 %collective-permute-start.4 = (bf16[11,16,512]{2,1,0:T(8,128)(2,1)S(1)}, bf16[11,16,512]{2,1,0:T(8,128)(2,1)S(1)}, u32[]{:S(2)}, u32[]{:S(2)}) collective-permute-start(bf16[11,16,512]{2,1,0:T(8,128)(2,1)S(1)} %constant_dynamic-update-slice_fusion), channel_id=1, source_target_pairs={{0,16},{1,17},{2,18},{3,19},{4,20},{5,21},{6,22},{7,23},{8,24},{9,... | collective-permute-start | bytes 540680 | tf_op jit(solution)/shard_map/ppermute | solution.py:54
  17.6 2.0 collective-permute-start.5
  19.6 1.5 collective-permute-start.6
  21.1 1.5 collective-permute-start.7
  22.7 2.3 %collective-permute-start.8 = (bf16[4,4,16,512]{3,2,1,0:T(8,128)(2,1)S(1)}, bf16[4,4,16,512]{3,2,1,0:T(8,128)(2,1)S(1)}, u32[]{:S(2)}, u32[]{:S(2)}) collective-permute-start(bf16[4,4,16,512]{3,2,1,0:T(8,128)(2,1)S(1)} %pad_maximum_fusion.5.refs_0_), channel_id=1, source_target_pairs={{0,6},{1,7},{2,4},{3,5},{4,2},{5,3},{6,0},{7,1},{8,14},{9,15},{10,... | collective-permute-start | bytes 786440 | tf_op jit(solution)/shard_map/ppermute | solution.py:54
  24.9 6.0 %collective-permute-done.4 = bf16[11,16,512]{2,1,0:T(8,128)(2,1)S(1)} collective-permute-done((bf16[11,16,512]{2,1,0:T(8,128)(2,1)S(1)}, bf16[11,16,512]{2,1,0:T(8,128)(2,1)S(1)}, u32[]{:S(2)}, u32[]{:S(2)}) %collective-permute-start.4) | collective-permute-done | bytes 180256 | tf_op jit(solution)/shard_map/ppermute | solution.py:54
  31.2 1.7 collective-permute-done.7.refs_2_
  33.9 1.3 collective-permute-start.10
  35.2 1.1 collective-permute-start.11
  36.3 2.8 %place.1 = (bf16[3,32,16,512]{3,2,1,0:T(8,128)(2,1)}, f32[16,512]{1,0:T(8,128)}) custom-call(s32[1]{0:T(128)} %bitcast.own_ref, bf16[4,4,16,512]{3,2,1,0:T(8,128)(2,1)} %copy-done.5, bf16[4,4,16,512]{3,2,1,0:T(8,128)(2,1)} %copy-done.10, bf16[4,4,16,512]{3,2,1,0:T(8,128)(2,1)} %copy-done.11, bf16[4,4,16,512]{3,2,1,0:T(8,128)(2,1)} %copy-done.12, ...), custom_call_target="tpu_custom_call" | custom-call | tf_op jit(solution)/shard_map/place/pallas_call | solution.py:183
  39.1 1.5 fusion.33
  41.9 1.7 convolution_convert_fusion.v_ref
  43.6 1.7 convolution_convert_fusion.1.k_ref
  45.3 1.7 convolution_convert_fusion.2.q_ref
  47.0 0.9 pad_maximum_fusion.1
  47.9 1.1 collective-permute-start.12
  50.7 1.0 copy.43.segc
  51.8 1.0 copy.44.posc
  52.8 14.2 %attn_fwd.1 = (bf16[1024,512]{1,0:T(8,128)(2,1)}, f32[4,2,1024]{2,1,0:T(2,128)}) custom-call(s32[1024,1]{1,0:T(8,128)} %copy.43.segc, s32[1024,1]{1,0:T(8,128)} %copy.44.posc, s32[1,1024]{1,0:T(1,128)} %bitcast.93, s32[1,1024]{1,0:T(1,128)} %bitcast.96, bf16[1024,512]{1,0:T(8,128)(2,1)} %convolution_convert_fusion.2.q_ref, ...), custom_call_target="tpu_custom_call" | custom-call | tf_op jit(solution)/shard_map/attn_fwd/pallas_call | solution.py:409
  67.6 1.2 constant_dynamic-update-slice_fusion.6.refs_0_
  69.0 1.6 constant_dynamic-update-slice_fusion.9.refs_1_
  72.1 2.1 %collective-permute-done.15.refs_3_ = bf16[16,5,16,512]{3,2,1,0:T(8,128)(2,1)S(1)} collective-permute-done((bf16[16,5,16,512]{3,2,1,0:T(8,128)(2,1)S(1)}, bf16[16,5,16,512]{3,2,1,0:T(8,128)(2,1)S(1)}, u32[]{:S(2)}, u32[]{:S(2)}) %collective-permute-start.15) | collective-permute-done | bytes 1310752 | tf_op jit(solution)/shard_map/ppermute | solution.py:54
  74.2 1.1 copy-done.9
  75.2 1.1 copy-done.8
  76.4 30.7 %ffn.1 = (bf16[1024,512]{1,0:T(8,128)(2,1)}, bf16[1024,512]{1,0:T(8,128)(2,1)}, f32[1024,512]{1,0:T(8,128)}, f32[1024,512]{1,0:T(8,128)}, f32[8,512]{1,0:T(8,128...) custom-call(s32[1]{0:T(128)} %bitcast.own_ref, ...), custom_call_target="tpu_custom_call" | custom-call | tf_op jit(solution)/shard_map/ffn/pallas_call | solution.py:626
  107.3 5.4 %collective-permute-done.16 = bf16[16,11,16,512]{3,2,1,0:T(8,128)(2,1)S(1)} collective-permute-done((bf16[16,11,16,512]{3,2,1,0:T(8,128)(2,1)}, bf16[16,11,16,512]{3,2,1,0:T(8,128)(2,1)S(1)}, u32[]{:S(2)}, u32[]{:S(2)}) %collective-permute-start.16) | collective-permute-done | bytes 2883616 | tf_op jit(solution)/shard_map/ppermute | solution.py:54
  112.7 4.1 %add_convert_fusion = (bf16[4,11,16,512]{3,2,1,0:T(8,128)(2,1)}, bf16[4,11,16,512]{3,2,1,0:T(8,128)(2,1)}, bf16[4,11,16,512]{3,2,1,0:T(8,128)(2,1)}, f32[4,11,16,512]{3,2,1,0:T(8,128)S(1)}) fusion(bf16[16,11,16,512]{3,2,1,0:T(8,128)(2,1)S(1)} %collective-permute-done.16, bf16[16,11,16,512]{3,2,1,0:T(8,128)(2,1)} %get-tuple-element.125), kind=kLoop, calls=%fused_computation.21 | loop fusion | flops 5406720 | bytes 9371648 | tf_op jit(solution)/shard_map/convert_element_type | solution.py:248
  116.8 1.2 collective-permute-start.17
  118.9 1.4 collective-permute-start.19
  120.3 29.5 %attn_bwd.1 = (bf16[16,3,16,512]{3,2,1,0:T(8,128)(2,1)}, bf16[16,3,16,512]{3,2,1,0:T(8,128)(2,1)}, f32[1024,512]{1,0:T(8,128)}) custom-call(s32[1]{0:T(128)} %bitcast.own_ref, s32[1024,1]{1,0:T(8,128)} %copy.43.segc, s32[1024,1]{1,0:T(8,128)} %copy.44.posc, s32[1,1024]{1,0:T(1,128)} %bitcast.94, s32[1,1024]{1,0:T(1,128)} %bitcast.97, ...), custom_call_target="tpu_custom_call" | custom-call | tf_op jit(solution)/shard_map/attn_bwd/pallas_call | solution.py:437
  149.8 1.9 collective-permute-done.18
  152.9 2.0 fusion.17
  154.9 1.6 collective-permute-start.21
  156.5 1.4 collective-permute-start.22
  157.9 1.5 collective-permute-start.23
  159.7 1.2 fusion.13
  161.0 1.2 collective-permute-start.24
  162.2 1.0 collective-permute-start.25
  163.1 2.4 %collective-permute-done.21 = bf16[11,16,512]{2,1,0:T(8,128)(2,1)S(1)} collective-permute-done((bf16[11,16,512]{2,1,0:T(8,128)(2,1)S(1)}, bf16[11,16,512]{2,1,0:T(8,128)(2,1)S(1)}, u32[]{:S(2)}, u32[]{:S(2)}) %collective-permute-start.21) | collective-permute-done | bytes 180256 | tf_op jit(solution)/shard_map/ppermute | solution.py:54
  165.5 1.5 collective-permute-start.26
  167.1 1.7 fusion.12
  168.8 3.8 %collective-permute-done.22 = bf16[11,16,512]{2,1,0:T(8,128)(2,1)S(1)} collective-permute-done((bf16[11,16,512]{2,1,0:T(8,128)(2,1)S(1)}, bf16[11,16,512]{2,1,0:T(8,128)(2,1)S(1)}, u32[]{:S(2)}, u32[]{:S(2)}) %collective-permute-start.22) | collective-permute-done | bytes 180256 | tf_op jit(solution)/shard_map/ppermute | solution.py:54
  173.0 3.5 %collective-permute-start.27 = (bf16[3,16,512]{2,1,0:T(8,128)(2,1)S(1)}, bf16[3,16,512]{2,1,0:T(8,128)(2,1)S(1)}, u32[]{:S(2)}, u32[]{:S(2)}) collective-permute-start(bf16[3,16,512]{2,1,0:T(8,128)(2,1)S(1)} %get-tuple-element.201), channel_id=1, source_target_pairs={{0,8},{1,9},{2,10},{3,11},{4,12},{5,13},{6,14},{7,15},{8,0},{9,1},... | collective-permute-start | bytes 147464 | tf_op jit(solution)/shard_map/ppermute | solution.py:54
  176.4 1.4 collective-permute-start.28
  177.8 1.4 collective-permute-start.29
  179.2 2.6 %multiply_reduce_fusion.1 = (f32[]{:T(128)}, f32[11,16,512]{2,1,0:T(8,128)}) fusion(bf16[11,16,512]{2,1,0:T(8,128)(2,1)S(1)} %collective-permute-done.23, bf16[11,16,512]{2,1,0:T(8,128)(2,1)S(1)} %collective-permute-done.22, bf16[11,16,512]{2,1,0:T(8,128)(2,1)S(1)} %collective-permute-done.21, bf16[4,11,16,512]{3,2,1,0:T(8,128)(2,1)} %collective-permute-done.19, ...), kind=kLoop, calls=%fused_computation.34 | loop fusion | flops 1261567 | bytes 1802244 | tf_op jit(solution)/shard_map/reduce_sum | solution.py:827
  182.7 1.1 collective-permute-done.29
  183.8 1.3 multiply_reduce_fusion.2
  186.6 1.2 collective-permute-done.30
  187.8 1.2 collective-permute-start.31
  189.1 2.7 %collective-permute-done.31 = f32[12,512]{1,0:T(8,128)S(1)} collective-permute-done((f32[12,512]{1,0:T(8,128)S(1)}, f32[12,512]{1,0:T(8,128)S(1)}, u32[]{:S(2)}, u32[]{:S(2)}) %collective-permute-start.31) | collective-permute-done | bytes 24608 | tf_op jit(solution)/shard_map/ppermute | solution.py:54
  191.8 1.5 collective-permute-start.32
  193.3 2.4 %collective-permute-done.32 = f32[12,512]{1,0:T(8,128)S(1)} collective-permute-done((f32[12,512]{1,0:T(8,128)S(1)}, f32[12,512]{1,0:T(8,128)S(1)}, u32[]{:S(2)}, u32[]{:S(2)}) %collective-permute-start.32) | collective-permute-done | bytes 24608 | tf_op jit(solution)/shard_map/ppermute | solution.py:54
  196.3 3.3 %collective-permute-done.33 = f32[12,512]{1,0:T(8,128)S(1)} collective-permute-done((f32[12,512]{1,0:T(8,128)S(1)}, f32[12,512]{1,0:T(8,128)S(1)}, u32[]{:S(2)}, u32[]{:S(2)}) %collective-permute-start.33) | collective-permute-done | bytes 24608 | tf_op jit(solution)/shard_map/ppermute | solution.py:54
  199.6 1.4 collective-permute-start.34
  201.0 3.8 %collective-permute-done.34 = f32[12,512]{1,0:T(8,128)S(1)} collective-permute-done((f32[12,512]{1,0:T(8,128)S(1)}, f32[12,512]{1,0:T(8,128)S(1)}, u32[]{:S(2)}, u32[]{:S(2)}) %collective-permute-start.34) | collective-permute-done | bytes 24608 | tf_op jit(solution)/shard_map/ppermute | solution.py:54
  205.4 3.0 %update.1 = (f32[1,1]{1,0:T(1,128)}, f32[4,16,512]{2,1,0:T(8,128)}, f32[4,16,512]{2,1,0:T(8,128)}, f32[4,16,512]{2,1,0:T(8,128)}, f32[2,16,512]{2,1,0:T(8,128)},...) custom-call(s32[1]{0:T(128)} %bitcast.own_ref, ...), custom_call_target="tpu_custom_call" | custom-call | tf_op jit(solution)/shard_map/update/pallas_call | solution.py:702
  (118 shorter events, 14.4 us)
Async XLA Ops:
  3.4 8.4 %collective-permute-start = (bf16[4,16,512]{2,1,0:T(8,128)(2,1)S(1)}, bf16[4,16,512]{2,1,0:T(8,128)(2,1)S(1)}, u32[]{:S(2)}, u32[]{:S(2)}) collective-permute-start(bf16[4,16,512]{2,1,0:T(8,128)(2,1)S(1)} %get-tuple-element.205), channel_id=1, source_target_pairs={{0,8},{1,9},{2,10},{3,11},{4,12},{5,13},{6,14},{7,15},{8,0},{9,1},... | collective-permute-start | bytes 196616 | tf_op jit(solution)/shard_map/ppermute | solution.py:54
  6.5 7.3 %collective-permute-start.1 = (bf16[4,16,512]{2,1,0:T(8,128)(2,1)S(1)}, bf16[4,16,512]{2,1,0:T(8,128)(2,1)S(1)}, u32[]{:S(2)}, u32[]{:S(2)}) collective-permute-start(bf16[4,16,512]{2,1,0:T(8,128)(2,1)S(1)} %get-tuple-element.205), channel_id=1, source_target_pairs={{0,16},{1,17},{2,18},{3,19},{4,20},{5,21},{6,22},{7,23},{8,24},{9,... | collective-permute-start | bytes 196616 | tf_op jit(solution)/shard_map/ppermute | solution.py:54
  9.1 6.1 %collective-permute-start.2 = (bf16[4,16,512]{2,1,0:T(8,128)(2,1)S(1)}, bf16[4,16,512]{2,1,0:T(8,128)(2,1)S(1)}, u32[]{:S(2)}, u32[]{:S(2)}) collective-permute-start(bf16[4,16,512]{2,1,0:T(8,128)(2,1)S(1)} %get-tuple-element.205), channel_id=1, source_target_pairs={{0,24},{1,25},{2,26},{3,27},{4,28},{5,29},{6,30},{7,31},{8,16},{9,... | collective-permute-start | bytes 196616 | tf_op jit(solution)/shard_map/ppermute | solution.py:54
  15.2 17.8 %copy-start.5 = (bf16[4,4,16,512]{3,2,1,0:T(8,128)(2,1)}, bf16[4,4,16,512]{3,2,1,0:T(8,128)(2,1)S(1)}, u32[]{:S(2)}) copy-start(bf16[4,4,16,512]{3,2,1,0:T(8,128)(2,1)S(1)} %pad_maximum_fusion.5.refs_0_) | copy-start | bytes 786436
  15.2 7.5 %collective-permute-start.3 = (bf16[11,16,512]{2,1,0:T(8,128)(2,1)S(1)}, bf16[11,16,512]{2,1,0:T(8,128)(2,1)S(1)}, u32[]{:S(2)}, u32[]{:S(2)}) collective-permute-start(bf16[11,16,512]{2,1,0:T(8,128)(2,1)S(1)} %constant_dynamic-update-slice_fusion), channel_id=1, source_target_pairs={{0,8},{1,9},{2,10},{3,11},{4,12},{5,13},{6,14},{7,15},{8,0},{9,1},... | collective-permute-start | bytes 540680 | tf_op jit(solution)/shard_map/ppermute | solution.py:54
  15.3 15.7 %collective-permute-start.4 = (bf16[11,16,512]{2,1,0:T(8,128)(2,1)S(1)}, bf16[11,16,512]{2,1,0:T(8,128)(2,1)S(1)}, u32[]{:S(2)}, u32[]{:S(2)}) collective-permute-start(bf16[11,16,512]{2,1,0:T(8,128)(2,1)S(1)} %constant_dynamic-update-slice_fusion), channel_id=1, source_target_pairs={{0,16},{1,17},{2,18},{3,19},{4,20},{5,21},{6,22},{7,23},{8,24},{9,... | collective-permute-start | bytes 540680 | tf_op jit(solution)/shard_map/ppermute | solution.py:54
  17.6 13.4 %collective-permute-start.5 = (bf16[11,16,512]{2,1,0:T(8,128)(2,1)S(1)}, bf16[11,16,512]{2,1,0:T(8,128)(2,1)S(1)}, u32[]{:S(2)}, u32[]{:S(2)}) collective-permute-start(bf16[11,16,512]{2,1,0:T(8,128)(2,1)S(1)} %constant_dynamic-update-slice_fusion), channel_id=1, source_target_pairs={{0,24},{1,25},{2,26},{3,27},{4,28},{5,29},{6,30},{7,31},{8,16},{9,... | collective-permute-start | bytes 540680 | tf_op jit(solution)/shard_map/ppermute | solution.py:54
  19.6 11.5 %collective-permute-start.6 = (bf16[4,4,16,512]{3,2,1,0:T(8,128)(2,1)S(1)}, bf16[4,4,16,512]{3,2,1,0:T(8,128)(2,1)S(1)}, u32[]{:S(2)}, u32[]{:S(2)}) collective-permute-start(bf16[4,4,16,512]{3,2,1,0:T(8,128)(2,1)S(1)} %pad_maximum_fusion.5.refs_0_), channel_id=1, source_target_pairs={{0,2},{1,3},{2,0},{3,1},{4,6},{5,7},{6,4},{7,5},{8,10},{9,11},{10,... | collective-permute-start | bytes 786440 | tf_op jit(solution)/shard_map/ppermute | solution.py:54
  21.1 11.7 %collective-permute-start.7 = (bf16[4,4,16,512]{3,2,1,0:T(8,128)(2,1)S(1)}, bf16[4,4,16,512]{3,2,1,0:T(8,128)(2,1)S(1)}, u32[]{:S(2)}, u32[]{:S(2)}) collective-permute-start(bf16[4,4,16,512]{3,2,1,0:T(8,128)(2,1)S(1)} %pad_maximum_fusion.5.refs_0_), channel_id=1, source_target_pairs={{0,4},{1,5},{2,6},{3,7},{4,0},{5,1},{6,2},{7,3},{8,12},{9,13},{10,... | collective-permute-start | bytes 786440 | tf_op jit(solution)/shard_map/ppermute | solution.py:54
  22.7 10.2 %collective-permute-start.8 = (bf16[4,4,16,512]{3,2,1,0:T(8,128)(2,1)S(1)}, bf16[4,4,16,512]{3,2,1,0:T(8,128)(2,1)S(1)}, u32[]{:S(2)}, u32[]{:S(2)}) collective-permute-start(bf16[4,4,16,512]{3,2,1,0:T(8,128)(2,1)S(1)} %pad_maximum_fusion.5.refs_0_), channel_id=1, source_target_pairs={{0,6},{1,7},{2,4},{3,5},{4,2},{5,3},{6,0},{7,1},{8,14},{9,15},{10,... | collective-permute-start | bytes 786440 | tf_op jit(solution)/shard_map/ppermute | solution.py:54
  31.1 2.0 copy-start
  31.2 2.7 %copy-start.10 = (bf16[4,4,16,512]{3,2,1,0:T(8,128)(2,1)}, bf16[4,4,16,512]{3,2,1,0:T(8,128)(2,1)S(1)}, u32[]{:S(2)}) copy-start(bf16[4,4,16,512]{3,2,1,0:T(8,128)(2,1)S(1)} %collective-permute-done.6.refs_1_) | copy-start | bytes 786436
  32.9 1.0 copy-start.11
  32.9 1.0 copy-start.12
  33.0 3.3 %collective-permute-start.9 = (bf16[16,4,16,512]{3,2,1,0:T(8,128)(2,1)S(1)}, bf16[16,4,16,512]{3,2,1,0:T(8,128)(2,1)}, u32[]{:S(2)}, u32[]{:S(2)}) collective-permute-start(bf16[16,4,16,512]{3,2,1,0:T(8,128)(2,1)S(1)} %pad_maximum_fusion), channel_id=1, source_target_pairs={{0,1},{1,0},{2,3},{3,2},{4,5},{5,4},{6,7},{7,6},{8,9},{9,8},{10,11... | collective-permute-start | bytes 3145736 | tf_op jit(solution)/shard_map/ppermute | solution.py:54
  33.9 13.1 %collective-permute-start.10 = (bf16[4,6,16,512]{3,2,1,0:T(8,128)(2,1)S(1)}, bf16[4,6,16,512]{3,2,1,0:T(8,128)(2,1)S(1)}, u32[]{:S(2)}, u32[]{:S(2)}) collective-permute-start(bf16[4,6,16,512]{3,2,1,0:T(8,128)(2,1)S(1)} %slice.280), channel_id=1, source_target_pairs={{0,2},{1,3},{2,0},{3,1},{4,6},{5,7},{6,4},{7,5},{8,10},{9,11},{10,... | collective-permute-start | bytes 1179656 | tf_op jit(solution)/shard_map/ppermute | solution.py:54
  35.2 11.8 %collective-permute-start.11 = (bf16[4,5,16,512]{3,2,1,0:T(8,128)(2,1)S(1)}, bf16[4,5,16,512]{3,2,1,0:T(8,128)(2,1)S(1)}, u32[]{:S(2)}, u32[]{:S(2)}) collective-permute-start(bf16[4,5,16,512]{3,2,1,0:T(8,128)(2,1)S(1)} %pad_maximum_fusion.4), channel_id=1, source_target_pairs={{0,4},{1,5},{2,6},{3,7},{4,0},{5,1},{6,2},{7,3},{8,12},{9,13},{10,... | collective-permute-start | bytes 983048 | tf_op jit(solution)/shard_map/ppermute | solution.py:54
  41.8 3.4 %copy-start.2 = (bf16[1024,512]{1,0:T(8,128)(2,1)}, bf16[1024,512]{1,0:T(8,128)(2,1)S(1)}, u32[]{:S(2)}) copy-start(bf16[1024,512]{1,0:T(8,128)(2,1)S(1)} %fusion.7.h_ref) | copy-start | bytes 3145732
  47.0 3.8 %copy-start.15 = (s32[1024]{0:T(1024)S(1)}, s32[1024]{0:T(1024)}, u32[]{:S(2)}) copy-start(s32[1024]{0:T(1024)} %param.23) | copy-start | bytes 12292
  47.0 4.8 %copy-start.16 = (s32[1024]{0:T(1024)S(1)}, s32[1024]{0:T(1024)}, u32[]{:S(2)}) copy-start(s32[1024]{0:T(1024)} %param.24) | copy-start | bytes 12292
  47.9 19.7 %collective-permute-start.12 = (bf16[8,6,16,512]{3,2,1,0:T(8,128)(2,1)}, bf16[8,6,16,512]{3,2,1,0:T(8,128)(2,1)}, u32[]{:S(2)}, u32[]{:S(2)}) collective-permute-start(bf16[8,6,16,512]{3,2,1,0:T(8,128)(2,1)} %pad_maximum_fusion.1), channel_id=1, source_target_pairs={{0,4},{1,5},{2,6},{3,7},{4,0},{5,1},{6,2},{7,3},{8,12},{9,13},{10,... | collective-permute-start | bytes 2359304 | tf_op jit(solution)/shard_map/ppermute | solution.py:54
  49.9 17.1 %collective-permute-start.13 = (bf16[8,5,16,512]{3,2,1,0:T(8,128)(2,1)}, bf16[8,5,16,512]{3,2,1,0:T(8,128)(2,1)}, u32[]{:S(2)}, u32[]{:S(2)}) collective-permute-start(bf16[8,5,16,512]{3,2,1,0:T(8,128)(2,1)} %pad_maximum_fusion.3), channel_id=1, source_target_pairs={{0,2},{1,3},{2,0},{3,1},{4,6},{5,7},{6,4},{7,5},{8,10},{9,11},{10,... | collective-permute-start | bytes 1966088 | tf_op jit(solution)/shard_map/ppermute | solution.py:54
  68.8 7.6 %copy-start.4 = (bf16[16,6,16,512]{3,2,1,0:T(8,128)(2,1)}, bf16[16,6,16,512]{3,2,1,0:T(8,128)(2,1)S(1)}, u32[]{:S(2)}) copy-start(bf16[16,6,16,512]{3,2,1,0:T(8,128)(2,1)S(1)} %constant_dynamic-update-slice_fusion.6.refs_0_) | copy-start | bytes 4718596
  68.8 5.4 %collective-permute-start.14 = (bf16[16,6,16,512]{3,2,1,0:T(8,128)(2,1)S(1)}, bf16[16,6,16,512]{3,2,1,0:T(8,128)(2,1)S(1)}, u32[]{:S(2)}, u32[]{:S(2)}) collective-permute-start(bf16[16,6,16,512]{3,2,1,0:T(8,128)(2,1)S(1)} %constant_dynamic-update-slice_fusion.6.refs_0_), channel_id=1, source_target_pairs={{0,1},{1,0},{2,3},{3,2},{4,5},{5,4},{6,7},{7,6},{8,9},{9,8},{10,11... | collective-permute-start | bytes 4718600 | tf_op jit(solution)/shard_map/ppermute | solution.py:54
  70.5 3.7 %copy-start.7 = (bf16[16,5,16,512]{3,2,1,0:T(8,128)(2,1)}, bf16[16,5,16,512]{3,2,1,0:T(8,128)(2,1)S(1)}, u32[]{:S(2)}) copy-start(bf16[16,5,16,512]{3,2,1,0:T(8,128)(2,1)S(1)} %constant_dynamic-update-slice_fusion.9.refs_1_) | copy-start | bytes 3932164
  70.5 3.6 %collective-permute-start.15 = (bf16[16,5,16,512]{3,2,1,0:T(8,128)(2,1)S(1)}, bf16[16,5,16,512]{3,2,1,0:T(8,128)(2,1)S(1)}, u32[]{:S(2)}, u32[]{:S(2)}) collective-permute-start(bf16[16,5,16,512]{3,2,1,0:T(8,128)(2,1)S(1)} %constant_dynamic-update-slice_fusion.9.refs_1_), channel_id=1, source_target_pairs={{0,1},{1,0},{2,3},{3,2},{4,5},{5,4},{6,7},{7,6},{8,9},{9,8},{10,11... | collective-permute-start | bytes 3932168 | tf_op jit(solution)/shard_map/ppermute | solution.py:54
  74.2 1.1 copy-start.9
  75.2 1.1 copy-start.8
  107.1 5.6 %collective-permute-start.16 = (bf16[16,11,16,512]{3,2,1,0:T(8,128)(2,1)}, bf16[16,11,16,512]{3,2,1,0:T(8,128)(2,1)S(1)}, u32[]{:S(2)}, u32[]{:S(2)}) collective-permute-start(bf16[16,11,16,512]{3,2,1,0:T(8,128)(2,1)} %get-tuple-element.121), channel_id=1, source_target_pairs={{0,1},{1,0},{2,3},{3,2},{4,5},{5,4},{6,7},{7,6},{8,9},{9,8},{10,11... | collective-permute-start | bytes 8650760 | tf_op jit(solution)/shard_map/ppermute | solution.py:54
  116.8 33.0 %collective-permute-start.17 = (bf16[4,11,16,512]{3,2,1,0:T(8,128)(2,1)}, bf16[4,11,16,512]{3,2,1,0:T(8,128)(2,1)S(1)}, u32[]{:S(2)}, u32[]{:S(2)}) collective-permute-start(bf16[4,11,16,512]{3,2,1,0:T(8,128)(2,1)} %get-tuple-element.134), channel_id=1, source_target_pairs={{0,2},{1,3},{2,0},{3,1},{4,6},{5,7},{6,4},{7,5},{8,10},{9,11},{10,... | collective-permute-start | bytes 2162696 | tf_op jit(solution)/shard_map/ppermute | solution.py:54
  118.0 33.7 %collective-permute-start.18 = (bf16[4,11,16,512]{3,2,1,0:T(8,128)(2,1)}, bf16[4,11,16,512]{3,2,1,0:T(8,128)(2,1)}, u32[]{:S(2)}, u32[]{:S(2)}) collective-permute-start(bf16[4,11,16,512]{3,2,1,0:T(8,128)(2,1)} %get-tuple-element.135), channel_id=1, source_target_pairs={{0,4},{1,5},{2,6},{3,7},{4,0},{5,1},{6,2},{7,3},{8,12},{9,13},{10,... | collective-permute-start | bytes 2162696 | tf_op jit(solution)/shard_map/ppermute | solution.py:54
  118.9 32.8 %collective-permute-start.19 = (bf16[4,11,16,512]{3,2,1,0:T(8,128)(2,1)}, bf16[4,11,16,512]{3,2,1,0:T(8,128)(2,1)}, u32[]{:S(2)}, u32[]{:S(2)}) collective-permute-start(bf16[4,11,16,512]{3,2,1,0:T(8,128)(2,1)} %get-tuple-element.136), channel_id=1, source_target_pairs={{0,6},{1,7},{2,4},{3,5},{4,2},{5,3},{6,0},{7,1},{8,14},{9,15},{10,... | collective-permute-start | bytes 2162696 | tf_op jit(solution)/shard_map/ppermute | solution.py:54
  120.3 31.9 %copy-start.18 = (f32[1,2048]{1,0:T(1,128)S(1)}, f32[1,2048]{1,0:T(1,128)}, u32[]{:S(2)}) copy-start(f32[1,2048]{1,0:T(1,128)} %get-tuple-element.152) | copy-start | bytes 24580
  149.8 9.6 %copy-start.13 = (bf16[16,3,16,512]{3,2,1,0:T(8,128)(2,1)S(1)}, bf16[16,3,16,512]{3,2,1,0:T(8,128)(2,1)}, u32[]{:S(2)}) copy-start(bf16[16,3,16,512]{3,2,1,0:T(8,128)(2,1)} %get-tuple-element.138) | copy-start | bytes 2359300
  149.8 1.9 copy-start.14
  151.7 7.7 %collective-permute-start.20 = (bf16[16,3,16,512]{3,2,1,0:T(8,128)(2,1)}, bf16[16,3,16,512]{3,2,1,0:T(8,128)(2,1)S(1)}, u32[]{:S(2)}, u32[]{:S(2)}) collective-permute-start(bf16[16,3,16,512]{3,2,1,0:T(8,128)(2,1)} %get-tuple-element.139), channel_id=1, source_target_pairs={{0,1},{1,0},{2,3},{3,2},{4,5},{5,4},{6,7},{7,6},{8,9},{9,8},{10,11... | collective-permute-start | bytes 2359304 | tf_op jit(solution)/shard_map/ppermute | solution.py:54
  152.9 6.8 %copy-start.1 = (bf16[1024,512]{1,0:T(8,128)(2,1)S(1)}, bf16[1024,512]{1,0:T(8,128)(2,1)}, u32[]{:S(2)}) copy-start(bf16[1024,512]{1,0:T(8,128)(2,1)} %x_ref.1) | copy-start | bytes 3145732
  152.9 6.8 %copy-start.3 = (f32[1024,512]{1,0:T(8,128)S(1)}, f32[1024,512]{1,0:T(8,128)}, u32[]{:S(2)}) copy-start(f32[1024,512]{1,0:T(8,128)} %get-tuple-element.140) | copy-start | bytes 6291460
  154.9 10.6 %collective-permute-start.21 = (bf16[11,16,512]{2,1,0:T(8,128)(2,1)S(1)}, bf16[11,16,512]{2,1,0:T(8,128)(2,1)S(1)}, u32[]{:S(2)}, u32[]{:S(2)}) collective-permute-start(bf16[11,16,512]{2,1,0:T(8,128)(2,1)S(1)} %get-tuple-element.193), channel_id=1, source_target_pairs={{0,8},{1,9},{2,10},{3,11},{4,12},{5,13},{6,14},{7,15},{8,0},{9,1},... | collective-permute-start | bytes 540680 | tf_op jit(solution)/shard_map/ppermute | solution.py:54
  156.5 16.1 %collective-permute-start.22 = (bf16[11,16,512]{2,1,0:T(8,128)(2,1)S(1)}, bf16[11,16,512]{2,1,0:T(8,128)(2,1)S(1)}, u32[]{:S(2)}, u32[]{:S(2)}) collective-permute-start(bf16[11,16,512]{2,1,0:T(8,128)(2,1)S(1)} %get-tuple-element.192), channel_id=1, source_target_pairs={{0,16},{1,17},{2,18},{3,19},{4,20},{5,21},{6,22},{7,23},{8,24},{9,... | collective-permute-start | bytes 540680 | tf_op jit(solution)/shard_map/ppermute | solution.py:54
  157.9 14.7 %collective-permute-start.23 = (bf16[11,16,512]{2,1,0:T(8,128)(2,1)S(1)}, bf16[11,16,512]{2,1,0:T(8,128)(2,1)S(1)}, u32[]{:S(2)}, u32[]{:S(2)}) collective-permute-start(bf16[11,16,512]{2,1,0:T(8,128)(2,1)S(1)} %get-tuple-element.191), channel_id=1, source_target_pairs={{0,24},{1,25},{2,26},{3,27},{4,28},{5,29},{6,30},{7,31},{8,16},{9,... | collective-permute-start | bytes 540680 | tf_op jit(solution)/shard_map/ppermute | solution.py:54
  159.7 7.4 %copy-start.6 = (f32[1024,512]{1,0:T(8,128)S(1)}, f32[1024,512]{1,0:T(8,128)}, u32[]{:S(2)}) copy-start(f32[1024,512]{1,0:T(8,128)} %get-tuple-element.120) | copy-start | bytes 6291460
  161.0 11.6 %collective-permute-start.24 = (bf16[4,3,16,512]{3,2,1,0:T(8,128)(2,1)S(1)}, bf16[4,3,16,512]{3,2,1,0:T(8,128)(2,1)S(1)}, u32[]{:S(2)}, u32[]{:S(2)}) collective-permute-start(bf16[4,3,16,512]{3,2,1,0:T(8,128)(2,1)S(1)} %get-tuple-element.145), channel_id=1, source_target_pairs={{0,2},{1,3},{2,0},{3,1},{4,6},{5,7},{6,4},{7,5},{8,10},{9,11},{10,... | collective-permute-start | bytes 589832 | tf_op jit(solution)/shard_map/ppermute | solution.py:54
  162.2 10.4 %collective-permute-start.25 = (bf16[4,3,16,512]{3,2,1,0:T(8,128)(2,1)S(1)}, bf16[4,3,16,512]{3,2,1,0:T(8,128)(2,1)S(1)}, u32[]{:S(2)}, u32[]{:S(2)}) collective-permute-start(bf16[4,3,16,512]{3,2,1,0:T(8,128)(2,1)S(1)} %get-tuple-element.146), channel_id=1, source_target_pairs={{0,4},{1,5},{2,6},{3,7},{4,0},{5,1},{6,2},{7,3},{8,12},{9,13},{10,... | collective-permute-start | bytes 589832 | tf_op jit(solution)/shard_map/ppermute | solution.py:54
  165.5 7.3 %collective-permute-start.26 = (bf16[4,3,16,512]{3,2,1,0:T(8,128)(2,1)S(1)}, bf16[4,3,16,512]{3,2,1,0:T(8,128)(2,1)S(1)}, u32[]{:S(2)}, u32[]{:S(2)}) collective-permute-start(bf16[4,3,16,512]{3,2,1,0:T(8,128)(2,1)S(1)} %get-tuple-element.147), channel_id=1, source_target_pairs={{0,6},{1,7},{2,4},{3,5},{4,2},{5,3},{6,0},{7,1},{8,14},{9,15},{10,... | collective-permute-start | bytes 589832 | tf_op jit(solution)/shard_map/ppermute | solution.py:54
  168.8 17.6 %copy-start.17 = (f32[8,512]{1,0:T(8,128)S(1)}, f32[8,512]{1,0:T(8,128)}, u32[]{:S(2)}) copy-start(f32[8,512]{1,0:T(8,128)} %get-tuple-element.151) | copy-start | bytes 49156
  173.0 8.9 %collective-permute-start.27 = (bf16[3,16,512]{2,1,0:T(8,128)(2,1)S(1)}, bf16[3,16,512]{2,1,0:T(8,128)(2,1)S(1)}, u32[]{:S(2)}, u32[]{:S(2)}) collective-permute-start(bf16[3,16,512]{2,1,0:T(8,128)(2,1)S(1)} %get-tuple-element.201), channel_id=1, source_target_pairs={{0,8},{1,9},{2,10},{3,11},{4,12},{5,13},{6,14},{7,15},{8,0},{9,1},... | collective-permute-start | bytes 147464 | tf_op jit(solution)/shard_map/ppermute | solution.py:54
  176.4 6.3 %collective-permute-start.28 = (bf16[3,16,512]{2,1,0:T(8,128)(2,1)S(1)}, bf16[3,16,512]{2,1,0:T(8,128)(2,1)S(1)}, u32[]{:S(2)}, u32[]{:S(2)}) collective-permute-start(bf16[3,16,512]{2,1,0:T(8,128)(2,1)S(1)} %get-tuple-element.203), channel_id=1, source_target_pairs={{0,16},{1,17},{2,18},{3,19},{4,20},{5,21},{6,22},{7,23},{8,24},{9,... | collective-permute-start | bytes 147464 | tf_op jit(solution)/shard_map/ppermute | solution.py:54
  177.8 6.0 %collective-permute-start.29 = (bf16[3,16,512]{2,1,0:T(8,128)(2,1)S(1)}, bf16[3,16,512]{2,1,0:T(8,128)(2,1)S(1)}, u32[]{:S(2)}, u32[]{:S(2)}) collective-permute-start(bf16[3,16,512]{2,1,0:T(8,128)(2,1)S(1)} %get-tuple-element.202), channel_id=1, source_target_pairs={{0,24},{1,25},{2,26},{3,27},{4,28},{5,29},{6,30},{7,31},{8,16},{9,... | collective-permute-start | bytes 147464 | tf_op jit(solution)/shard_map/ppermute | solution.py:54
  186.6 1.3 collective-permute-start.30
  187.8 3.9 %collective-permute-start.31 = (f32[12,512]{1,0:T(8,128)S(1)}, f32[12,512]{1,0:T(8,128)S(1)}, u32[]{:S(2)}, u32[]{:S(2)}) collective-permute-start(f32[12,512]{1,0:T(8,128)S(1)} %add.262), channel_id=1, source_target_pairs={{0,2},{1,3},{2,0},{3,1},{4,6},{5,7},{6,4},{7,5},{8,10},{9,11},{10,... | collective-permute-start | bytes 73736 | tf_op jit(solution)/shard_map/ppermute | solution.py:54
  191.8 3.9 %collective-permute-start.32 = (f32[12,512]{1,0:T(8,128)S(1)}, f32[12,512]{1,0:T(8,128)S(1)}, u32[]{:S(2)}, u32[]{:S(2)}) collective-permute-start(f32[12,512]{1,0:T(8,128)S(1)} %add.263), channel_id=1, source_target_pairs={{0,4},{1,5},{2,6},{3,7},{4,0},{5,1},{6,2},{7,3},{8,12},{9,13},{10,... | collective-permute-start | bytes 73736 | tf_op jit(solution)/shard_map/ppermute | solution.py:54
  195.7 3.9 %collective-permute-start.33 = (f32[12,512]{1,0:T(8,128)S(1)}, f32[12,512]{1,0:T(8,128)S(1)}, u32[]{:S(2)}, u32[]{:S(2)}) collective-permute-start(f32[12,512]{1,0:T(8,128)S(1)} %add.264), channel_id=1, source_target_pairs={{0,8},{1,9},{2,10},{3,11},{4,12},{5,13},{6,14},{7,15},{8,0},{9,1},... | collective-permute-start | bytes 73736 | tf_op jit(solution)/shard_map/ppermute | solution.py:54
  199.6 5.2 %collective-permute-start.34 = (f32[12,512]{1,0:T(8,128)S(1)}, f32[12,512]{1,0:T(8,128)S(1)}, u32[]{:S(2)}, u32[]{:S(2)}) collective-permute-start(f32[12,512]{1,0:T(8,128)S(1)} %add.265), channel_id=1, source_target_pairs={{0,16},{1,17},{2,18},{3,19},{4,20},{5,21},{6,22},{7,23},{8,24},{9,... | collective-permute-start | bytes 73736 | tf_op jit(solution)/shard_map/ppermute | solution.py:54

commit v2 on v1

--- a/solution.py
+++ b/solution.py
@@ -82,161 +82,53 @@
     return table + [[offset | 1 for row in table for offset in row]]
 
 
-def plane_orders(groups):
-    _, (first_bit, bits), _ = stage_bits(groups)
-    order = list(range(first_bit, first_bit + bits))
-    return order, order[bits // 2 :] + order[: bits // 2]
-
-
-def z_offsets(groups):
-    _, _, (first_bit, bits) = stage_bits(groups)
-    return [z << first_bit for z in range(2**bits)]
-
-
-def send_halves(arrays, orders, position, groups):
-    count = 2 ** sum(groups)
-    return [swap_with(array, 1 << order[position], count) for array, order in zip(arrays, orders)]
-
-
-def join_halves(arrays, received, tables, orders, position):
-    arrays = [jnp.concatenate(pair) for pair in zip(arrays, received)]
-    tables = [
-        table + [offset | (1 << order[position]) for offset in table] for table, order in zip(tables, orders)
-    ]
-    return arrays, tables
-
-
 def vmem_spec():
     return pl.BlockSpec(memory_space=pltpu.VMEM)
 
 
 def smem_spec():
     return pl.BlockSpec(memory_space=pltpu.SMEM)
-
-
-def matrix_shape(kind, pieces, count, step, width):
-    if kind == "stack":
-        return (pieces, count, step, width)
-    if kind == "rows":
-        return (count, pieces, step, width)
-    return (count, step, pieces * width)
-
-
-def place_kernel(tables, layout, own_ref, *refs):
-    parts = refs[: len(tables)]
-    outs = refs[len(tables) :]
-    own = own_ref[0]
-    total = None
-    where_to = [
-        (index, kind, piece) for index, (kind, _, pieces) in enumerate(layout) for piece in range(pieces)
-    ]
-    for part, (row, first) in zip(parts, tables):
-        width = part.shape[3]
-        for entry, offset in enumerate(row):
-            owner = own ^ offset
-            for source in range(part.shape[1]):
-                index, kind, piece = where_to[first + source]
-                block = part[entry, source]
-                if kind == "sum":
-                    block = block.astype(jnp.float32)
-                    total = block if total is None else total + block
-                elif kind == "stack":
-                    outs[index][piece, owner] = block
-                elif kind == "rows":
-                    outs[index][owner, piece] = block
-                else:
-                    outs[index][owner, :, piece * width : (piece + 1) * width] = block
-    for index, (kind, _, _) in enumerate(layout):
-        if kind == "sum":
-            outs[index][...] = total
 
 
 def place(own, parts, tables, layout, groups):
     count = 2 ** sum(groups)
     step, width = parts[0].shape[2:]
-    if step % 16:
-        firsts = sorted({first for _, first in tables})
-        groups_of = []
-        for first in firsts:
-            chosen = [(part, row) for part, (row, base) in zip(parts, tables) if base == first]
-            order = jnp.argsort(jnp.array([o for _, row in chosen for o in row]) ^ own)
-            groups_of.append(jnp.concatenate([part for part, _ in chosen])[order])
-        full = jnp.concatenate(groups_of, 1)
-        result = []
-        for kind, first, pieces in layout:
-            chosen = full[:, first : first + pieces]
-            if kind == "sum":
-                result.append(jnp.sum(chosen.astype(jnp.float32), 0).reshape(pieces * step, width))
-            elif kind == "stack":
-                result.append(jnp.moveaxis(chosen, 0, 1))
-            elif kind == "rows":
-                result.append(chosen)
-            else:
-                result.append(jnp.moveaxis(chosen, 1, 2).reshape(count, step, pieces * width))
-        return result
-    shapes = [
-        jax.ShapeDtypeStruct((step, width), jnp.float32)
-        if kind == "sum"
-        else jax.ShapeDtypeStruct(matrix_shape(kind, pieces, count, step, width), jnp.bfloat16)
-        for kind, _, pieces in layout
-    ]
-    return pl.pallas_call(
-        functools.partial(place_kernel, tables, layout),
-        in_specs=[smem_spec()] + [vmem_spec() for _ in parts],
-        out_specs=[vmem_spec() for _ in layout],
-        out_shape=shapes,
-        name="place",
-    )(own[None].astype(jnp.int32), *parts)
-
-
-def split_kernel(offsets, layout, own_ref, *refs):
-    ins = refs[: len(layout)]
-    kept, sent = refs[len(layout) :]
-    own = own_ref[0]
-    for entry, offset in enumerate(offsets):
-        for side, target in enumerate((kept, sent)):
-            owner = own ^ (offset | side)
-            for index, (kind, first, pieces) in enumerate(layout):
-                width = target.shape[3]
-                for piece in range(pieces):
-                    if kind == "sum":
-                        block = ins[index][...]
-                    elif kind == "stack":
-                        block = ins[index][piece, owner]
-                    elif kind == "rows":
-                        block = ins[index][owner, piece]
-                    else:
-                        block = ins[index][owner, :, piece * width : (piece + 1) * width]
-                    target[entry, first + piece] = block
+    firsts = sorted({first for _, first in tables})
+    groups_of = []
+    for first in firsts:
+        chosen = [(part, row) for part, (row, base) in zip(parts, tables) if base == first]
+        order = jnp.argsort(jnp.array([o for _, row in chosen for o in row]) ^ own)
+        groups_of.append(jnp.concatenate([part for part, _ in chosen])[order])
+    full = jnp.concatenate(groups_of, 1)
+    result = []
+    for kind, first, pieces in layout:
+        chosen = full[:, first : first + pieces]
+        if kind == "sum":
+            result.append(jnp.sum(chosen.astype(jnp.float32), 0).reshape(pieces * step, width))
+        elif kind == "stack":
+            result.append(jnp.moveaxis(chosen, 0, 1))
+        elif kind == "rows":
+            result.append(chosen)
+        else:
+            result.append(jnp.moveaxis(chosen, 1, 2).reshape(count, step, pieces * width))
+    return result
 
 
 def split(own, grads, layout, groups):
     count = 2 ** sum(groups)
     width = 512
-    total = sum(pieces for _, _, pieces in layout)
     step = grads[0].shape[-2]
     offsets = [offset for row in offsets_of(groups)[:-1] for offset in row]
-    if step % 16:
-        pieces_of = []
-        for grad, (kind, _, pieces) in zip(grads, layout):
-            if kind == "sum":
-                grad = jnp.broadcast_to(grad.reshape(1, pieces, step, width), (count, pieces, step, width))
-            elif kind == "stack":
-                grad = jnp.moveaxis(grad, 1, 0)
-            elif kind == "columns":
-                grad = jnp.moveaxis(grad.reshape(count, step, pieces, width), 2, 1)
-            pieces_of.append(grad)
-        full = jnp.concatenate(pieces_of, 1)
-        order = jnp.array(offsets) ^ own
-        return full[order], full[order ^ 1]
-    shape = jax.ShapeDtypeStruct((len(offsets), total, step, width), jnp.bfloat16)
-    return pl.pallas_call(
-        functools.partial(split_kernel, offsets, layout),
-        in_specs=[smem_spec()] + [vmem_spec() for _ in grads],
-        out_specs=[vmem_spec(), vmem_spec()],
-        out_shape=[shape, shape],
-        name="split",
-    )(own[None].astype(jnp.int32), *grads)
+    pieces_of = []
+    for grad, (kind, _, pieces) in zip(grads, layout):
+        if kind == "stack":
+            grad = jnp.moveaxis(grad, 1, 0)
+        elif kind == "columns":
+            grad = jnp.moveaxis(grad.reshape(count, step, pieces, width), 2, 1)
+        pieces_of.append(grad)
+    full = jnp.concatenate(pieces_of, 1)
+    order = jnp.array(offsets) ^ own
+    return full[order], full[order ^ 1]
 
 
 def plane_sums(kept, received, groups):
@@ -310,29 +202,53 @@
     lane=lax.broadcasted_iota(jnp.int32,shape,1)
     return (lane//HEAD)==which
 
-def attn_fwd_kernel(segc,posc,segr,posr,q_ref,k_ref,v_ref,o_ref,lse_ref,bias_ref):
-    @pl.when(pl.program_id(0)==0)
+def attn_fwd_kernel(direct, tables, layout, own_ref, segc, posc, segr, posr, x_ref, *refs):
+    part_count = len(tables) if direct else 2
+    parts = refs[:part_count]
+    h_ref, q_ref, k_ref, v_ref, o_ref, lse_ref, *rest = refs[part_count:]
+    bias_ref, q_all, k_all, v_all = rest[-4:]
+    rows = x_ref.shape[0]
+    step = min(BLOCK, rows)
+    lanes = q_ref.shape[1]
+    pair = lanes // HEAD
+    const = HEAD**-0.5 * LOG2E
+    low = lambda value: value.astype(jnp.bfloat16)
+    weights, vectors = rest[:2] if direct else parts
+    tile = pl.program_id(0)
+
+    @pl.when(tile == 0)
     def _():
-        fill_bias(bias_ref,segc,posc,segr,posr)
-    rows=q_ref.shape[0]; step=min(BLOCK,rows)
-    pair=q_ref.shape[1]//HEAD
-    const=HEAD**-0.5*LOG2E
-    for first in range(0,rows,step):
-        keys=first+step
-        q=q_ref[first:keys,:]
-        mixed=None
+        if direct:
+            copy_parts(tables, layout, own_ref[0], parts, [weights, vectors])
+        fill_bias(bias_ref, segc, posc, segr, posr)
+        for first in range(0, rows, step):
+            x = x_ref[first : first + step, :].astype(jnp.float32)
+            h_ref[first : first + step, :] = low(normalize_parts(x, vectors[0:1, :], vectors[1:2, :])[0])
+        for j, target in enumerate((q_all, k_all, v_all)):
+            whole = low(mat(h_ref[...], weights[j].reshape(-1, weights.shape[-1]), ((1,), (0,))))
+            for which in range(target.shape[0]):
+                target[which] = whole[:, which * lanes : (which + 1) * lanes]
+
+    q_ref[...] = q_all[tile]
+    k_ref[...] = k_all[tile]
+    v_ref[...] = v_all[tile]
+    for first in range(0, rows, step):
+        keys = first + step
+        q = q_ref[first:keys, :]
+        mixed = None
         for which in range(pair):
-            own=head_lanes(q.shape,which)
-            qh=jnp.where(own,q,jnp.zeros_like(q))
-            s=mat(k_ref[:keys,:],qh,((1,),(1,)))*const+bias_ref[:keys,first:keys]
-            m=jnp.max(s,0,keepdims=True)
-            w=jnp.exp2(s-m)
-            total=jnp.sum(w,0,keepdims=True)
-            p=(w*(1.0/total)).astype(jnp.bfloat16)
-            o=mat(p,v_ref[:keys,:],((0,),(0,)))
-            mixed=o if mixed is None else jnp.where(own,o,mixed)
-            lse_ref[0,which:which+1,first:keys]=m+jnp.log2(total)
-        o_ref[first:keys,:]=mixed.astype(jnp.bfloat16)
+            own = head_lanes(q.shape, which)
+            qh = jnp.where(own, q, jnp.zeros_like(q))
+            s = mat(k_ref[:keys, :], qh, ((1,), (1,))) * const + bias_ref[:keys, first:keys]
+            m = jnp.max(s, 0, keepdims=True)
+            w = jnp.exp2(s - m)
+            total = jnp.sum(w, 0, keepdims=True)
+            p = (w * (1.0 / total)).astype(jnp.bfloat16)
+            o = mat(p, v_ref[:keys, :], ((0,), (0,)))
+            mixed = o if mixed is None else jnp.where(own, o, mixed)
+            lse_ref[0, which : which + 1, first:keys] = m + jnp.log2(total)
+        o_ref[first:keys, :] = mixed.astype(jnp.bfloat16)
+
 
 def attn_bwd_kernel(
     offsets, own_ref, segc, posc, segr, posr, q_ref, k_ref, v_ref, do_ref, lse_ref, h_ref, w_ref, start_ref, *refs
@@ -401,18 +317,43 @@
 def seg_args(segments,positions):
     return (segments[:,None],positions[:,None],segments[None],positions[None])
 
-def attend(q,k,v,segments,positions):
-    rows,width=q.shape
-    pairs=width//128
-    blk=pl.BlockSpec((rows,128),lambda j:(0,j))
-    col=pl.BlockSpec((rows,1),const_map); row=pl.BlockSpec((1,rows),const_map)
-    return pl.pallas_call(attn_fwd_kernel,grid=(pairs,),
-        in_specs=[col,col,row,row,blk,blk,blk],
-        out_specs=[blk,pl.BlockSpec((1,2,rows),lambda j:(j,0,0))],
-        out_shape=[jax.ShapeDtypeStruct((rows,width),jnp.bfloat16),jax.ShapeDtypeStruct((pairs,2,rows),jnp.float32)],
-        scratch_shapes=[pltpu.VMEM((rows,rows),jnp.float32)],
+def attend(own, tokens, segments, positions, parts, tables, layout, groups):
+    rows, width = tokens.shape
+    count = 2 ** sum(groups)
+    step = parts[0].shape[2]
+    lanes = 2 * HEAD
+    pairs = width // lanes
+    low = jnp.bfloat16
+    direct = step % 16 == 0
+    blk = pl.BlockSpec((rows, lanes), lambda j: (0, j))
+    whole = lambda shape: pl.BlockSpec(shape, lambda j: (0,) * len(shape), pipeline_mode=pl.Buffered(1))
+    half = jax.ShapeDtypeStruct((rows, width), low)
+    out_shape = [half] * 5 + [jax.ShapeDtypeStruct((pairs, 2, rows), jnp.float32)]
+    out_specs = [whole((rows, width)), blk, blk, blk, blk, pl.BlockSpec((1, 2, rows), lambda j: (j, 0, 0))]
+    if direct:
+        extra = [
+            jax.ShapeDtypeStruct((3, count, step, width), low),
+            jax.ShapeDtypeStruct((step, width), jnp.float32),
+        ]
+        out_shape += extra
+        out_specs += [whole(item.shape) for item in extra]
+    else:
+        parts = place(own, parts, tables, layout, groups)
+    result = pl.pallas_call(
+        functools.partial(attn_fwd_kernel, direct, tables, layout),
+        grid=(pairs,),
+        in_specs=[smem_spec(), whole((rows, 1)), whole((rows, 1)), whole((1, rows)), whole((1, rows))]
+        + [whole((rows, width))]
+        + [whole(part.shape) for part in parts],
+        out_specs=out_specs,
+        out_shape=out_shape,
+        scratch_shapes=[pltpu.VMEM((rows, rows), jnp.float32)] + [pltpu.VMEM((pairs, rows, lanes), low)] * 3,
         name="attn_fwd",
-    )(*seg_args(segments,positions),q,k,v)
+    )(own[None].astype(jnp.int32), *seg_args(segments, positions), tokens, *parts)
+    if not direct:
+        result = list(result) + list(parts)
+    return result
+
 
 def attend_back(own, q, k, v, do, lse, segments, positions, normed, w_qkv, start, groups):
     rows, width = q.shape
@@ -464,18 +405,26 @@
     where_to = [
         (index, kind, piece) for index, (kind, _, pieces) in enumerate(layout) for piece in range(pieces)
     ]
+    total = None
     for part, (row, first) in zip(parts, tables):
         width = part.shape[3]
         for entry, offset in enumerate(row):
             owner = own ^ offset
             for source in range(part.shape[1]):
                 index, kind, piece = where_to[first + source]
-                if kind == "stack":
-                    outs[index][owner] = part[entry, source]
+                block = part[entry, source]
+                if kind == "sum":
+                    block = block.astype(jnp.float32)
+                    total = block if total is None else total + block
+                elif kind == "stack":
+                    outs[index][piece, owner] = block
                 elif kind == "rows":
-                    outs[index][owner, piece] = part[entry, source]
+                    outs[index][owner, piece] = block
                 else:
-                    outs[index][owner, :, piece * width : (piece + 1) * width] = part[entry, source]
+                    outs[index][owner, :, piece * width : (piece + 1) * width] = block
+    for index, (kind, _, _) in enumerate(layout):
+        if kind == "sum":
+            outs[index][...] = total
 
 
 def copy_blocks(offsets, layout, own, ins, kept, sent):
@@ -486,7 +435,7 @@
             for index, (kind, first, pieces) in enumerate(layout):
                 for piece in range(pieces):
                     if kind == "stack":
-                        block = ins[index][owner]
+                        block = ins[index][piece, owner]
                     elif kind == "rows":
                         block = ins[index][owner, piece]
                     else:
@@ -614,7 +563,7 @@
     if direct:
         shape = (len(offsets), 3 + 2 * chunks, step, width)
         grads = [jax.ShapeDtypeStruct(shape, low)] * 2
-        scratch += [pltpu.VMEM((count, step, width), low)] * 3
+        scratch += [pltpu.VMEM((1, count, step, width), low)] * 3
         scratch += [pltpu.VMEM((count, step, hidden), low), pltpu.VMEM((count, chunks, step, width), low)]
     else:
         placed = place(own, parts, tables, FFN_LAYOUT, groups)
@@ -752,40 +701,35 @@
             low(out_weight).reshape(4, step, width),
         ]
     )
-    cut = 6
-    orders = plane_orders(groups)
-    plane_steps = range(len(orders[0]))
     z_first = gather_z(first_shard, groups)
     z_first, second_shard = tie(z_first, second_shard)
     plane_first = gather_plane(z_first, groups)
     z_second = gather_z(second_shard, groups)
-    halves = [z_second[:, :cut], z_second[:, cut:]]
-    tied = tie(*halves, z_first, *plane_first)
-    halves, z_first, plane_first = tied[:2], tied[2], list(tied[3:])
+    z_first, z_second, *plane_first = tie(z_first, z_second, *plane_first)
     core_first = gather_core(z_first, plane_first, groups)
-    received = send_halves(halves, orders, 0, groups)
-    w_qkv, vectors = place(
+    plane_second = gather_plane(z_second, groups)
+    relative = offsets_of(groups)
+    normed, queries, keys, values, mixed_heads, log_total, w_qkv, vectors = attend(
         own,
+        tokens,
+        segments,
+        positions,
         [z_first] + plane_first + [core_first],
-        [(row, 0) for row in offsets_of(groups)],
+        [(row, 0) for row in relative],
         [("stack", 0, 3), ("sum", 3, extra)],
         groups,
     )
     w_qkv = w_qkv.reshape(3, count * step, width)
     bias = vectors[7:11].reshape(-1)
     inputs = tokens.astype(jnp.float32)
-    normed_full, unit_one, scale_one = normalize_parts(inputs, vectors[0], vectors[1])
-    normed = low(normed_full)
-    queries, keys, values = [low(dot("td,de->te", normed, w_qkv[j])) for j in range(3)]
-    queries, keys, values, *received = tie(queries, keys, values, *received)
-    tables = [z_offsets(groups)] * 2
-    for position in plane_steps[1:]:
-        halves, tables = join_halves(halves, received, tables, orders, position - 1)
-        received = send_halves(halves, orders, position, groups)
-    mixed_heads, log_total = attend(queries, keys, values, segments, positions)
-    mixed_heads, *received = tie(mixed_heads, *received)
-    second_step, tables = join_halves(halves, received, tables, orders, plane_steps[-1])
-    others = [swap_with(half, 1, count) for half in second_step]
+    mean_one = jnp.mean(inputs, -1, keepdims=True)
+    scale_one = lax.rsqrt(jnp.mean((inputs - mean_one) * (inputs - mean_one), -1, keepdims=True) + norm_eps)
+    core_second = [swap_with(z_second, 1, count)]
+    mixed_heads, mean_one, scale_one, core_second[0], *plane_second = tie(
+        mixed_heads, mean_one, scale_one, core_second[0], *plane_second
+    )
+    unit_one = (inputs - mean_one) * scale_one
+    core_second += [swap_with(part, 1, count) for part in plane_second]
     layer_out, grad_mixed, grad_normed, grad_inputs, sums, grad_bias, kept_b, sent_b = ffn(
         own,
         tokens,
@@ -794,9 +738,8 @@
         mixed_heads,
         vectors,
         bias,
-        list(second_step) + others,
-        [(tables[0], 0), (tables[1], cut)]
-        + [([offset | 1 for offset in table], first) for table, first in zip(tables, (0, cut))],
+        [z_second] + plane_second + core_second,
+        [(row, 0) for row in relative[:-1]] + [([offset | 1 for offset in row], 0) for row in relative[:-1]],
         groups,
     )
     core_b = swap_with(sent_b, 1, count)

time: 209 us -> 211 us (level)
  waiting for transfers between devices: 42.9 us -> 55.2 us
  matrix products: 5.11 us -> 0 us
  local copies, waits for them, and re-layouts: 13.2 us -> 9.75 us
    ppermute x35 -> x36, waiting for transfers between devices: 42.9 us -> 55.2 us  [swap_with(): lax.ppermute(array, AXES, [(source, source ^ offset) for source in range(...]
    dot_general x3 -> x0, matrix products: 5.11 us -> none  [body(): dot('td,de->te', normed, w_qkv[j])]
    concatenate x2 -> x0, local copies, waits for them, and re-layouts: 2.74 us -> none  [join_halves(): arrays = [jnp.concatenate(pair) for pair in zip(arrays, received)]]
    unnamed x49 -> x45, local copies, waits for them, and re-layouts: 3.8 us -> 4.7 us
    ppermute x35 -> x36, starting transfers between devices: 42.8 us -> 42 us  [swap_with(): lax.ppermute(array, AXES, [(source, source ^ offset) for source in range(...]
    pallas_call x2 -> x1, Pallas kernels: 17 us -> 17.2 us  [attend(): pl.pallas_call(functools.partial(attn_fwd_kernel, direct, tables, layout)...]
  transfers between devices with their start and end apart: 35 -> 36, of which waited for: 18 -> 22; matrix products, arithmetic and copies ran while one was open for 13% -> 8% of each run, Pallas kernels for 22% -> 22%
where the time goes in v2:
time: 211 us; the launch traced here: 210 us
  Pallas kernels  80.4 us (38%)
  waiting for transfers between devices  55.2 us (26%)
  starting transfers between devices  42 us (20%)
  other arithmetic  20.3 us (10%)
  local copies, waits for them, and re-layouts  9.75 us (5%)
  between operations  2.57 us (1%)
    ppermute x36, waiting for transfers between devices, swap_with(): lax.ppermute(array, AXES, [(source, source ^ offset) for source in range(...  55.2 us
    ppermute x36, starting transfers between devices, swap_with(): lax.ppermute(array, AXES, [(source, source ^ offset) for source in range(...  42 us
    pallas_call x1, Pallas kernels, ffn(): pl.pallas_call(functools.partial(ffn_kernel, direct, len(parts), tables,...  30.7 us
    pallas_call x1, Pallas kernels, attend_back(): pl.pallas_call(functools.partial(attn_bwd_kernel, offsets), grid=(width /...  29.5 us
    pallas_call x1, Pallas kernels, attend(): pl.pallas_call(functools.partial(attn_fwd_kernel, direct, tables, layout)...  17.2 us
    unnamed x45, local copies, waits for them, and re-layouts  4.7 us
    convert_element_type x2, other arithmetic, plane_sums(): total(offset).astype(jnp.bfloat16)  4.43 us
  transfers between devices with their start and end apart: 36, of which 22 were waited for; matrix products, arithmetic and copies ran while one was open for 8% of the time, Pallas kernels for 22%

profile of v2, /device:TPU:0, one launch (start us, length us, event | category | flops | bytes accessed | tf_op | source)
XLA Modules:
  0.0 210.2 jit_solution(17298182725195378514)
XLA Ops:
  2.3 0.9 convert.28
  3.4 3.1 %collective-permute-start = (bf16[4,16,512]{2,1,0:T(8,128)(2,1)S(1)}, bf16[4,16,512]{2,1,0:T(8,128)(2,1)S(1)}, u32[]{:S(2)}, u32[]{:S(2)}) collective-permute-start(bf16[4,16,512]{2,1,0:T(8,128)(2,1)S(1)} %get-tuple-element.206), channel_id=1, source_target_pairs={{0,8},{1,9},{2,10},{3,11},{4,12},{5,13},{6,14},{7,15},{8,0},{9,1},... | collective-permute-start | bytes 196616 | tf_op jit(solution)/shard_map/ppermute | solution.py:54
  6.5 2.6 %collective-permute-start.1 = (bf16[4,16,512]{2,1,0:T(8,128)(2,1)S(1)}, bf16[4,16,512]{2,1,0:T(8,128)(2,1)S(1)}, u32[]{:S(2)}, u32[]{:S(2)}) collective-permute-start(bf16[4,16,512]{2,1,0:T(8,128)(2,1)S(1)} %get-tuple-element.206), channel_id=1, source_target_pairs={{0,16},{1,17},{2,18},{3,19},{4,20},{5,21},{6,22},{7,23},{8,24},{9,... | collective-permute-start | bytes 196616 | tf_op jit(solution)/shard_map/ppermute | solution.py:54
  9.1 0.9 convert_element_type.207
  10.0 0.8 convert_dynamic-update-slice_fusion
  10.9 0.9 convert_element_type.208
  11.8 1.9 collective-permute-done.1
  13.7 1.4 collective-permute-done.2
  15.3 2.3 %collective-permute-start.4 = (bf16[11,16,512]{2,1,0:T(8,128)(2,1)S(1)}, bf16[11,16,512]{2,1,0:T(8,128)(2,1)S(1)}, u32[]{:S(2)}, u32[]{:S(2)}) collective-permute-start(bf16[11,16,512]{2,1,0:T(8,128)(2,1)S(1)} %constant_dynamic-update-slice_fusion), channel_id=1, source_target_pairs={{0,16},{1,17},{2,18},{3,19},{4,20},{5,21},{6,22},{7,23},{8,24},{9,... | collective-permute-start | bytes 540680 | tf_op jit(solution)/shard_map/ppermute | solution.py:54
  17.6 2.0 collective-permute-start.5
  19.7 1.5 collective-permute-start.6
  21.1 1.5 collective-permute-start.7
  22.7 2.3 %collective-permute-start.8 = (bf16[4,4,16,512]{3,2,1,0:T(8,128)(2,1)S(1)}, bf16[4,4,16,512]{3,2,1,0:T(8,128)(2,1)S(1)}, u32[]{:S(2)}, u32[]{:S(2)}) collective-permute-start(bf16[4,4,16,512]{3,2,1,0:T(8,128)(2,1)S(1)} %pad_maximum_fusion.2.refs_0_), channel_id=1, source_target_pairs={{0,6},{1,7},{2,4},{3,5},{4,2},{5,3},{6,0},{7,1},{8,14},{9,15},{10,... | collective-permute-start | bytes 786440 | tf_op jit(solution)/shard_map/ppermute | solution.py:54
  24.9 6.0 %collective-permute-done.4 = bf16[11,16,512]{2,1,0:T(8,128)(2,1)S(1)} collective-permute-done((bf16[11,16,512]{2,1,0:T(8,128)(2,1)S(1)}, bf16[11,16,512]{2,1,0:T(8,128)(2,1)S(1)}, u32[]{:S(2)}, u32[]{:S(2)}) %collective-permute-start.4) | collective-permute-done | bytes 180256 | tf_op jit(solution)/shard_map/ppermute | solution.py:54
  31.1 1.8 collective-permute-done.7.refs_2_
  34.3 1.1 pad_maximum_fusion
  35.4 1.1 copy.43.segc
  36.5 1.0 copy.44.posc
  38.5 1.8 collective-permute-start.12
  40.3 1.2 collective-permute-start.13
  42.3 1.0 copy-done.6
  43.3 17.2 %attn_fwd.1 = (bf16[1024,512]{1,0:T(8,128)(2,1)}, bf16[1024,512]{1,0:T(8,128)(2,1)}, bf16[1024,512]{1,0:T(8,128)(2,1)}, bf16[1024,512]{1,0:T(8,128)(2,1)}, bf16[...) custom-call(s32[1]{0:T(128)} %bitcast.own_ref, ...), custom_call_target="tpu_custom_call" | custom-call | tf_op jit(solution)/shard_map/attn_fwd/pallas_call | solution.py:342
  60.5 10.6 %collective-permute-done.12.refs_2_ = bf16[4,11,16,512]{3,2,1,0:T(8,128)(2,1)} collective-permute-done((bf16[4,11,16,512]{3,2,1,0:T(8,128)(2,1)S(1)}, bf16[4,11,16,512]{3,2,1,0:T(8,128)(2,1)}, u32[]{:S(2)}, u32[]{:S(2)}) %collective-permute-start.12) | collective-permute-done | bytes 720928 | tf_op jit(solution)/shard_map/ppermute | solution.py:54
  71.1 1.5 collective-permute-done.13.refs_3_
  73.1 0.8 slice_bitcast_fusion.4
  75.0 1.0 collective-permute-done.15.refs_6_
  76.0 1.0 collective-permute-done.16.refs_7_
  77.0 0.9 copy-done.14
  77.9 30.7 %ffn.1 = (bf16[1024,512]{1,0:T(8,128)(2,1)}, bf16[1024,512]{1,0:T(8,128)(2,1)}, f32[1024,512]{1,0:T(8,128)}, f32[1024,512]{1,0:T(8,128)}, f32[8,512]{1,0:T(8,128...) custom-call(s32[1]{0:T(128)} %bitcast.own_ref, ...), custom_call_target="tpu_custom_call" | custom-call | tf_op jit(solution)/shard_map/ffn/pallas_call | solution.py:575
  108.8 5.4 %collective-permute-done.17 = bf16[16,11,16,512]{3,2,1,0:T(8,128)(2,1)S(1)} collective-permute-done((bf16[16,11,16,512]{3,2,1,0:T(8,128)(2,1)}, bf16[16,11,16,512]{3,2,1,0:T(8,128)(2,1)S(1)}, u32[]{:S(2)}, u32[]{:S(2)}) %collective-permute-start.17) | collective-permute-done | bytes 2883616 | tf_op jit(solution)/shard_map/ppermute | solution.py:54
  114.2 4.1 %add_convert_fusion = (bf16[4,11,16,512]{3,2,1,0:T(8,128)(2,1)}, bf16[4,11,16,512]{3,2,1,0:T(8,128)(2,1)}, bf16[4,11,16,512]{3,2,1,0:T(8,128)(2,1)}, f32[4,11,16,512]{3,2,1,0:T(8,128)S(1)}) fusion(bf16[16,11,16,512]{3,2,1,0:T(8,128)(2,1)S(1)} %collective-permute-done.17, bf16[16,11,16,512]{3,2,1,0:T(8,128)(2,1)} %get-tuple-element.127), kind=kLoop, calls=%fused_computation.16 | loop fusion | flops 5406720 | bytes 9371648 | tf_op jit(solution)/shard_map/convert_element_type | solution.py:140
  118.3 0.8 collective-permute-start.18
  119.1 1.5 collective-permute-start.19
  120.6 1.2 collective-permute-start.20
  121.8 29.5 %attn_bwd.1 = (bf16[16,3,16,512]{3,2,1,0:T(8,128)(2,1)}, bf16[16,3,16,512]{3,2,1,0:T(8,128)(2,1)}, f32[1024,512]{1,0:T(8,128)}) custom-call(s32[1]{0:T(128)} %bitcast.own_ref, s32[1024,1]{1,0:T(8,128)} %copy.43.segc, s32[1024,1]{1,0:T(8,128)} %copy.44.posc, s32[1,1024]{1,0:T(1,128)} %bitcast.81, s32[1,1024]{1,0:T(1,128)} %bitcast.84, ...), custom_call_target="tpu_custom_call" | custom-call | tf_op jit(solution)/shard_map/attn_bwd/pallas_call | solution.py:378
  151.9 0.9 collective-permute-done.20
  152.8 0.7 slice.212
  154.7 2.0 fusion.14
  156.7 1.5 collective-permute-start.22
  158.2 1.4 collective-permute-start.23
  159.6 1.6 collective-permute-start.24
  161.5 1.2 fusion.11
  162.8 1.3 collective-permute-start.25
  164.0 1.1 collective-permute-start.26
  165.1 2.2 %collective-permute-done.22 = bf16[11,16,512]{2,1,0:T(8,128)(2,1)S(1)} collective-permute-done((bf16[11,16,512]{2,1,0:T(8,128)(2,1)S(1)}, bf16[11,16,512]{2,1,0:T(8,128)(2,1)S(1)}, u32[]{:S(2)}, u32[]{:S(2)}) %collective-permute-start.22) | collective-permute-done | bytes 180256 | tf_op jit(solution)/shard_map/ppermute | solution.py:54
  167.3 1.7 collective-permute-start.27
  169.1 1.7 fusion.10
  170.8 3.5 %collective-permute-done.23 = bf16[11,16,512]{2,1,0:T(8,128)(2,1)S(1)} collective-permute-done((bf16[11,16,512]{2,1,0:T(8,128)(2,1)S(1)}, bf16[11,16,512]{2,1,0:T(8,128)(2,1)S(1)}, u32[]{:S(2)}, u32[]{:S(2)}) %collective-permute-start.23) | collective-permute-done | bytes 180256 | tf_op jit(solution)/shard_map/ppermute | solution.py:54
  174.8 3.4 %collective-permute-start.28 = (bf16[3,16,512]{2,1,0:T(8,128)(2,1)S(1)}, bf16[3,16,512]{2,1,0:T(8,128)(2,1)S(1)}, u32[]{:S(2)}, u32[]{:S(2)}) collective-permute-start(bf16[3,16,512]{2,1,0:T(8,128)(2,1)S(1)} %get-tuple-element.202), channel_id=1, source_target_pairs={{0,8},{1,9},{2,10},{3,11},{4,12},{5,13},{6,14},{7,15},{8,0},{9,1},... | collective-permute-start | bytes 147464 | tf_op jit(solution)/shard_map/ppermute | solution.py:54
  178.1 1.4 collective-permute-start.29
  179.5 1.4 collective-permute-start.30
  180.9 2.6 %multiply_reduce_fusion.1 = (f32[]{:T(128)}, f32[11,16,512]{2,1,0:T(8,128)}) fusion(bf16[11,16,512]{2,1,0:T(8,128)(2,1)S(1)} %collective-permute-done.24, bf16[11,16,512]{2,1,0:T(8,128)(2,1)S(1)} %collective-permute-done.23, bf16[11,16,512]{2,1,0:T(8,128)(2,1)S(1)} %collective-permute-done.22, bf16[4,11,16,512]{3,2,1,0:T(8,128)(2,1)} %collective-permute-done.20, ...), kind=kLoop, calls=%fused_computation.27 | loop fusion | flops 1261567 | bytes 1802244 | tf_op jit(solution)/shard_map/reduce_sum | solution.py:770
  183.5 0.9 collective-permute-done.29
  184.4 1.1 collective-permute-done.30
  185.5 1.3 multiply_reduce_fusion.2
  188.3 1.2 collective-permute-done.31
  189.5 0.8 collective-permute-start.32
  190.3 3.1 %collective-permute-done.32 = f32[12,512]{1,0:T(8,128)S(1)} collective-permute-done((f32[12,512]{1,0:T(8,128)S(1)}, f32[12,512]{1,0:T(8,128)S(1)}, u32[]{:S(2)}, u32[]{:S(2)}) %collective-permute-start.32) | collective-permute-done | bytes 24608 | tf_op jit(solution)/shard_map/ppermute | solution.py:54
  193.5 0.8 collective-permute-start.33
  194.3 3.1 %collective-permute-done.33 = f32[12,512]{1,0:T(8,128)S(1)} collective-permute-done((f32[12,512]{1,0:T(8,128)S(1)}, f32[12,512]{1,0:T(8,128)S(1)}, u32[]{:S(2)}, u32[]{:S(2)}) %collective-permute-start.33) | collective-permute-done | bytes 24608 | tf_op jit(solution)/shard_map/ppermute | solution.py:54
  198.0 3.3 %collective-permute-done.34 = f32[12,512]{1,0:T(8,128)S(1)} collective-permute-done((f32[12,512]{1,0:T(8,128)S(1)}, f32[12,512]{1,0:T(8,128)S(1)}, u32[]{:S(2)}, u32[]{:S(2)}) %collective-permute-start.34) | collective-permute-done | bytes 24608 | tf_op jit(solution)/shard_map/ppermute | solution.py:54
  201.3 1.4 collective-permute-start.35
  202.7 3.8 %collective-permute-done.35 = f32[12,512]{1,0:T(8,128)S(1)} collective-permute-done((f32[12,512]{1,0:T(8,128)S(1)}, f32[12,512]{1,0:T(8,128)S(1)}, u32[]{:S(2)}, u32[]{:S(2)}) %collective-permute-start.35) | collective-permute-done | bytes 24608 | tf_op jit(solution)/shard_map/ppermute | solution.py:54
  207.1 3.0 %update.1 = (f32[1,1]{1,0:T(1,128)}, f32[4,16,512]{2,1,0:T(8,128)}, f32[4,16,512]{2,1,0:T(8,128)}, f32[4,16,512]{2,1,0:T(8,128)}, f32[2,16,512]{2,1,0:T(8,128)},...) custom-call(s32[1]{0:T(128)} %bitcast.own_ref, ...), custom_call_target="tpu_custom_call" | custom-call | tf_op jit(solution)/shard_map/update/pallas_call | solution.py:651
  (104 shorter events, 11.0 us)
Async XLA Ops:
  3.4 8.5 %collective-permute-start = (bf16[4,16,512]{2,1,0:T(8,128)(2,1)S(1)}, bf16[4,16,512]{2,1,0:T(8,128)(2,1)S(1)}, u32[]{:S(2)}, u32[]{:S(2)}) collective-permute-start(bf16[4,16,512]{2,1,0:T(8,128)(2,1)S(1)} %get-tuple-element.206), channel_id=1, source_target_pairs={{0,8},{1,9},{2,10},{3,11},{4,12},{5,13},{6,14},{7,15},{8,0},{9,1},... | collective-permute-start | bytes 196616 | tf_op jit(solution)/shard_map/ppermute | solution.py:54
  6.5 7.3 %collective-permute-start.1 = (bf16[4,16,512]{2,1,0:T(8,128)(2,1)S(1)}, bf16[4,16,512]{2,1,0:T(8,128)(2,1)S(1)}, u32[]{:S(2)}, u32[]{:S(2)}) collective-permute-start(bf16[4,16,512]{2,1,0:T(8,128)(2,1)S(1)} %get-tuple-element.206), channel_id=1, source_target_pairs={{0,16},{1,17},{2,18},{3,19},{4,20},{5,21},{6,22},{7,23},{8,24},{9,... | collective-permute-start | bytes 196616 | tf_op jit(solution)/shard_map/ppermute | solution.py:54
  9.1 6.1 %collective-permute-start.2 = (bf16[4,16,512]{2,1,0:T(8,128)(2,1)S(1)}, bf16[4,16,512]{2,1,0:T(8,128)(2,1)S(1)}, u32[]{:S(2)}, u32[]{:S(2)}) collective-permute-start(bf16[4,16,512]{2,1,0:T(8,128)(2,1)S(1)} %get-tuple-element.206), channel_id=1, source_target_pairs={{0,24},{1,25},{2,26},{3,27},{4,28},{5,29},{6,30},{7,31},{8,16},{9,... | collective-permute-start | bytes 196616 | tf_op jit(solution)/shard_map/ppermute | solution.py:54
  11.8 23.6 %copy-start.15 = (s32[1024]{0:T(1024)S(1)}, s32[1024]{0:T(1024)}, u32[]{:S(2)}) copy-start(s32[1024]{0:T(1024)} %param.23) | copy-start | bytes 12292
  15.2 22.3 %copy-start.4 = (bf16[4,4,16,512]{3,2,1,0:T(8,128)(2,1)}, bf16[4,4,16,512]{3,2,1,0:T(8,128)(2,1)S(1)}, u32[]{:S(2)}) copy-start(bf16[4,4,16,512]{3,2,1,0:T(8,128)(2,1)S(1)} %pad_maximum_fusion.2.refs_0_) | copy-start | bytes 786436
  15.2 21.3 %copy-start.16 = (s32[1024]{0:T(1024)S(1)}, s32[1024]{0:T(1024)}, u32[]{:S(2)}) copy-start(s32[1024]{0:T(1024)} %param.24) | copy-start | bytes 12292
  15.2 7.5 %collective-permute-start.3 = (bf16[11,16,512]{2,1,0:T(8,128)(2,1)S(1)}, bf16[11,16,512]{2,1,0:T(8,128)(2,1)S(1)}, u32[]{:S(2)}, u32[]{:S(2)}) collective-permute-start(bf16[11,16,512]{2,1,0:T(8,128)(2,1)S(1)} %constant_dynamic-update-slice_fusion), channel_id=1, source_target_pairs={{0,8},{1,9},{2,10},{3,11},{4,12},{5,13},{6,14},{7,15},{8,0},{9,1},... | collective-permute-start | bytes 540680 | tf_op jit(solution)/shard_map/ppermute | solution.py:54
  15.3 15.7 %collective-permute-start.4 = (bf16[11,16,512]{2,1,0:T(8,128)(2,1)S(1)}, bf16[11,16,512]{2,1,0:T(8,128)(2,1)S(1)}, u32[]{:S(2)}, u32[]{:S(2)}) collective-permute-start(bf16[11,16,512]{2,1,0:T(8,128)(2,1)S(1)} %constant_dynamic-update-slice_fusion), channel_id=1, source_target_pairs={{0,16},{1,17},{2,18},{3,19},{4,20},{5,21},{6,22},{7,23},{8,24},{9,... | collective-permute-start | bytes 540680 | tf_op jit(solution)/shard_map/ppermute | solution.py:54
  17.6 13.4 %collective-permute-start.5 = (bf16[11,16,512]{2,1,0:T(8,128)(2,1)S(1)}, bf16[11,16,512]{2,1,0:T(8,128)(2,1)S(1)}, u32[]{:S(2)}, u32[]{:S(2)}) collective-permute-start(bf16[11,16,512]{2,1,0:T(8,128)(2,1)S(1)} %constant_dynamic-update-slice_fusion), channel_id=1, source_target_pairs={{0,24},{1,25},{2,26},{3,27},{4,28},{5,29},{6,30},{7,31},{8,16},{9,... | collective-permute-start | bytes 540680 | tf_op jit(solution)/shard_map/ppermute | solution.py:54
  19.7 11.4 %collective-permute-start.6 = (bf16[4,4,16,512]{3,2,1,0:T(8,128)(2,1)S(1)}, bf16[4,4,16,512]{3,2,1,0:T(8,128)(2,1)S(1)}, u32[]{:S(2)}, u32[]{:S(2)}) collective-permute-start(bf16[4,4,16,512]{3,2,1,0:T(8,128)(2,1)S(1)} %pad_maximum_fusion.2.refs_0_), channel_id=1, source_target_pairs={{0,2},{1,3},{2,0},{3,1},{4,6},{5,7},{6,4},{7,5},{8,10},{9,11},{10,... | collective-permute-start | bytes 786440 | tf_op jit(solution)/shard_map/ppermute | solution.py:54
  21.1 11.7 %collective-permute-start.7 = (bf16[4,4,16,512]{3,2,1,0:T(8,128)(2,1)S(1)}, bf16[4,4,16,512]{3,2,1,0:T(8,128)(2,1)S(1)}, u32[]{:S(2)}, u32[]{:S(2)}) collective-permute-start(bf16[4,4,16,512]{3,2,1,0:T(8,128)(2,1)S(1)} %pad_maximum_fusion.2.refs_0_), channel_id=1, source_target_pairs={{0,4},{1,5},{2,6},{3,7},{4,0},{5,1},{6,2},{7,3},{8,12},{9,13},{10,... | collective-permute-start | bytes 786440 | tf_op jit(solution)/shard_map/ppermute | solution.py:54
  22.7 10.2 %collective-permute-start.8 = (bf16[4,4,16,512]{3,2,1,0:T(8,128)(2,1)S(1)}, bf16[4,4,16,512]{3,2,1,0:T(8,128)(2,1)S(1)}, u32[]{:S(2)}, u32[]{:S(2)}) collective-permute-start(bf16[4,4,16,512]{3,2,1,0:T(8,128)(2,1)S(1)} %pad_maximum_fusion.2.refs_0_), channel_id=1, source_target_pairs={{0,6},{1,7},{2,4},{3,5},{4,2},{5,3},{6,0},{7,1},{8,14},{9,15},{10,... | collective-permute-start | bytes 786440 | tf_op jit(solution)/shard_map/ppermute | solution.py:54
  31.0 10.5 %copy-start = (bf16[1024,512]{1,0:T(8,128)(2,1)S(1)}, bf16[1024,512]{1,0:T(8,128)(2,1)}, u32[]{:S(2)}) copy-start(bf16[1024,512]{1,0:T(8,128)(2,1)} %x_ref.3) | copy-start | bytes 3145732
  31.1 10.7 %copy-start.3 = (bf16[4,11,16,512]{3,2,1,0:T(8,128)(2,1)}, bf16[4,11,16,512]{3,2,1,0:T(8,128)(2,1)S(1)}, u32[]{:S(2)}) copy-start(bf16[4,11,16,512]{3,2,1,0:T(8,128)(2,1)S(1)} %pad_maximum_fusion.1.refs_0_) | copy-start | bytes 2162692
  31.1 10.6 %copy-start.7 = (bf16[4,4,16,512]{3,2,1,0:T(8,128)(2,1)}, bf16[4,4,16,512]{3,2,1,0:T(8,128)(2,1)S(1)}, u32[]{:S(2)}) copy-start(bf16[4,4,16,512]{3,2,1,0:T(8,128)(2,1)S(1)} %collective-permute-done.6.refs_1_) | copy-start | bytes 786436
  32.9 0.7 copy-start.8
  33.6 0.7 copy-start.9
  35.4 6.9 %collective-permute-start.9 = (bf16[16,4,16,512]{3,2,1,0:T(8,128)(2,1)}, bf16[16,4,16,512]{3,2,1,0:T(8,128)(2,1)S(1)}, u32[]{:S(2)}, u32[]{:S(2)}) collective-permute-start(bf16[16,4,16,512]{3,2,1,0:T(8,128)(2,1)} %pad_maximum_fusion), channel_id=1, source_target_pairs={{0,1},{1,0},{2,3},{3,2},{4,5},{5,4},{6,7},{7,6},{8,9},{9,8},{10,11... | collective-permute-start | bytes 3145736 | tf_op jit(solution)/shard_map/ppermute | solution.py:54
  37.5 23.0 %collective-permute-start.10 = (bf16[4,11,16,512]{3,2,1,0:T(8,128)(2,1)S(1)}, bf16[4,11,16,512]{3,2,1,0:T(8,128)(2,1)}, u32[]{:S(2)}, u32[]{:S(2)}) collective-permute-start(bf16[4,11,16,512]{3,2,1,0:T(8,128)(2,1)S(1)} %pad_maximum_fusion.1.refs_0_), channel_id=1, source_target_pairs={{0,1},{1,0},{2,3},{3,2},{4,5},{5,4},{6,7},{7,6},{8,9},{9,8},{10,11... | collective-permute-start | bytes 2162696 | tf_op jit(solution)/shard_map/ppermute | solution.py:54
  38.0 22.5 %collective-permute-start.11 = (bf16[4,11,16,512]{3,2,1,0:T(8,128)(2,1)S(1)}, bf16[4,11,16,512]{3,2,1,0:T(8,128)(2,1)}, u32[]{:S(2)}, u32[]{:S(2)}) collective-permute-start(bf16[4,11,16,512]{3,2,1,0:T(8,128)(2,1)S(1)} %pad_maximum_fusion.1.refs_0_), channel_id=1, source_target_pairs={{0,2},{1,3},{2,0},{3,1},{4,6},{5,7},{6,4},{7,5},{8,10},{9,11},{10,... | collective-permute-start | bytes 2162696 | tf_op jit(solution)/shard_map/ppermute | solution.py:54
  38.5 32.6 %collective-permute-start.12 = (bf16[4,11,16,512]{3,2,1,0:T(8,128)(2,1)S(1)}, bf16[4,11,16,512]{3,2,1,0:T(8,128)(2,1)}, u32[]{:S(2)}, u32[]{:S(2)}) collective-permute-start(bf16[4,11,16,512]{3,2,1,0:T(8,128)(2,1)S(1)} %pad_maximum_fusion.1.refs_0_), channel_id=1, source_target_pairs={{0,4},{1,5},{2,6},{3,7},{4,0},{5,1},{6,2},{7,3},{8,12},{9,13},{10,... | collective-permute-start | bytes 2162696 | tf_op jit(solution)/shard_map/ppermute | solution.py:54
  40.3 32.2 %collective-permute-start.13 = (bf16[4,11,16,512]{3,2,1,0:T(8,128)(2,1)S(1)}, bf16[4,11,16,512]{3,2,1,0:T(8,128)(2,1)}, u32[]{:S(2)}, u32[]{:S(2)}) collective-permute-start(bf16[4,11,16,512]{3,2,1,0:T(8,128)(2,1)S(1)} %pad_maximum_fusion.1.refs_0_), channel_id=1, source_target_pairs={{0,6},{1,7},{2,4},{3,5},{4,2},{5,3},{6,0},{7,1},{8,14},{9,15},{10,... | collective-permute-start | bytes 2162696 | tf_op jit(solution)/shard_map/ppermute | solution.py:54
  42.3 1.0 copy-start.6
  72.6 2.4 %collective-permute-start.14 = (bf16[4,11,16,512]{3,2,1,0:T(8,128)(2,1)}, bf16[4,11,16,512]{3,2,1,0:T(8,128)(2,1)S(1)}, u32[]{:S(2)}, u32[]{:S(2)}) collective-permute-start(bf16[4,11,16,512]{3,2,1,0:T(8,128)(2,1)} %collective-permute-done.11.refs_1_), channel_id=1, source_target_pairs={{0,1},{1,0},{2,3},{3,2},{4,5},{5,4},{6,7},{7,6},{8,9},{9,8},{10,11... | collective-permute-start | bytes 2162696 | tf_op jit(solution)/shard_map/ppermute | solution.py:54
  72.6 3.4 %collective-permute-start.15 = (bf16[4,11,16,512]{3,2,1,0:T(8,128)(2,1)}, bf16[4,11,16,512]{3,2,1,0:T(8,128)(2,1)S(1)}, u32[]{:S(2)}, u32[]{:S(2)}) collective-permute-start(bf16[4,11,16,512]{3,2,1,0:T(8,128)(2,1)} %collective-permute-done.12.refs_2_), channel_id=1, source_target_pairs={{0,1},{1,0},{2,3},{3,2},{4,5},{5,4},{6,7},{7,6},{8,9},{9,8},{10,11... | collective-permute-start | bytes 2162696 | tf_op jit(solution)/shard_map/ppermute | solution.py:54
  73.1 4.0 %collective-permute-start.16 = (bf16[4,11,16,512]{3,2,1,0:T(8,128)(2,1)}, bf16[4,11,16,512]{3,2,1,0:T(8,128)(2,1)S(1)}, u32[]{:S(2)}, u32[]{:S(2)}) collective-permute-start(bf16[4,11,16,512]{3,2,1,0:T(8,128)(2,1)} %collective-permute-done.13.refs_3_), channel_id=1, source_target_pairs={{0,1},{1,0},{2,3},{3,2},{4,5},{5,4},{6,7},{7,6},{8,9},{9,8},{10,11... | collective-permute-start | bytes 2162696 | tf_op jit(solution)/shard_map/ppermute | solution.py:54
  75.0 2.1 copy-start.12
  76.0 1.0 copy-start.13
  77.0 0.9 copy-start.14
  108.6 5.6 %collective-permute-start.17 = (bf16[16,11,16,512]{3,2,1,0:T(8,128)(2,1)}, bf16[16,11,16,512]{3,2,1,0:T(8,128)(2,1)S(1)}, u32[]{:S(2)}, u32[]{:S(2)}) collective-permute-start(bf16[16,11,16,512]{3,2,1,0:T(8,128)(2,1)} %get-tuple-element.123), channel_id=1, source_target_pairs={{0,1},{1,0},{2,3},{3,2},{4,5},{5,4},{6,7},{7,6},{8,9},{9,8},{10,11... | collective-permute-start | bytes 8650760 | tf_op jit(solution)/shard_map/ppermute | solution.py:54
  118.3 33.0 %collective-permute-start.18 = (bf16[4,11,16,512]{3,2,1,0:T(8,128)(2,1)}, bf16[4,11,16,512]{3,2,1,0:T(8,128)(2,1)S(1)}, u32[]{:S(2)}, u32[]{:S(2)}) collective-permute-start(bf16[4,11,16,512]{3,2,1,0:T(8,128)(2,1)} %get-tuple-element.137), channel_id=1, source_target_pairs={{0,2},{1,3},{2,0},{3,1},{4,6},{5,7},{6,4},{7,5},{8,10},{9,11},{10,... | collective-permute-start | bytes 2162696 | tf_op jit(solution)/shard_map/ppermute | solution.py:54
  119.1 32.7 %collective-permute-start.19 = (bf16[4,11,16,512]{3,2,1,0:T(8,128)(2,1)}, bf16[4,11,16,512]{3,2,1,0:T(8,128)(2,1)}, u32[]{:S(2)}, u32[]{:S(2)}) collective-permute-start(bf16[4,11,16,512]{3,2,1,0:T(8,128)(2,1)} %get-tuple-element.138), channel_id=1, source_target_pairs={{0,4},{1,5},{2,6},{3,7},{4,0},{5,1},{6,2},{7,3},{8,12},{9,13},{10,... | collective-permute-start | bytes 2162696 | tf_op jit(solution)/shard_map/ppermute | solution.py:54
  120.6 32.2 %collective-permute-start.20 = (bf16[4,11,16,512]{3,2,1,0:T(8,128)(2,1)}, bf16[4,11,16,512]{3,2,1,0:T(8,128)(2,1)}, u32[]{:S(2)}, u32[]{:S(2)}) collective-permute-start(bf16[4,11,16,512]{3,2,1,0:T(8,128)(2,1)} %get-tuple-element.139), channel_id=1, source_target_pairs={{0,6},{1,7},{2,4},{3,5},{4,2},{5,3},{6,0},{7,1},{8,14},{9,15},{10,... | collective-permute-start | bytes 2162696 | tf_op jit(solution)/shard_map/ppermute | solution.py:54
  121.8 32.2 %copy-start.18 = (f32[1,2048]{1,0:T(1,128)S(1)}, f32[1,2048]{1,0:T(1,128)}, u32[]{:S(2)}) copy-start(f32[1,2048]{1,0:T(1,128)} %get-tuple-element.156) | copy-start | bytes 24580
  151.3 9.9 %copy-start.10 = (bf16[16,3,16,512]{3,2,1,0:T(8,128)(2,1)S(1)}, bf16[16,3,16,512]{3,2,1,0:T(8,128)(2,1)}, u32[]{:S(2)}) copy-start(bf16[16,3,16,512]{3,2,1,0:T(8,128)(2,1)} %get-tuple-element.141) | copy-start | bytes 2359300
  151.3 1.5 copy-start.11
  152.8 8.4 %collective-permute-start.21 = (bf16[16,3,16,512]{3,2,1,0:T(8,128)(2,1)}, bf16[16,3,16,512]{3,2,1,0:T(8,128)(2,1)S(1)}, u32[]{:S(2)}, u32[]{:S(2)}) collective-permute-start(bf16[16,3,16,512]{3,2,1,0:T(8,128)(2,1)} %get-tuple-element.142), channel_id=1, source_target_pairs={{0,1},{1,0},{2,3},{3,2},{4,5},{5,4},{6,7},{7,6},{8,9},{9,8},{10,11... | collective-permute-start | bytes 2359304 | tf_op jit(solution)/shard_map/ppermute | solution.py:54
  154.7 6.8 %copy-start.2 = (f32[1024,512]{1,0:T(8,128)S(1)}, f32[1024,512]{1,0:T(8,128)}, u32[]{:S(2)}) copy-start(f32[1024,512]{1,0:T(8,128)} %get-tuple-element.143) | copy-start | bytes 6291460
  156.7 4.8 %copy-start.1 = (bf16[1024,512]{1,0:T(8,128)(2,1)S(1)}, bf16[1024,512]{1,0:T(8,128)(2,1)}, u32[]{:S(2)}) copy-start(bf16[1024,512]{1,0:T(8,128)(2,1)} %x_ref.3) | copy-start | bytes 3145732
  156.7 10.6 %collective-permute-start.22 = (bf16[11,16,512]{2,1,0:T(8,128)(2,1)S(1)}, bf16[11,16,512]{2,1,0:T(8,128)(2,1)S(1)}, u32[]{:S(2)}, u32[]{:S(2)}) collective-permute-start(bf16[11,16,512]{2,1,0:T(8,128)(2,1)S(1)} %get-tuple-element.197), channel_id=1, source_target_pairs={{0,8},{1,9},{2,10},{3,11},{4,12},{5,13},{6,14},{7,15},{8,0},{9,1},... | collective-permute-start | bytes 540680 | tf_op jit(solution)/shard_map/ppermute | solution.py:54
  158.2 16.1 %collective-permute-start.23 = (bf16[11,16,512]{2,1,0:T(8,128)(2,1)S(1)}, bf16[11,16,512]{2,1,0:T(8,128)(2,1)S(1)}, u32[]{:S(2)}, u32[]{:S(2)}) collective-permute-start(bf16[11,16,512]{2,1,0:T(8,128)(2,1)S(1)} %get-tuple-element.196), channel_id=1, source_target_pairs={{0,16},{1,17},{2,18},{3,19},{4,20},{5,21},{6,22},{7,23},{8,24},{9,... | collective-permute-start | bytes 540680 | tf_op jit(solution)/shard_map/ppermute | solution.py:54
  159.6 14.7 %collective-permute-start.24 = (bf16[11,16,512]{2,1,0:T(8,128)(2,1)S(1)}, bf16[11,16,512]{2,1,0:T(8,128)(2,1)S(1)}, u32[]{:S(2)}, u32[]{:S(2)}) collective-permute-start(bf16[11,16,512]{2,1,0:T(8,128)(2,1)S(1)} %get-tuple-element.195), channel_id=1, source_target_pairs={{0,24},{1,25},{2,26},{3,27},{4,28},{5,29},{6,30},{7,31},{8,16},{9,... | collective-permute-start | bytes 540680 | tf_op jit(solution)/shard_map/ppermute | solution.py:54
  161.5 7.6 %copy-start.5 = (f32[1024,512]{1,0:T(8,128)S(1)}, f32[1024,512]{1,0:T(8,128)}, u32[]{:S(2)}) copy-start(f32[1024,512]{1,0:T(8,128)} %get-tuple-element.118) | copy-start | bytes 6291460
  162.8 11.5 %collective-permute-start.25 = (bf16[4,3,16,512]{3,2,1,0:T(8,128)(2,1)S(1)}, bf16[4,3,16,512]{3,2,1,0:T(8,128)(2,1)S(1)}, u32[]{:S(2)}, u32[]{:S(2)}) collective-permute-start(bf16[4,3,16,512]{3,2,1,0:T(8,128)(2,1)S(1)} %get-tuple-element.149), channel_id=1, source_target_pairs={{0,2},{1,3},{2,0},{3,1},{4,6},{5,7},{6,4},{7,5},{8,10},{9,11},{10,... | collective-permute-start | bytes 589832 | tf_op jit(solution)/shard_map/ppermute | solution.py:54
  164.0 10.3 %collective-permute-start.26 = (bf16[4,3,16,512]{3,2,1,0:T(8,128)(2,1)S(1)}, bf16[4,3,16,512]{3,2,1,0:T(8,128)(2,1)S(1)}, u32[]{:S(2)}, u32[]{:S(2)}) collective-permute-start(bf16[4,3,16,512]{3,2,1,0:T(8,128)(2,1)S(1)} %get-tuple-element.150), channel_id=1, source_target_pairs={{0,4},{1,5},{2,6},{3,7},{4,0},{5,1},{6,2},{7,3},{8,12},{9,13},{10,... | collective-permute-start | bytes 589832 | tf_op jit(solution)/shard_map/ppermute | solution.py:54
  167.3 7.4 %collective-permute-start.27 = (bf16[4,3,16,512]{3,2,1,0:T(8,128)(2,1)S(1)}, bf16[4,3,16,512]{3,2,1,0:T(8,128)(2,1)S(1)}, u32[]{:S(2)}, u32[]{:S(2)}) collective-permute-start(bf16[4,3,16,512]{3,2,1,0:T(8,128)(2,1)S(1)} %get-tuple-element.151), channel_id=1, source_target_pairs={{0,6},{1,7},{2,4},{3,5},{4,2},{5,3},{6,0},{7,1},{8,14},{9,15},{10,... | collective-permute-start | bytes 589832 | tf_op jit(solution)/shard_map/ppermute | solution.py:54
  170.8 17.3 %copy-start.17 = (f32[8,512]{1,0:T(8,128)S(1)}, f32[8,512]{1,0:T(8,128)}, u32[]{:S(2)}) copy-start(f32[8,512]{1,0:T(8,128)} %get-tuple-element.155) | copy-start | bytes 49156
  174.8 8.7 %collective-permute-start.28 = (bf16[3,16,512]{2,1,0:T(8,128)(2,1)S(1)}, bf16[3,16,512]{2,1,0:T(8,128)(2,1)S(1)}, u32[]{:S(2)}, u32[]{:S(2)}) collective-permute-start(bf16[3,16,512]{2,1,0:T(8,128)(2,1)S(1)} %get-tuple-element.202), channel_id=1, source_target_pairs={{0,8},{1,9},{2,10},{3,11},{4,12},{5,13},{6,14},{7,15},{8,0},{9,1},... | collective-permute-start | bytes 147464 | tf_op jit(solution)/shard_map/ppermute | solution.py:54
  178.1 6.3 %collective-permute-start.29 = (bf16[3,16,512]{2,1,0:T(8,128)(2,1)S(1)}, bf16[3,16,512]{2,1,0:T(8,128)(2,1)S(1)}, u32[]{:S(2)}, u32[]{:S(2)}) collective-permute-start(bf16[3,16,512]{2,1,0:T(8,128)(2,1)S(1)} %get-tuple-element.204), channel_id=1, source_target_pairs={{0,16},{1,17},{2,18},{3,19},{4,20},{5,21},{6,22},{7,23},{8,24},{9,... | collective-permute-start | bytes 147464 | tf_op jit(solution)/shard_map/ppermute | solution.py:54
  179.5 6.0 %collective-permute-start.30 = (bf16[3,16,512]{2,1,0:T(8,128)(2,1)S(1)}, bf16[3,16,512]{2,1,0:T(8,128)(2,1)S(1)}, u32[]{:S(2)}, u32[]{:S(2)}) collective-permute-start(bf16[3,16,512]{2,1,0:T(8,128)(2,1)S(1)} %get-tuple-element.203), channel_id=1, source_target_pairs={{0,24},{1,25},{2,26},{3,27},{4,28},{5,29},{6,30},{7,31},{8,16},{9,... | collective-permute-start | bytes 147464 | tf_op jit(solution)/shard_map/ppermute | solution.py:54
  188.3 1.3 collective-permute-start.31
  189.5 3.9 %collective-permute-start.32 = (f32[12,512]{1,0:T(8,128)S(1)}, f32[12,512]{1,0:T(8,128)S(1)}, u32[]{:S(2)}, u32[]{:S(2)}) collective-permute-start(f32[12,512]{1,0:T(8,128)S(1)} %add.253), channel_id=1, source_target_pairs={{0,2},{1,3},{2,0},{3,1},{4,6},{5,7},{6,4},{7,5},{8,10},{9,11},{10,... | collective-permute-start | bytes 73736 | tf_op jit(solution)/shard_map/ppermute | solution.py:54
  193.5 3.9 %collective-permute-start.33 = (f32[12,512]{1,0:T(8,128)S(1)}, f32[12,512]{1,0:T(8,128)S(1)}, u32[]{:S(2)}, u32[]{:S(2)}) collective-permute-start(f32[12,512]{1,0:T(8,128)S(1)} %add.254), channel_id=1, source_target_pairs={{0,4},{1,5},{2,6},{3,7},{4,0},{5,1},{6,2},{7,3},{8,12},{9,13},{10,... | collective-permute-start | bytes 73736 | tf_op jit(solution)/shard_map/ppermute | solution.py:54
  197.4 3.9 %collective-permute-start.34 = (f32[12,512]{1,0:T(8,128)S(1)}, f32[12,512]{1,0:T(8,128)S(1)}, u32[]{:S(2)}, u32[]{:S(2)}) collective-permute-start(f32[12,512]{1,0:T(8,128)S(1)} %add.255), channel_id=1, source_target_pairs={{0,8},{1,9},{2,10},{3,11},{4,12},{5,13},{6,14},{7,15},{8,0},{9,1},... | collective-permute-start | bytes 73736 | tf_op jit(solution)/shard_map/ppermute | solution.py:54
  201.3 5.2 %collective-permute-start.35 = (f32[12,512]{1,0:T(8,128)S(1)}, f32[12,512]{1,0:T(8,128)S(1)}, u32[]{:S(2)}, u32[]{:S(2)}) collective-permute-start(f32[12,512]{1,0:T(8,128)S(1)} %add.256), channel_id=1, source_target_pairs={{0,16},{1,17},{2,18},{3,19},{4,20},{5,21},{6,22},{7,23},{8,24},{9,... | collective-permute-start | bytes 73736 | tf_op jit(solution)/shard_map/ppermute | solution.py:54

commit v3 on v2

--- a/solution.py
+++ b/solution.py
@@ -80,6 +80,26 @@
         [(plane << plane_bit) | (z << z_bit) for z in range(2**z_bits)] for plane in range(2**plane_bits)
     ]
     return table + [[offset | 1 for row in table for offset in row]]
+
+
+def plane_orders(groups):
+    _, (first_bit, bits), _ = stage_bits(groups)
+    order = list(range(first_bit, first_bit + bits))
+    return order, order[bits // 2 :] + order[: bits // 2]
+
+
+def z_offsets(groups):
+    _, _, (first_bit, bits) = stage_bits(groups)
+    return [z << first_bit for z in range(2**bits)]
+
+
+def send_halves(arrays, orders, position, groups):
+    count = 2 ** sum(groups)
+    return [swap_with(array, 1 << order[position], count) for array, order in zip(arrays, orders)]
+
+
+def flip_tables(tables, bits):
+    return [[offset ^ (1 << bit) for offset in table] for table, bit in zip(tables, bits)]
 
 
 def vmem_spec():
@@ -317,7 +337,7 @@
 def seg_args(segments,positions):
     return (segments[:,None],positions[:,None],segments[None],positions[None])
 
-def attend(own, tokens, segments, positions, parts, tables, layout, groups):
+def attend(own, tokens, marks, parts, tables, layout, groups):
     rows, width = tokens.shape
     count = 2 ** sum(groups)
     step = parts[0].shape[2]
@@ -349,13 +369,13 @@
         out_shape=out_shape,
         scratch_shapes=[pltpu.VMEM((rows, rows), jnp.float32)] + [pltpu.VMEM((pairs, rows, lanes), low)] * 3,
         name="attn_fwd",
-    )(own[None].astype(jnp.int32), *seg_args(segments, positions), tokens, *parts)
+    )(own[None].astype(jnp.int32), *marks, tokens, *parts)
     if not direct:
         result = list(result) + list(parts)
     return result
 
 
-def attend_back(own, q, k, v, do, lse, segments, positions, normed, w_qkv, start, groups):
+def attend_back(own, q, k, v, do, lse, marks, normed, w_qkv, start, groups):
     rows, width = q.shape
     lanes = 2 * HEAD
     count = 2 ** sum(groups)
@@ -395,7 +415,7 @@
             dw_scratch,
         ],
         name="attn_bwd",
-    )(own[None].astype(jnp.int32), *seg_args(segments, positions), q, k, v, do, lse, normed, w_qkv, start)
+    )(own[None].astype(jnp.int32), *marks, q, k, v, do, lse, normed, w_qkv, start)
     if offsets is None:
         grads = split(own, [grads[0].reshape(3, count, step, width)], [("stack", 0, 3)], groups)
     return grads[0], grads[1], dh
@@ -701,19 +721,36 @@
             low(out_weight).reshape(4, step, width),
         ]
     )
+    cut = 6
+    orders = plane_orders(groups)
     z_first = gather_z(first_shard, groups)
-    z_first, second_shard = tie(z_first, second_shard)
     plane_first = gather_plane(z_first, groups)
     z_second = gather_z(second_shard, groups)
-    z_first, z_second, *plane_first = tie(z_first, z_second, *plane_first)
+    tied = tie(z_first, z_second[:, :cut], z_second[:, cut:], *plane_first)
+    z_first, halves, plane_first = tied[0], tied[1:3], list(tied[3:])
     core_first = gather_core(z_first, plane_first, groups)
-    plane_second = gather_plane(z_second, groups)
+    tables = [z_offsets(groups)] * 2
+    received = send_halves(halves, orders, 0, groups)
+    inputs = tokens.astype(jnp.float32)
+    mean_one = jnp.mean(inputs, -1, keepdims=True)
+    scale_one = lax.rsqrt(jnp.mean((inputs - mean_one) * (inputs - mean_one), -1, keepdims=True) + norm_eps)
+    marks = seg_args(segments, positions)
+    core_first, mean_one, scale_one, *tied = tie(core_first, mean_one, scale_one, *marks, *received)
+    marks, received = tied[:4], tied[4:]
+    last = len(orders[0]) - 1
+    for position in range(last):
+        tables = [
+            table + row
+            for table, row in zip(tables, flip_tables(tables, [order[position] for order in orders]))
+        ]
+        halves = [jnp.concatenate(pair) for pair in zip(halves, received)]
+        received = send_halves(halves, orders, position + 1, groups)
+    far_tables = flip_tables(tables, [order[last] for order in orders])
     relative = offsets_of(groups)
     normed, queries, keys, values, mixed_heads, log_total, w_qkv, vectors = attend(
         own,
         tokens,
-        segments,
-        positions,
+        marks,
         [z_first] + plane_first + [core_first],
         [(row, 0) for row in relative],
         [("stack", 0, 3), ("sum", 3, extra)],
@@ -721,15 +758,11 @@
     )
     w_qkv = w_qkv.reshape(3, count * step, width)
     bias = vectors[7:11].reshape(-1)
-    inputs = tokens.astype(jnp.float32)
-    mean_one = jnp.mean(inputs, -1, keepdims=True)
-    scale_one = lax.rsqrt(jnp.mean((inputs - mean_one) * (inputs - mean_one), -1, keepdims=True) + norm_eps)
-    core_second = [swap_with(z_second, 1, count)]
-    mixed_heads, mean_one, scale_one, core_second[0], *plane_second = tie(
-        mixed_heads, mean_one, scale_one, core_second[0], *plane_second
-    )
+    core_near = [swap_with(half, 1, count) for half in halves]
+    mixed_heads, *tied = tie(mixed_heads, *core_near, *received)
+    core_near, received = tied[:2], tied[2:]
+    core_far = [swap_with(half, 1, count) for half in received]
     unit_one = (inputs - mean_one) * scale_one
-    core_second += [swap_with(part, 1, count) for part in plane_second]
     layer_out, grad_mixed, grad_normed, grad_inputs, sums, grad_bias, kept_b, sent_b = ffn(
         own,
         tokens,
@@ -738,8 +771,13 @@
         mixed_heads,
         vectors,
         bias,
-        [z_second] + plane_second + core_second,
-        [(row, 0) for row in relative[:-1]] + [([offset | 1 for offset in row], 0) for row in relative[:-1]],
+        list(halves) + list(received) + list(core_near) + core_far,
+        [
+            ([offset | core for offset in table], first)
+            for core in range(2)
+            for half_tables in (tables, far_tables)
+            for table, first in zip(half_tables, (0, cut))
+        ],
         groups,
     )
     core_b = swap_with(sent_b, 1, count)
@@ -748,7 +786,7 @@
     own_b, log_total, *parts_b = tie(own_b, log_total, *parts_b)
     plane_b = plane_send(parts_b, groups)
     kept_a, sent_a, grad_normed = attend_back(
-        own, queries, keys, values, grad_mixed, log_total, segments, positions, normed, w_qkv, grad_normed, groups
+        own, queries, keys, values, grad_mixed, log_total, marks, normed, w_qkv, grad_normed, groups
     )
     kept_a, sent_a, grad_normed, own_b, *plane_b = tie(kept_a, sent_a, grad_normed, own_b, *plane_b)
     core_a = swap_with(sent_a, 1, count)

time: 211 us -> 203 us (0.962)
  waiting for transfers between devices: 55.2 us -> 47.2 us
  starting transfers between devices: 42 us -> 44.2 us
    ppermute x36 -> x37, waiting for transfers between devices: 55.2 us -> 47.2 us  [swap_with(): lax.ppermute(array, AXES, [(source, source ^ offset) for source in range(...]
    ppermute x36 -> x37, starting transfers between devices: 42 us -> 44.2 us  [swap_with(): lax.ppermute(array, AXES, [(source, source ^ offset) for source in range(...]
    unnamed x45 -> x49, local copies, waits for them, and re-layouts: 4.7 us -> 3.1 us
  transfers between devices with their start and end apart: 36 -> 37, of which waited for: 22 -> 17; matrix products, arithmetic and copies ran while one was open for 8% -> 8% of each run, Pallas kernels for 22% -> 23%
where the time goes in v3:
time: 203 us; the launch traced here: 202 us
  Pallas kernels  80.5 us (40%)
  waiting for transfers between devices  47.2 us (23%)
  starting transfers between devices  44.2 us (22%)
  other arithmetic  19.4 us (10%)
  local copies, waits for them, and re-layouts  8.21 us (4%)
  between operations  2.67 us (1%)
    ppermute x37, waiting for transfers between devices, swap_with(): lax.ppermute(array, AXES, [(source, source ^ offset) for source in range(...  47.2 us
    ppermute x37, starting transfers between devices, swap_with(): lax.ppermute(array, AXES, [(source, source ^ offset) for source in range(...  44.2 us
    pallas_call x1, Pallas kernels, ffn(): pl.pallas_call(functools.partial(ffn_kernel, direct, len(parts), tables,...  30.7 us
    pallas_call x1, Pallas kernels, attend_back(): pl.pallas_call(functools.partial(attn_bwd_kernel, offsets), grid=(width /...  29.5 us
    pallas_call x1, Pallas kernels, attend(): pl.pallas_call(functools.partial(attn_fwd_kernel, direct, tables, layout)...  17.3 us
    convert_element_type x2, other arithmetic, plane_sums(): total(offset).astype(jnp.bfloat16)  4.42 us
  transfers between devices with their start and end apart: 37, of which 17 were waited for; matrix products, arithmetic and copies ran while one was open for 8% of the time, Pallas kernels for 23%

profile of v3, /device:TPU:0, one launch (start us, length us, event | category | flops | bytes accessed | tf_op | source)
XLA Modules:
  0.0 202.1 jit_solution(15696268711252084876)
XLA Ops:
  0.7 0.9 convert.28
  1.6 0.7 tile.8
  2.4 0.7 tile.19
  3.3 3.1 %collective-permute-start = (bf16[4,16,512]{2,1,0:T(8,128)(2,1)S(1)}, bf16[4,16,512]{2,1,0:T(8,128)(2,1)S(1)}, u32[]{:S(2)}, u32[]{:S(2)}) collective-permute-start(bf16[4,16,512]{2,1,0:T(8,128)(2,1)S(1)} %get-tuple-element.218), channel_id=1, source_target_pairs={{0,8},{1,9},{2,10},{3,11},{4,12},{5,13},{6,14},{7,15},{8,0},{9,1},... | collective-permute-start | bytes 196616 | tf_op jit(solution)/shard_map/ppermute | solution.py:54
  6.5 2.6 %collective-permute-start.1 = (bf16[4,16,512]{2,1,0:T(8,128)(2,1)S(1)}, bf16[4,16,512]{2,1,0:T(8,128)(2,1)S(1)}, u32[]{:S(2)}, u32[]{:S(2)}) collective-permute-start(bf16[4,16,512]{2,1,0:T(8,128)(2,1)S(1)} %get-tuple-element.218), channel_id=1, source_target_pairs={{0,16},{1,17},{2,18},{3,19},{4,20},{5,21},{6,22},{7,23},{8,24},{9,... | collective-permute-start | bytes 196616 | tf_op jit(solution)/shard_map/ppermute | solution.py:54
  9.0 0.9 convert_element_type.207
  10.0 0.8 convert_dynamic-update-slice_fusion
  10.8 0.9 convert_element_type.208
  11.8 1.0 collective-permute-start.3
  12.7 3.5 %collective-permute-start.4 = (bf16[11,16,512]{2,1,0:T(8,128)(2,1)S(1)}, bf16[11,16,512]{2,1,0:T(8,128)(2,1)S(1)}, u32[]{:S(2)}, u32[]{:S(2)}) collective-permute-start(bf16[11,16,512]{2,1,0:T(8,128)(2,1)S(1)} %constant_dynamic-update-slice_fusion), channel_id=1, source_target_pairs={{0,16},{1,17},{2,18},{3,19},{4,20},{5,21},{6,22},{7,23},{8,24},{9,... | collective-permute-start | bytes 540680 | tf_op jit(solution)/shard_map/ppermute | solution.py:54
  16.3 1.8 collective-permute-start.6
  18.1 1.5 collective-permute-start.7
  19.6 1.4 collective-permute-done.3
  21.0 2.4 %collective-permute-start.8 = (bf16[4,4,16,512]{3,2,1,0:T(8,128)(2,1)S(1)}, bf16[4,4,16,512]{3,2,1,0:T(8,128)(2,1)S(1)}, u32[]{:S(2)}, u32[]{:S(2)}) collective-permute-start(bf16[4,4,16,512]{3,2,1,0:T(8,128)(2,1)S(1)} %pad_maximum_fusion.3.refs_0_), channel_id=1, source_target_pairs={{0,6},{1,7},{2,4},{3,5},{4,2},{5,3},{6,0},{7,1},{8,14},{9,15},{10,... | collective-permute-start | bytes 786440 | tf_op jit(solution)/shard_map/ppermute | solution.py:54
  23.5 5.8 %collective-permute-done.4 = bf16[11,16,512]{2,1,0:T(8,128)(2,1)S(1)} collective-permute-done((bf16[11,16,512]{2,1,0:T(8,128)(2,1)S(1)}, bf16[11,16,512]{2,1,0:T(8,128)(2,1)S(1)}, u32[]{:S(2)}, u32[]{:S(2)}) %collective-permute-start.4) | collective-permute-done | bytes 180256 | tf_op jit(solution)/shard_map/ppermute | solution.py:54
  31.0 1.7 collective-permute-start.10
  33.3 1.6 collective-permute-start.11
  34.9 7.2 %collective-permute-done.11 = bf16[4,5,16,512]{3,2,1,0:T(8,128)(2,1)S(1)} collective-permute-done((bf16[4,5,16,512]{3,2,1,0:T(8,128)(2,1)S(1)}, bf16[4,5,16,512]{3,2,1,0:T(8,128)(2,1)S(1)}, u32[]{:S(2)}, u32[]{:S(2)}) %collective-permute-start.11) | collective-permute-done | bytes 327712 | tf_op jit(solution)/shard_map/ppermute | solution.py:54
  42.3 1.6 collective-permute-start.14
  44.1 1.0 collective-permute-start.15
  45.1 1.0 copy.43.segc
  46.2 1.0 copy.44.posc
  47.2 17.3 %attn_fwd.1 = (bf16[1024,512]{1,0:T(8,128)(2,1)}, bf16[1024,512]{1,0:T(8,128)(2,1)}, bf16[1024,512]{1,0:T(8,128)(2,1)}, bf16[1024,512]{1,0:T(8,128)(2,1)}, bf16[...) custom-call(s32[1]{0:T(128)} %bitcast.own_ref, ...), custom_call_target="tpu_custom_call" | custom-call | tf_op jit(solution)/shard_map/attn_fwd/pallas_call | solution.py:362
  65.1 0.8 slice_bitcast_fusion.4
  65.9 0.6 copy.47
  66.5 1.6 collective-permute-done.17.refs_7_
  68.1 0.8 copy-done.15
  69.2 30.7 %ffn.1 = (bf16[1024,512]{1,0:T(8,128)(2,1)}, bf16[1024,512]{1,0:T(8,128)(2,1)}, f32[1024,512]{1,0:T(8,128)}, f32[1024,512]{1,0:T(8,128)}, f32[8,512]{1,0:T(8,128...) custom-call(s32[1]{0:T(128)} %bitcast.own_ref, ...), custom_call_target="tpu_custom_call" | custom-call | tf_op jit(solution)/shard_map/ffn/pallas_call | solution.py:595
  100.1 5.4 %collective-permute-done.18 = bf16[16,11,16,512]{3,2,1,0:T(8,128)(2,1)S(1)} collective-permute-done((bf16[16,11,16,512]{3,2,1,0:T(8,128)(2,1)}, bf16[16,11,16,512]{3,2,1,0:T(8,128)(2,1)S(1)}, u32[]{:S(2)}, u32[]{:S(2)}) %collective-permute-start.18) | collective-permute-done | bytes 2883616 | tf_op jit(solution)/shard_map/ppermute | solution.py:54
  105.5 4.1 %add_convert_fusion = (bf16[4,11,16,512]{3,2,1,0:T(8,128)(2,1)}, bf16[4,11,16,512]{3,2,1,0:T(8,128)(2,1)}, bf16[4,11,16,512]{3,2,1,0:T(8,128)(2,1)}, f32[4,11,16,512]{3,2,1,0:T(8,128)S(1)}) fusion(bf16[16,11,16,512]{3,2,1,0:T(8,128)(2,1)S(1)} %collective-permute-done.18, bf16[16,11,16,512]{3,2,1,0:T(8,128)(2,1)} %get-tuple-element.139), kind=kLoop, calls=%fused_computation.16 | loop fusion | flops 5406720 | bytes 9371648 | tf_op jit(solution)/shard_map/convert_element_type | solution.py:160
  109.6 1.0 collective-permute-start.19
  111.2 2.0 collective-permute-start.21
  113.1 29.5 %attn_bwd.1 = (bf16[16,3,16,512]{3,2,1,0:T(8,128)(2,1)}, bf16[16,3,16,512]{3,2,1,0:T(8,128)(2,1)}, f32[1024,512]{1,0:T(8,128)}) custom-call(s32[1]{0:T(128)} %bitcast.own_ref, s32[1024,1]{1,0:T(8,128)} %copy.43.segc, s32[1024,1]{1,0:T(8,128)} %copy.44.posc, s32[1,1024]{1,0:T(1,128)} %bitcast.85, s32[1,1024]{1,0:T(1,128)} %bitcast.88, ...), custom_call_target="tpu_custom_call" | custom-call | tf_op jit(solution)/shard_map/attn_bwd/pallas_call | solution.py:398
  142.6 1.7 collective-permute-done.20
  144.3 0.7 slice.220
  145.6 0.7 reduce.3
  146.3 2.0 fusion.14
  148.3 2.6 %collective-permute-start.23 = (bf16[11,16,512]{2,1,0:T(8,128)(2,1)S(1)}, bf16[11,16,512]{2,1,0:T(8,128)(2,1)S(1)}, u32[]{:S(2)}, u32[]{:S(2)}) collective-permute-start(bf16[11,16,512]{2,1,0:T(8,128)(2,1)S(1)} %get-tuple-element.209), channel_id=1, source_target_pairs={{0,8},{1,9},{2,10},{3,11},{4,12},{5,13},{6,14},{7,15},{8,0},{9,1},... | collective-permute-start | bytes 540680 | tf_op jit(solution)/shard_map/ppermute | solution.py:54
  150.8 1.7 collective-permute-start.24
  152.5 0.8 collective-permute-start.25
  153.6 1.2 fusion.11
  154.8 1.1 collective-permute-start.26
  156.0 0.7 collective-permute-start.27
  156.6 2.8 %collective-permute-done.23 = bf16[11,16,512]{2,1,0:T(8,128)(2,1)S(1)} collective-permute-done((bf16[11,16,512]{2,1,0:T(8,128)(2,1)S(1)}, bf16[11,16,512]{2,1,0:T(8,128)(2,1)S(1)}, u32[]{:S(2)}, u32[]{:S(2)}) %collective-permute-start.23) | collective-permute-done | bytes 180256 | tf_op jit(solution)/shard_map/ppermute | solution.py:54
  159.4 1.2 collective-permute-start.28
  160.6 1.7 fusion.10
  162.3 4.6 %collective-permute-done.24 = bf16[11,16,512]{2,1,0:T(8,128)(2,1)S(1)} collective-permute-done((bf16[11,16,512]{2,1,0:T(8,128)(2,1)S(1)}, bf16[11,16,512]{2,1,0:T(8,128)(2,1)S(1)}, u32[]{:S(2)}, u32[]{:S(2)}) %collective-permute-start.24) | collective-permute-done | bytes 180256 | tf_op jit(solution)/shard_map/ppermute | solution.py:54
  167.1 3.6 %collective-permute-start.29 = (bf16[3,16,512]{2,1,0:T(8,128)(2,1)S(1)}, bf16[3,16,512]{2,1,0:T(8,128)(2,1)S(1)}, u32[]{:S(2)}, u32[]{:S(2)}) collective-permute-start(bf16[3,16,512]{2,1,0:T(8,128)(2,1)S(1)} %get-tuple-element.214), channel_id=1, source_target_pairs={{0,8},{1,9},{2,10},{3,11},{4,12},{5,13},{6,14},{7,15},{8,0},{9,1},... | collective-permute-start | bytes 147464 | tf_op jit(solution)/shard_map/ppermute | solution.py:54
  170.8 1.0 collective-permute-start.30
  171.8 1.4 collective-permute-start.31
  173.2 2.6 %multiply_reduce_fusion.1 = (f32[]{:T(128)}, f32[11,16,512]{2,1,0:T(8,128)}) fusion(bf16[11,16,512]{2,1,0:T(8,128)(2,1)S(1)} %collective-permute-done.25, bf16[11,16,512]{2,1,0:T(8,128)(2,1)S(1)} %collective-permute-done.24, bf16[11,16,512]{2,1,0:T(8,128)(2,1)S(1)} %collective-permute-done.23, bf16[4,11,16,512]{3,2,1,0:T(8,128)(2,1)} %collective-permute-done.21, ...), kind=kLoop, calls=%fused_computation.27 | loop fusion | flops 1261567 | bytes 1802244 | tf_op jit(solution)/shard_map/reduce_sum | solution.py:808
  175.8 1.0 collective-permute-done.30
  176.8 1.0 collective-permute-done.31
  177.8 1.3 multiply_reduce_fusion.2
  180.6 1.2 collective-permute-done.32
  181.8 1.0 collective-permute-start.33
  182.8 2.9 %collective-permute-done.33 = f32[12,512]{1,0:T(8,128)S(1)} collective-permute-done((f32[12,512]{1,0:T(8,128)S(1)}, f32[12,512]{1,0:T(8,128)S(1)}, u32[]{:S(2)}, u32[]{:S(2)}) %collective-permute-start.33) | collective-permute-done | bytes 24608 | tf_op jit(solution)/shard_map/ppermute | solution.py:54
  185.7 0.8 collective-permute-start.34
  186.5 3.2 %collective-permute-done.34 = f32[12,512]{1,0:T(8,128)S(1)} collective-permute-done((f32[12,512]{1,0:T(8,128)S(1)}, f32[12,512]{1,0:T(8,128)S(1)}, u32[]{:S(2)}, u32[]{:S(2)}) %collective-permute-start.34) | collective-permute-done | bytes 24608 | tf_op jit(solution)/shard_map/ppermute | solution.py:54
  189.6 0.6 collective-permute-start.35
  190.3 3.3 %collective-permute-done.35 = f32[12,512]{1,0:T(8,128)S(1)} collective-permute-done((f32[12,512]{1,0:T(8,128)S(1)}, f32[12,512]{1,0:T(8,128)S(1)}, u32[]{:S(2)}, u32[]{:S(2)}) %collective-permute-start.35) | collective-permute-done | bytes 24608 | tf_op jit(solution)/shard_map/ppermute | solution.py:54
  193.6 1.3 collective-permute-start.36
  194.9 3.5 %collective-permute-done.36 = f32[12,512]{1,0:T(8,128)S(1)} collective-permute-done((f32[12,512]{1,0:T(8,128)S(1)}, f32[12,512]{1,0:T(8,128)S(1)}, u32[]{:S(2)}, u32[]{:S(2)}) %collective-permute-start.36) | collective-permute-done | bytes 24608 | tf_op jit(solution)/shard_map/ppermute | solution.py:54
  199.0 3.0 %update.1 = (f32[1,1]{1,0:T(1,128)}, f32[4,16,512]{2,1,0:T(8,128)}, f32[4,16,512]{2,1,0:T(8,128)}, f32[4,16,512]{2,1,0:T(8,128)}, f32[2,16,512]{2,1,0:T(8,128)},...) custom-call(s32[1]{0:T(128)} %bitcast.own_ref, ...), custom_call_target="tpu_custom_call" | custom-call | tf_op jit(solution)/shard_map/update/pallas_call | solution.py:671
  (114 shorter events, 6.5 us)
Async XLA Ops:
  3.3 12.9 %collective-permute-start = (bf16[4,16,512]{2,1,0:T(8,128)(2,1)S(1)}, bf16[4,16,512]{2,1,0:T(8,128)(2,1)S(1)}, u32[]{:S(2)}, u32[]{:S(2)}) collective-permute-start(bf16[4,16,512]{2,1,0:T(8,128)(2,1)S(1)} %get-tuple-element.218), channel_id=1, source_target_pairs={{0,8},{1,9},{2,10},{3,11},{4,12},{5,13},{6,14},{7,15},{8,0},{9,1},... | collective-permute-start | bytes 196616 | tf_op jit(solution)/shard_map/ppermute | solution.py:54
  6.5 9.8 %collective-permute-start.1 = (bf16[4,16,512]{2,1,0:T(8,128)(2,1)S(1)}, bf16[4,16,512]{2,1,0:T(8,128)(2,1)S(1)}, u32[]{:S(2)}, u32[]{:S(2)}) collective-permute-start(bf16[4,16,512]{2,1,0:T(8,128)(2,1)S(1)} %get-tuple-element.218), channel_id=1, source_target_pairs={{0,16},{1,17},{2,18},{3,19},{4,20},{5,21},{6,22},{7,23},{8,24},{9,... | collective-permute-start | bytes 196616 | tf_op jit(solution)/shard_map/ppermute | solution.py:54
  9.0 7.2 %collective-permute-start.2 = (bf16[4,16,512]{2,1,0:T(8,128)(2,1)S(1)}, bf16[4,16,512]{2,1,0:T(8,128)(2,1)S(1)}, u32[]{:S(2)}, u32[]{:S(2)}) collective-permute-start(bf16[4,16,512]{2,1,0:T(8,128)(2,1)S(1)} %get-tuple-element.218), channel_id=1, source_target_pairs={{0,24},{1,25},{2,26},{3,27},{4,28},{5,29},{6,30},{7,31},{8,16},{9,... | collective-permute-start | bytes 196616 | tf_op jit(solution)/shard_map/ppermute | solution.py:54
  11.8 9.2 %collective-permute-start.3 = (bf16[11,16,512]{2,1,0:T(8,128)(2,1)S(1)}, bf16[11,16,512]{2,1,0:T(8,128)(2,1)S(1)}, u32[]{:S(2)}, u32[]{:S(2)}) collective-permute-start(bf16[11,16,512]{2,1,0:T(8,128)(2,1)S(1)} %constant_dynamic-update-slice_fusion), channel_id=1, source_target_pairs={{0,8},{1,9},{2,10},{3,11},{4,12},{5,13},{6,14},{7,15},{8,0},{9,1},... | collective-permute-start | bytes 540680 | tf_op jit(solution)/shard_map/ppermute | solution.py:54
  12.7 16.6 %collective-permute-start.4 = (bf16[11,16,512]{2,1,0:T(8,128)(2,1)S(1)}, bf16[11,16,512]{2,1,0:T(8,128)(2,1)S(1)}, u32[]{:S(2)}, u32[]{:S(2)}) collective-permute-start(bf16[11,16,512]{2,1,0:T(8,128)(2,1)S(1)} %constant_dynamic-update-slice_fusion), channel_id=1, source_target_pairs={{0,16},{1,17},{2,18},{3,19},{4,20},{5,21},{6,22},{7,23},{8,24},{9,... | collective-permute-start | bytes 540680 | tf_op jit(solution)/shard_map/ppermute | solution.py:54
  16.2 13.1 %collective-permute-start.5 = (bf16[11,16,512]{2,1,0:T(8,128)(2,1)S(1)}, bf16[11,16,512]{2,1,0:T(8,128)(2,1)S(1)}, u32[]{:S(2)}, u32[]{:S(2)}) collective-permute-start(bf16[11,16,512]{2,1,0:T(8,128)(2,1)S(1)} %constant_dynamic-update-slice_fusion), channel_id=1, source_target_pairs={{0,24},{1,25},{2,26},{3,27},{4,28},{5,29},{6,30},{7,31},{8,16},{9,... | collective-permute-start | bytes 540680 | tf_op jit(solution)/shard_map/ppermute | solution.py:54
  16.3 13.9 %copy-start.3 = (bf16[4,4,16,512]{3,2,1,0:T(8,128)(2,1)}, bf16[4,4,16,512]{3,2,1,0:T(8,128)(2,1)S(1)}, u32[]{:S(2)}) copy-start(bf16[4,4,16,512]{3,2,1,0:T(8,128)(2,1)S(1)} %pad_maximum_fusion.3.refs_0_) | copy-start | bytes 786436
  16.3 13.2 %collective-permute-start.6 = (bf16[4,4,16,512]{3,2,1,0:T(8,128)(2,1)S(1)}, bf16[4,4,16,512]{3,2,1,0:T(8,128)(2,1)S(1)}, u32[]{:S(2)}, u32[]{:S(2)}) collective-permute-start(bf16[4,4,16,512]{3,2,1,0:T(8,128)(2,1)S(1)} %pad_maximum_fusion.3.refs_0_), channel_id=1, source_target_pairs={{0,2},{1,3},{2,0},{3,1},{4,6},{5,7},{6,4},{7,5},{8,10},{9,11},{10,... | collective-permute-start | bytes 786440 | tf_op jit(solution)/shard_map/ppermute | solution.py:54
  18.1 12.0 %collective-permute-start.7 = (bf16[4,4,16,512]{3,2,1,0:T(8,128)(2,1)S(1)}, bf16[4,4,16,512]{3,2,1,0:T(8,128)(2,1)S(1)}, u32[]{:S(2)}, u32[]{:S(2)}) collective-permute-start(bf16[4,4,16,512]{3,2,1,0:T(8,128)(2,1)S(1)} %pad_maximum_fusion.3.refs_0_), channel_id=1, source_target_pairs={{0,4},{1,5},{2,6},{3,7},{4,0},{5,1},{6,2},{7,3},{8,12},{9,13},{10,... | collective-permute-start | bytes 786440 | tf_op jit(solution)/shard_map/ppermute | solution.py:54
  21.0 9.0 %collective-permute-start.8 = (bf16[4,4,16,512]{3,2,1,0:T(8,128)(2,1)S(1)}, bf16[4,4,16,512]{3,2,1,0:T(8,128)(2,1)S(1)}, u32[]{:S(2)}, u32[]{:S(2)}) collective-permute-start(bf16[4,4,16,512]{3,2,1,0:T(8,128)(2,1)S(1)} %pad_maximum_fusion.3.refs_0_), channel_id=1, source_target_pairs={{0,6},{1,7},{2,4},{3,5},{4,2},{5,3},{6,0},{7,1},{8,14},{9,15},{10,... | collective-permute-start | bytes 786440 | tf_op jit(solution)/shard_map/ppermute | solution.py:54
  29.4 1.3 copy-start
  29.5 3.7 %copy-start.8 = (bf16[4,4,16,512]{3,2,1,0:T(8,128)(2,1)}, bf16[4,4,16,512]{3,2,1,0:T(8,128)(2,1)S(1)}, u32[]{:S(2)}) copy-start(bf16[4,4,16,512]{3,2,1,0:T(8,128)(2,1)S(1)} %collective-permute-done.6.refs_1_) | copy-start | bytes 786436
  30.1 3.2 %copy-start.9 = (bf16[4,4,16,512]{3,2,1,0:T(8,128)(2,1)}, bf16[4,4,16,512]{3,2,1,0:T(8,128)(2,1)S(1)}, u32[]{:S(2)}) copy-start(bf16[4,4,16,512]{3,2,1,0:T(8,128)(2,1)S(1)} %collective-permute-done.7.refs_2_) | copy-start | bytes 786436
  30.1 3.2 %copy-start.10 = (bf16[4,4,16,512]{3,2,1,0:T(8,128)(2,1)}, bf16[4,4,16,512]{3,2,1,0:T(8,128)(2,1)S(1)}, u32[]{:S(2)}) copy-start(bf16[4,4,16,512]{3,2,1,0:T(8,128)(2,1)S(1)} %collective-permute-done.8.refs_3_) | copy-start | bytes 786436
  30.2 11.9 %collective-permute-start.9 = (bf16[16,4,16,512]{3,2,1,0:T(8,128)(2,1)S(1)}, bf16[16,4,16,512]{3,2,1,0:T(8,128)(2,1)S(1)}, u32[]{:S(2)}, u32[]{:S(2)}) collective-permute-start(bf16[16,4,16,512]{3,2,1,0:T(8,128)(2,1)S(1)} %pad_maximum_fusion), channel_id=1, source_target_pairs={{0,1},{1,0},{2,3},{3,2},{4,5},{5,4},{6,7},{7,6},{8,9},{9,8},{10,11... | collective-permute-start | bytes 3145736 | tf_op jit(solution)/shard_map/ppermute | solution.py:54
  30.9 14.2 %copy-start.16 = (s32[1024]{0:T(1024)S(1)}, s32[1024]{0:T(1024)}, u32[]{:S(2)}) copy-start(s32[1024]{0:T(1024)} %param.23) | copy-start | bytes 12292
  31.0 15.2 %copy-start.17 = (s32[1024]{0:T(1024)S(1)}, s32[1024]{0:T(1024)}, u32[]{:S(2)}) copy-start(s32[1024]{0:T(1024)} %param.24) | copy-start | bytes 12292
  31.0 11.1 %collective-permute-start.10 = (bf16[4,6,16,512]{3,2,1,0:T(8,128)(2,1)S(1)}, bf16[4,6,16,512]{3,2,1,0:T(8,128)(2,1)S(1)}, u32[]{:S(2)}, u32[]{:S(2)}) collective-permute-start(bf16[4,6,16,512]{3,2,1,0:T(8,128)(2,1)S(1)} %slice.260), channel_id=1, source_target_pairs={{0,2},{1,3},{2,0},{3,1},{4,6},{5,7},{6,4},{7,5},{8,10},{9,11},{10,... | collective-permute-start | bytes 1179656 | tf_op jit(solution)/shard_map/ppermute | solution.py:54
  33.3 8.8 %collective-permute-start.11 = (bf16[4,5,16,512]{3,2,1,0:T(8,128)(2,1)S(1)}, bf16[4,5,16,512]{3,2,1,0:T(8,128)(2,1)S(1)}, u32[]{:S(2)}, u32[]{:S(2)}) collective-permute-start(bf16[4,5,16,512]{3,2,1,0:T(8,128)(2,1)S(1)} %pad_maximum_fusion.2), channel_id=1, source_target_pairs={{0,4},{1,5},{2,6},{3,7},{4,0},{5,1},{6,2},{7,3},{8,12},{9,13},{10,... | collective-permute-start | bytes 983048 | tf_op jit(solution)/shard_map/ppermute | solution.py:54
  42.1 5.1 %copy-start.7 = (bf16[16,4,16,512]{3,2,1,0:T(8,128)(2,1)}, bf16[16,4,16,512]{3,2,1,0:T(8,128)(2,1)S(1)}, u32[]{:S(2)}) copy-start(bf16[16,4,16,512]{3,2,1,0:T(8,128)(2,1)S(1)} %collective-permute-done.9.refs_4_) | copy-start | bytes 3145732
  42.2 22.3 %copy-start.5 = (bf16[8,6,16,512]{3,2,1,0:T(8,128)(2,1)}, bf16[8,6,16,512]{3,2,1,0:T(8,128)(2,1)S(1)}, u32[]{:S(2)}) copy-start(bf16[8,6,16,512]{3,2,1,0:T(8,128)(2,1)S(1)} %constant_dynamic-update-slice_fusion.6.refs_0_) | copy-start | bytes 2359300
  42.2 22.3 %collective-permute-start.12 = (bf16[8,6,16,512]{3,2,1,0:T(8,128)(2,1)S(1)}, bf16[8,6,16,512]{3,2,1,0:T(8,128)(2,1)S(1)}, u32[]{:S(2)}, u32[]{:S(2)}) collective-permute-start(bf16[8,6,16,512]{3,2,1,0:T(8,128)(2,1)S(1)} %constant_dynamic-update-slice_fusion.6.refs_0_), channel_id=1, source_target_pairs={{0,1},{1,0},{2,3},{3,2},{4,5},{5,4},{6,7},{7,6},{8,9},{9,8},{10,11... | collective-permute-start | bytes 2359304 | tf_op jit(solution)/shard_map/ppermute | solution.py:54
  42.3 22.3 %collective-permute-start.14 = (bf16[8,6,16,512]{3,2,1,0:T(8,128)(2,1)S(1)}, bf16[8,6,16,512]{3,2,1,0:T(8,128)(2,1)}, u32[]{:S(2)}, u32[]{:S(2)}) collective-permute-start(bf16[8,6,16,512]{3,2,1,0:T(8,128)(2,1)S(1)} %constant_dynamic-update-slice_fusion.6.refs_0_), channel_id=1, source_target_pairs={{0,4},{1,5},{2,6},{3,7},{4,0},{5,1},{6,2},{7,3},{8,12},{9,13},{10,... | collective-permute-start | bytes 2359304 | tf_op jit(solution)/shard_map/ppermute | solution.py:54
  43.9 20.6 %copy-start.6 = (bf16[8,5,16,512]{3,2,1,0:T(8,128)(2,1)}, bf16[8,5,16,512]{3,2,1,0:T(8,128)(2,1)S(1)}, u32[]{:S(2)}) copy-start(bf16[8,5,16,512]{3,2,1,0:T(8,128)(2,1)S(1)} %constant_dynamic-update-slice_fusion.8.refs_1_) | copy-start | bytes 1966084
  43.9 20.6 %collective-permute-start.13 = (bf16[8,5,16,512]{3,2,1,0:T(8,128)(2,1)S(1)}, bf16[8,5,16,512]{3,2,1,0:T(8,128)(2,1)}, u32[]{:S(2)}, u32[]{:S(2)}) collective-permute-start(bf16[8,5,16,512]{3,2,1,0:T(8,128)(2,1)S(1)} %constant_dynamic-update-slice_fusion.8.refs_1_), channel_id=1, source_target_pairs={{0,1},{1,0},{2,3},{3,2},{4,5},{5,4},{6,7},{7,6},{8,9},{9,8},{10,11... | collective-permute-start | bytes 1966088 | tf_op jit(solution)/shard_map/ppermute | solution.py:54
  44.1 20.4 %collective-permute-start.15 = (bf16[8,5,16,512]{3,2,1,0:T(8,128)(2,1)S(1)}, bf16[8,5,16,512]{3,2,1,0:T(8,128)(2,1)}, u32[]{:S(2)}, u32[]{:S(2)}) collective-permute-start(bf16[8,5,16,512]{3,2,1,0:T(8,128)(2,1)S(1)} %constant_dynamic-update-slice_fusion.8.refs_1_), channel_id=1, source_target_pairs={{0,2},{1,3},{2,0},{3,1},{4,6},{5,7},{6,4},{7,5},{8,10},{9,11},{10,... | collective-permute-start | bytes 1966088 | tf_op jit(solution)/shard_map/ppermute | solution.py:54
  64.5 3.5 %copy-start.11 = (bf16[8,6,16,512]{3,2,1,0:T(8,128)(2,1)}, bf16[8,6,16,512]{3,2,1,0:T(8,128)(2,1)S(1)}, u32[]{:S(2)}) copy-start(bf16[8,6,16,512]{3,2,1,0:T(8,128)(2,1)S(1)} %collective-permute-done.12.refs_4_) | copy-start | bytes 2359300
  64.6 3.5 %collective-permute-start.16 = (bf16[8,6,16,512]{3,2,1,0:T(8,128)(2,1)}, bf16[8,6,16,512]{3,2,1,0:T(8,128)(2,1)S(1)}, u32[]{:S(2)}, u32[]{:S(2)}) collective-permute-start(bf16[8,6,16,512]{3,2,1,0:T(8,128)(2,1)} %collective-permute-done.14.refs_2_), channel_id=1, source_target_pairs={{0,1},{1,0},{2,3},{3,2},{4,5},{5,4},{6,7},{7,6},{8,9},{9,8},{10,11... | collective-permute-start | bytes 2359304 | tf_op jit(solution)/shard_map/ppermute | solution.py:54
  64.7 3.4 %collective-permute-start.17 = (bf16[8,5,16,512]{3,2,1,0:T(8,128)(2,1)}, bf16[8,5,16,512]{3,2,1,0:T(8,128)(2,1)S(1)}, u32[]{:S(2)}, u32[]{:S(2)}) collective-permute-start(bf16[8,5,16,512]{3,2,1,0:T(8,128)(2,1)} %collective-permute-done.15.refs_3_), channel_id=1, source_target_pairs={{0,1},{1,0},{2,3},{3,2},{4,5},{5,4},{6,7},{7,6},{8,9},{9,8},{10,11... | collective-permute-start | bytes 1966088 | tf_op jit(solution)/shard_map/ppermute | solution.py:54
  68.0 0.9 copy-start.15
  68.1 1.2 copy-start.12
  99.9 5.6 %collective-permute-start.18 = (bf16[16,11,16,512]{3,2,1,0:T(8,128)(2,1)}, bf16[16,11,16,512]{3,2,1,0:T(8,128)(2,1)S(1)}, u32[]{:S(2)}, u32[]{:S(2)}) collective-permute-start(bf16[16,11,16,512]{3,2,1,0:T(8,128)(2,1)} %get-tuple-element.135), channel_id=1, source_target_pairs={{0,1},{1,0},{2,3},{3,2},{4,5},{5,4},{6,7},{7,6},{8,9},{9,8},{10,11... | collective-permute-start | bytes 8650760 | tf_op jit(solution)/shard_map/ppermute | solution.py:54
  109.6 33.0 %collective-permute-start.19 = (bf16[4,11,16,512]{3,2,1,0:T(8,128)(2,1)}, bf16[4,11,16,512]{3,2,1,0:T(8,128)(2,1)S(1)}, u32[]{:S(2)}, u32[]{:S(2)}) collective-permute-start(bf16[4,11,16,512]{3,2,1,0:T(8,128)(2,1)} %get-tuple-element.149), channel_id=1, source_target_pairs={{0,2},{1,3},{2,0},{3,1},{4,6},{5,7},{6,4},{7,5},{8,10},{9,11},{10,... | collective-permute-start | bytes 2162696 | tf_op jit(solution)/shard_map/ppermute | solution.py:54
  110.7 33.7 %collective-permute-start.20 = (bf16[4,11,16,512]{3,2,1,0:T(8,128)(2,1)}, bf16[4,11,16,512]{3,2,1,0:T(8,128)(2,1)}, u32[]{:S(2)}, u32[]{:S(2)}) collective-permute-start(bf16[4,11,16,512]{3,2,1,0:T(8,128)(2,1)} %get-tuple-element.150), channel_id=1, source_target_pairs={{0,4},{1,5},{2,6},{3,7},{4,0},{5,1},{6,2},{7,3},{8,12},{9,13},{10,... | collective-permute-start | bytes 2162696 | tf_op jit(solution)/shard_map/ppermute | solution.py:54
  111.2 33.2 %collective-permute-start.21 = (bf16[4,11,16,512]{3,2,1,0:T(8,128)(2,1)}, bf16[4,11,16,512]{3,2,1,0:T(8,128)(2,1)}, u32[]{:S(2)}, u32[]{:S(2)}) collective-permute-start(bf16[4,11,16,512]{3,2,1,0:T(8,128)(2,1)} %get-tuple-element.151), channel_id=1, source_target_pairs={{0,6},{1,7},{2,4},{3,5},{4,2},{5,3},{6,0},{7,1},{8,14},{9,15},{10,... | collective-permute-start | bytes 2162696 | tf_op jit(solution)/shard_map/ppermute | solution.py:54
  113.1 32.5 %copy-start.19 = (f32[1,2048]{1,0:T(1,128)S(1)}, f32[1,2048]{1,0:T(1,128)}, u32[]{:S(2)}) copy-start(f32[1,2048]{1,0:T(1,128)} %get-tuple-element.168) | copy-start | bytes 24580
  142.6 10.6 %copy-start.13 = (bf16[16,3,16,512]{3,2,1,0:T(8,128)(2,1)S(1)}, bf16[16,3,16,512]{3,2,1,0:T(8,128)(2,1)}, u32[]{:S(2)}) copy-start(bf16[16,3,16,512]{3,2,1,0:T(8,128)(2,1)} %get-tuple-element.153) | copy-start | bytes 2359300
  142.6 1.7 copy-start.14
  144.3 8.9 %collective-permute-start.22 = (bf16[16,3,16,512]{3,2,1,0:T(8,128)(2,1)}, bf16[16,3,16,512]{3,2,1,0:T(8,128)(2,1)S(1)}, u32[]{:S(2)}, u32[]{:S(2)}) collective-permute-start(bf16[16,3,16,512]{3,2,1,0:T(8,128)(2,1)} %get-tuple-element.154), channel_id=1, source_target_pairs={{0,1},{1,0},{2,3},{3,2},{4,5},{5,4},{6,7},{7,6},{8,9},{9,8},{10,11... | collective-permute-start | bytes 2359304 | tf_op jit(solution)/shard_map/ppermute | solution.py:54
  146.3 7.3 %copy-start.2 = (f32[1024,512]{1,0:T(8,128)S(1)}, f32[1024,512]{1,0:T(8,128)}, u32[]{:S(2)}) copy-start(f32[1024,512]{1,0:T(8,128)} %get-tuple-element.155) | copy-start | bytes 6291460
  148.2 5.3 %copy-start.1 = (bf16[1024,512]{1,0:T(8,128)(2,1)S(1)}, bf16[1024,512]{1,0:T(8,128)(2,1)}, u32[]{:S(2)}) copy-start(bf16[1024,512]{1,0:T(8,128)(2,1)} %x_ref.3) | copy-start | bytes 3145732
  148.3 11.2 %collective-permute-start.23 = (bf16[11,16,512]{2,1,0:T(8,128)(2,1)S(1)}, bf16[11,16,512]{2,1,0:T(8,128)(2,1)S(1)}, u32[]{:S(2)}, u32[]{:S(2)}) collective-permute-start(bf16[11,16,512]{2,1,0:T(8,128)(2,1)S(1)} %get-tuple-element.209), channel_id=1, source_target_pairs={{0,8},{1,9},{2,10},{3,11},{4,12},{5,13},{6,14},{7,15},{8,0},{9,1},... | collective-permute-start | bytes 540680 | tf_op jit(solution)/shard_map/ppermute | solution.py:54
  150.8 16.1 %collective-permute-start.24 = (bf16[11,16,512]{2,1,0:T(8,128)(2,1)S(1)}, bf16[11,16,512]{2,1,0:T(8,128)(2,1)S(1)}, u32[]{:S(2)}, u32[]{:S(2)}) collective-permute-start(bf16[11,16,512]{2,1,0:T(8,128)(2,1)S(1)} %get-tuple-element.208), channel_id=1, source_target_pairs={{0,16},{1,17},{2,18},{3,19},{4,20},{5,21},{6,22},{7,23},{8,24},{9,... | collective-permute-start | bytes 540680 | tf_op jit(solution)/shard_map/ppermute | solution.py:54
  152.5 14.4 %collective-permute-start.25 = (bf16[11,16,512]{2,1,0:T(8,128)(2,1)S(1)}, bf16[11,16,512]{2,1,0:T(8,128)(2,1)S(1)}, u32[]{:S(2)}, u32[]{:S(2)}) collective-permute-start(bf16[11,16,512]{2,1,0:T(8,128)(2,1)S(1)} %get-tuple-element.207), channel_id=1, source_target_pairs={{0,24},{1,25},{2,26},{3,27},{4,28},{5,29},{6,30},{7,31},{8,16},{9,... | collective-permute-start | bytes 540680 | tf_op jit(solution)/shard_map/ppermute | solution.py:54
  153.6 7.1 %copy-start.4 = (f32[1024,512]{1,0:T(8,128)S(1)}, f32[1024,512]{1,0:T(8,128)}, u32[]{:S(2)}) copy-start(f32[1024,512]{1,0:T(8,128)} %get-tuple-element.130) | copy-start | bytes 6291460
  154.8 12.1 %collective-permute-start.26 = (bf16[4,3,16,512]{3,2,1,0:T(8,128)(2,1)S(1)}, bf16[4,3,16,512]{3,2,1,0:T(8,128)(2,1)S(1)}, u32[]{:S(2)}, u32[]{:S(2)}) collective-permute-start(bf16[4,3,16,512]{3,2,1,0:T(8,128)(2,1)S(1)} %get-tuple-element.161), channel_id=1, source_target_pairs={{0,2},{1,3},{2,0},{3,1},{4,6},{5,7},{6,4},{7,5},{8,10},{9,11},{10,... | collective-permute-start | bytes 589832 | tf_op jit(solution)/shard_map/ppermute | solution.py:54
  156.0 11.0 %collective-permute-start.27 = (bf16[4,3,16,512]{3,2,1,0:T(8,128)(2,1)S(1)}, bf16[4,3,16,512]{3,2,1,0:T(8,128)(2,1)S(1)}, u32[]{:S(2)}, u32[]{:S(2)}) collective-permute-start(bf16[4,3,16,512]{3,2,1,0:T(8,128)(2,1)S(1)} %get-tuple-element.162), channel_id=1, source_target_pairs={{0,4},{1,5},{2,6},{3,7},{4,0},{5,1},{6,2},{7,3},{8,12},{9,13},{10,... | collective-permute-start | bytes 589832 | tf_op jit(solution)/shard_map/ppermute | solution.py:54
  159.4 7.6 %collective-permute-start.28 = (bf16[4,3,16,512]{3,2,1,0:T(8,128)(2,1)S(1)}, bf16[4,3,16,512]{3,2,1,0:T(8,128)(2,1)S(1)}, u32[]{:S(2)}, u32[]{:S(2)}) collective-permute-start(bf16[4,3,16,512]{3,2,1,0:T(8,128)(2,1)S(1)} %get-tuple-element.163), channel_id=1, source_target_pairs={{0,6},{1,7},{2,4},{3,5},{4,2},{5,3},{6,0},{7,1},{8,14},{9,15},{10,... | collective-permute-start | bytes 589832 | tf_op jit(solution)/shard_map/ppermute | solution.py:54
  162.3 18.0 %copy-start.18 = (f32[8,512]{1,0:T(8,128)S(1)}, f32[8,512]{1,0:T(8,128)}, u32[]{:S(2)}) copy-start(f32[8,512]{1,0:T(8,128)} %get-tuple-element.167) | copy-start | bytes 49156
  167.1 8.6 %collective-permute-start.29 = (bf16[3,16,512]{2,1,0:T(8,128)(2,1)S(1)}, bf16[3,16,512]{2,1,0:T(8,128)(2,1)S(1)}, u32[]{:S(2)}, u32[]{:S(2)}) collective-permute-start(bf16[3,16,512]{2,1,0:T(8,128)(2,1)S(1)} %get-tuple-element.214), channel_id=1, source_target_pairs={{0,8},{1,9},{2,10},{3,11},{4,12},{5,13},{6,14},{7,15},{8,0},{9,1},... | collective-permute-start | bytes 147464 | tf_op jit(solution)/shard_map/ppermute | solution.py:54
  170.8 6.0 %collective-permute-start.30 = (bf16[3,16,512]{2,1,0:T(8,128)(2,1)S(1)}, bf16[3,16,512]{2,1,0:T(8,128)(2,1)S(1)}, u32[]{:S(2)}, u32[]{:S(2)}) collective-permute-start(bf16[3,16,512]{2,1,0:T(8,128)(2,1)S(1)} %get-tuple-element.216), channel_id=1, source_target_pairs={{0,16},{1,17},{2,18},{3,19},{4,20},{5,21},{6,22},{7,23},{8,24},{9,... | collective-permute-start | bytes 147464 | tf_op jit(solution)/shard_map/ppermute | solution.py:54
  171.8 6.0 %collective-permute-start.31 = (bf16[3,16,512]{2,1,0:T(8,128)(2,1)S(1)}, bf16[3,16,512]{2,1,0:T(8,128)(2,1)S(1)}, u32[]{:S(2)}, u32[]{:S(2)}) collective-permute-start(bf16[3,16,512]{2,1,0:T(8,128)(2,1)S(1)} %get-tuple-element.215), channel_id=1, source_target_pairs={{0,24},{1,25},{2,26},{3,27},{4,28},{5,29},{6,30},{7,31},{8,16},{9,... | collective-permute-start | bytes 147464 | tf_op jit(solution)/shard_map/ppermute | solution.py:54
  180.5 1.3 collective-permute-start.32
  181.8 3.9 %collective-permute-start.33 = (f32[12,512]{1,0:T(8,128)S(1)}, f32[12,512]{1,0:T(8,128)S(1)}, u32[]{:S(2)}, u32[]{:S(2)}) collective-permute-start(f32[12,512]{1,0:T(8,128)S(1)} %add.253), channel_id=1, source_target_pairs={{0,2},{1,3},{2,0},{3,1},{4,6},{5,7},{6,4},{7,5},{8,10},{9,11},{10,... | collective-permute-start | bytes 73736 | tf_op jit(solution)/shard_map/ppermute | solution.py:54
  185.7 3.9 %collective-permute-start.34 = (f32[12,512]{1,0:T(8,128)S(1)}, f32[12,512]{1,0:T(8,128)S(1)}, u32[]{:S(2)}, u32[]{:S(2)}) collective-permute-start(f32[12,512]{1,0:T(8,128)S(1)} %add.254), channel_id=1, source_target_pairs={{0,4},{1,5},{2,6},{3,7},{4,0},{5,1},{6,2},{7,3},{8,12},{9,13},{10,... | collective-permute-start | bytes 73736 | tf_op jit(solution)/shard_map/ppermute | solution.py:54
  189.6 3.9 %collective-permute-start.35 = (f32[12,512]{1,0:T(8,128)S(1)}, f32[12,512]{1,0:T(8,128)S(1)}, u32[]{:S(2)}, u32[]{:S(2)}) collective-permute-start(f32[12,512]{1,0:T(8,128)S(1)} %add.255), channel_id=1, source_target_pairs={{0,8},{1,9},{2,10},{3,11},{4,12},{5,13},{6,14},{7,15},{8,0},{9,1},... | collective-permute-start | bytes 73736 | tf_op jit(solution)/shard_map/ppermute | solution.py:54
  193.6 4.8 %collective-permute-start.36 = (f32[12,512]{1,0:T(8,128)S(1)}, f32[12,512]{1,0:T(8,128)S(1)}, u32[]{:S(2)}, u32[]{:S(2)}) collective-permute-start(f32[12,512]{1,0:T(8,128)S(1)} %add.256), channel_id=1, source_target_pairs={{0,16},{1,17},{2,18},{3,19},{4,20},{5,21},{6,22},{7,23},{8,24},{9,... | collective-permute-start | bytes 73736 | tf_op jit(solution)/shard_map/ppermute | solution.py:54

commit v4 on v3

--- a/solution.py
+++ b/solution.py
@@ -170,7 +170,7 @@
     first_bit, bits = stage_bits(groups)[2]
     total = lambda z: own_part[z] + sum(part[z].astype(jnp.float32) for part in arrived)
     return total(0), [
-        swap_with(total(z).astype(jnp.bfloat16), z << first_bit, count) for z in range(1, 2**bits)
+        swap_with(total(z).astype(jnp.bfloat16), z << first_bit, count) for z in range(2**bits - 1, 0, -1)
     ]
 
 
@@ -179,8 +179,12 @@
 
 
 def sum_all(value, groups):
-    for bit in range(sum(groups)):
-        value = value + swap_with(value, 1 << bit, 2 ** sum(groups))
+    count = 2 ** sum(groups)
+    for first_bit, bits in stage_bits(groups):
+        values = [value] + [swap_with(value, offset << first_bit, count) for offset in range(1, 2**bits)]
+        while len(values) > 1:
+            values = [one + two for one, two in zip(values[::2], values[1::2])]
+        value = values[0]
     return value
 
 
@@ -209,20 +213,22 @@
 def mat(a,b,dims):
     return lax.dot_general(a,b,(dims,((),())),preferred_element_type=jnp.float32)
 
-def fill_bias(bias_ref, seg_col, pos_col, seg_row, pos_row):
-    rows=bias_ref.shape[0]
-    step=min(BLOCK,rows)
-    for first in range(0,rows,step):
-        sc=seg_col[first:first+step,:]; pc=pos_col[first:first+step,:]
-        sr=seg_row[:,first:]; pr=pos_row[:,first:]
-        allowed=(sc==sr)&(pc<=pr)
-        bias_ref[first:first+step,first:]=jnp.where(allowed,0.0,masked_score)
+def fill_bias(bias_ref, seg_row, pos_row):
+    rows = bias_ref.shape[0]
+    step = min(BLOCK, rows)
+    for first in range(0, rows, step):
+        seg_keys, pos_keys = [
+            jnp.broadcast_to(ref[:, first : first + step], (8, step)).T[:, 0:1] for ref in (seg_row, pos_row)
+        ]
+        allowed = (seg_keys == seg_row[:, first:]) & (pos_keys <= pos_row[:, first:])
+        bias_ref[first : first + step, first:] = jnp.where(allowed, 0.0, masked_score)
+
 
 def head_lanes(shape, which):
     lane=lax.broadcasted_iota(jnp.int32,shape,1)
     return (lane//HEAD)==which
 
-def attn_fwd_kernel(direct, tables, layout, own_ref, segc, posc, segr, posr, x_ref, *refs):
+def attn_fwd_kernel(direct, tables, layout, own_ref, segr, posr, x_ref, *refs):
     part_count = len(tables) if direct else 2
     parts = refs[:part_count]
     h_ref, q_ref, k_ref, v_ref, o_ref, lse_ref, *rest = refs[part_count:]
@@ -240,7 +246,7 @@
     def _():
         if direct:
             copy_parts(tables, layout, own_ref[0], parts, [weights, vectors])
-        fill_bias(bias_ref, segc, posc, segr, posr)
+        fill_bias(bias_ref, segr, posr)
         for first in range(0, rows, step):
             x = x_ref[first : first + step, :].astype(jnp.float32)
             h_ref[first : first + step, :] = low(normalize_parts(x, vectors[0:1, :], vectors[1:2, :])[0])
@@ -271,14 +277,14 @@
 
 
 def attn_bwd_kernel(
-    offsets, own_ref, segc, posc, segr, posr, q_ref, k_ref, v_ref, do_ref, lse_ref, h_ref, w_ref, start_ref, *refs
+    offsets, own_ref, segr, posr, q_ref, k_ref, v_ref, do_ref, lse_ref, h_ref, w_ref, start_ref, *refs
 ):
     *outs, dh_ref, bias_ref, dk_acc, dv_acc, ht_ref, dw_ref = refs
     rows = q_ref.shape[0]
 
     @pl.when(pl.program_id(0) == 0)
     def _():
-        fill_bias(bias_ref, segc, posc, segr, posr)
+        fill_bias(bias_ref, segr, posr)
         ht_ref[...] = h_ref[...].T
         dh_ref[...] = start_ref[...]
 
@@ -334,9 +340,6 @@
 
 def const_map(*_): return (0,0)
 
-def seg_args(segments,positions):
-    return (segments[:,None],positions[:,None],segments[None],positions[None])
-
 def attend(own, tokens, marks, parts, tables, layout, groups):
     rows, width = tokens.shape
     count = 2 ** sum(groups)
@@ -362,7 +365,7 @@
     result = pl.pallas_call(
         functools.partial(attn_fwd_kernel, direct, tables, layout),
         grid=(pairs,),
-        in_specs=[smem_spec(), whole((rows, 1)), whole((rows, 1)), whole((1, rows)), whole((1, rows))]
+        in_specs=[smem_spec(), whole((1, rows)), whole((1, rows))]
         + [whole((rows, width))]
         + [whole(part.shape) for part in parts],
         out_specs=out_specs,
@@ -382,7 +385,6 @@
     inputs = w_qkv.shape[1]
     step = inputs // count
     blk = pl.BlockSpec((rows, lanes), lambda j: (0, j))
-    col = pl.BlockSpec((rows, 1), const_map)
     row = pl.BlockSpec((1, rows), const_map)
     offsets = None
     if step % 16 == 0:
@@ -398,7 +400,7 @@
     *grads, dh = pl.pallas_call(
         functools.partial(attn_bwd_kernel, offsets),
         grid=(width // lanes,),
-        in_specs=[smem_spec(), col, col, row, row, blk, blk, blk, blk]
+        in_specs=[smem_spec(), row, row, blk, blk, blk, blk]
         + [
             pl.BlockSpec((1, 2, rows), lambda j: (j, 0, 0)),
             pl.BlockSpec((rows, inputs), const_map),
@@ -463,13 +465,13 @@
                     target[entry, first + piece] = block
 
 
-def ffn_kernel(direct, part_count, tables, offsets, layout, own_ref, x_ref, cot_ref, h_ref, o_ref, vec_ref, bias_ref, *refs):
+def ffn_kernel(direct, part_count, tables, offsets, layout, own_ref, x_ref, cot_ref, h_ref, o_ref, vec_ref, *refs):
     low = lambda value: value.astype(jnp.bfloat16)
     parts = refs[:part_count]
-    out_count = 6 + (2 if direct else 5)
+    out_count = 5 + (2 if direct else 5)
     outs = refs[part_count : part_count + out_count]
     scratch = refs[part_count + out_count :]
-    y_ref, do_ref, dh_ref, dx_ref, dvec_ref, dbias_ref = outs[:6]
+    y_ref, do_ref, dh_ref, dx_ref, dvec_ref = outs[:5]
     r_ref, dz_ref, h2_ref, df_ref, dzf_ref, da_ref, dza_ref = scratch[:7]
     tile = pl.program_id(0)
     if direct:
@@ -480,7 +482,7 @@
             copy_parts(tables, layout, own_ref[0], parts, weights)
 
     else:
-        weights, targets = parts, outs[6:]
+        weights, targets = parts, outs[5:]
     width = x_ref.shape[1]
     size = x_ref.shape[0]
     chunks = r_ref.shape[0]
@@ -490,7 +492,6 @@
     @pl.when(tile == 0)
     def _():
         dvec_ref[...] = jnp.zeros_like(dvec_ref)
-        dbias_ref[...] = jnp.zeros_like(dbias_ref)
 
     forward = ((1,), (0,))
     backward = ((1,), (1,))
@@ -501,7 +502,8 @@
     gain = vec_ref[2:3, :]
     h2_full, n2, s2 = normalize_parts(x1, gain, vec_ref[3:4, :])
     h2 = low(h2_full)
-    z = mat(h2, load(3), forward) + bias_ref[...]
+    bias = jnp.concatenate([vec_ref[7 + chunk : 8 + chunk, :] for chunk in range(chunks)], 1)
+    z = mat(h2, load(3), forward) + bias
     r = low(jnp.maximum(z, 0.0))
     f = mat(r, load(4), forward) + vec_ref[6:7, :]
     gf = jax.nn.sigmoid(mat(h2, load(2), forward) + vec_ref[5:6, :])
@@ -523,12 +525,11 @@
     do_ref[...] = low(mat(da, load(0), backward))
     dh_ref[...] = mat(dzab, load(1), backward)
     total = lambda value: jnp.sum(value, 0, keepdims=True)
-    dvec_ref[0:1, :] += total(dh2 * n2)
-    dvec_ref[1:2, :] += total(dh2)
-    dvec_ref[2:3, :] += total(dza)
-    dvec_ref[3:4, :] += total(dzf)
-    dvec_ref[4:5, :] += total(df)
-    dbias_ref[...] += total(dz)
+    sums = [total(dh2 * n2), total(dh2), total(dza), total(dzf), total(df)]
+    hidden_sums = total(dz)
+    sums += [hidden_sums[:, chunk * width : (chunk + 1) * width] for chunk in range(chunks)]
+    for index, value in enumerate(sums):
+        dvec_ref[2 + index : 3 + index, :] += value
     for chunk in range(chunks):
         r_ref[chunk, rows, :] = r[:, chunk * width : (chunk + 1) * width]
         dz_ref[chunk, rows, :] = dzb[:, chunk * width : (chunk + 1) * width]
@@ -559,17 +560,16 @@
                 targets[3][:, lanes] = grad_in
                 targets[4][lanes, :] = grad_out
         if direct:
-            copy_blocks(offsets, layout, own_ref[0], targets, *outs[6:])
+            copy_blocks(offsets, layout, own_ref[0], targets, *outs[5:])
 
 
 FFN_LAYOUT = [("stack", 0, 1), ("stack", 1, 1), ("stack", 2, 1), ("columns", 3, 4), ("rows", 7, 4)]
 
 
-def ffn(own, tokens, cotangent, normed, mixed_heads, vectors, bias, parts, tables, groups):
+def ffn(own, tokens, cotangent, normed, mixed_heads, vectors, hidden, parts, tables, groups):
     rows, width = tokens.shape
     count = 2 ** sum(groups)
     step = parts[0].shape[2]
-    hidden = bias.shape[0]
     chunks = hidden // width
     tile = min(256, rows)
     direct = step % 16 == 0
@@ -591,22 +591,22 @@
         grads = [jax.ShapeDtypeStruct(shape, low) for shape in matrices]
     full = jax.ShapeDtypeStruct((rows, width), jnp.float32)
     half = jax.ShapeDtypeStruct((rows, width), low)
-    small = [jax.ShapeDtypeStruct((8, width), jnp.float32), jax.ShapeDtypeStruct((1, hidden), jnp.float32)]
+    small = [jax.ShapeDtypeStruct((12, width), jnp.float32)]
     result = pl.pallas_call(
         functools.partial(ffn_kernel, direct, len(parts), tables, offsets, FFN_LAYOUT),
         grid=(rows // tile,),
         in_specs=[smem_spec(), block, block, whole((rows, width)), whole((rows, width))]
-        + [whole(vectors.shape), whole((1, hidden))]
+        + [whole(vectors.shape)]
         + [whole(part.shape) for part in parts],
         out_specs=[block] * 4 + [whole(item.shape) for item in small + grads],
         out_shape=[half, half, full, full] + small + grads,
         scratch_shapes=scratch,
         name="ffn",
-    )(own[None].astype(jnp.int32), tokens, cotangent, normed, mixed_heads, vectors, bias[None], *parts)
+    )(own[None].astype(jnp.int32), tokens, cotangent, normed, mixed_heads, vectors, *parts)
     if not direct:
-        blocks = [grad.reshape(1, count, step, width) for grad in result[6:9]]
-        blocks += [result[9].reshape(count, step, hidden), result[10].reshape(count, chunks, step, width)]
-        result = list(result[:6]) + list(split(own, blocks, FFN_LAYOUT, groups))
+        blocks = [grad.reshape(1, count, step, width) for grad in result[5:8]]
+        blocks += [result[8].reshape(count, step, hidden), result[9].reshape(count, chunks, step, width)]
+        result = list(result[:5]) + list(split(own, blocks, FFN_LAYOUT, groups))
     return result
 
 
@@ -734,9 +734,9 @@
     inputs = tokens.astype(jnp.float32)
     mean_one = jnp.mean(inputs, -1, keepdims=True)
     scale_one = lax.rsqrt(jnp.mean((inputs - mean_one) * (inputs - mean_one), -1, keepdims=True) + norm_eps)
-    marks = seg_args(segments, positions)
+    marks = (segments[None], positions[None])
     core_first, mean_one, scale_one, *tied = tie(core_first, mean_one, scale_one, *marks, *received)
-    marks, received = tied[:4], tied[4:]
+    marks, received = tied[:2], tied[2:]
     last = len(orders[0]) - 1
     for position in range(last):
         tables = [
@@ -757,20 +757,19 @@
         groups,
     )
     w_qkv = w_qkv.reshape(3, count * step, width)
-    bias = vectors[7:11].reshape(-1)
     core_near = [swap_with(half, 1, count) for half in halves]
-    mixed_heads, *tied = tie(mixed_heads, *core_near, *received)
+    mixed_heads, gain_one, *tied = tie(mixed_heads, vectors[0], *core_near, *received)
     core_near, received = tied[:2], tied[2:]
     core_far = [swap_with(half, 1, count) for half in received]
     unit_one = (inputs - mean_one) * scale_one
-    layer_out, grad_mixed, grad_normed, grad_inputs, sums, grad_bias, kept_b, sent_b = ffn(
+    layer_out, grad_mixed, grad_normed, grad_inputs, sums, kept_b, sent_b = ffn(
         own,
         tokens,
         cotangent,
         normed,
         mixed_heads,
         vectors,
-        bias,
+        in_weight.shape[1],
         list(halves) + list(received) + list(core_near) + core_far,
         [
             ([offset | core for offset in table], first)
@@ -795,26 +794,19 @@
     grad_normed, own_a, *parts_a = tie(grad_normed, own_a, *parts_a)
     grad_gain_one = jnp.sum(grad_normed * unit_one, 0)
     grad_shift_one = jnp.sum(grad_normed, 0)
-    grad_inputs = grad_inputs + normalize_back(grad_normed, unit_one, scale_one, vectors[0])
+    grad_inputs = grad_inputs + normalize_back(grad_normed, unit_one, scale_one, gain_one)
     input_grad = low(grad_inputs)
     plane_a = plane_send(parts_a, groups)
-    input_grad, grad_gain_one, grad_shift_one, *arrived = tie(
-        input_grad, grad_gain_one, grad_shift_one, *z_b, *plane_a
-    )
-    z_b, plane_a = arrived[: len(z_b)], arrived[len(z_b) :]
+    input_grad, grad_gain_one, grad_shift_one, *plane_a = tie(
+        input_grad, grad_gain_one, grad_shift_one, *plane_a
+    )
     own_a, z_a = reduce_z(own_a, plane_a, groups)
     total_b = reduce_end(own_b, z_b)
     total_a = reduce_end(own_a, z_a)
     local_squares = jnp.sum(total_b * total_b) + jnp.sum(total_a * total_a)
-    payload = jnp.concatenate(
-        [
-            grad_gain_one[None],
-            grad_shift_one[None],
-            sums[:5],
-            grad_bias.reshape(4, width),
-            jnp.full((1, width), local_squares),
-        ]
-    )
+    line = lax.broadcasted_iota(jnp.int32, sums.shape, 0)
+    payload = jnp.where(line == 0, grad_gain_one, jnp.where(line == 1, grad_shift_one, sums))
+    payload = jnp.where(line == 11, local_squares, payload)
     payload = sum_all(payload, groups)
     states = (
         (attn_weight, attn_m, attn_v),

time: 203 us -> 195 us (0.961)
  waiting for transfers between devices: 47.2 us -> 42.9 us
  local copies, waits for them, and re-layouts: 8.21 us -> 4.04 us
  starting transfers between devices: 44.2 us -> 46.9 us
    ppermute x37 -> x39, waiting for transfers between devices: 47.2 us -> 42.9 us  [swap_with(): lax.ppermute(array, AXES, [(source, source ^ offset) for source in range(...]
    ppermute x37 -> x39, starting transfers between devices: 44.2 us -> 46.9 us  [swap_with(): lax.ppermute(array, AXES, [(source, source ^ offset) for source in range(...]
    optimization_barrier x2 -> x0, local copies, waits for them, and re-layouts: 2.08 us -> none  [tie(): return lax.optimization_barrier(values)]
  transfers between devices with their start and end apart: 37 -> 39, of which waited for: 17 -> 16; matrix products, arithmetic and copies ran while one was open for 8% -> 6% of each run, Pallas kernels for 23% -> 24%
where the time goes in v4:
time: 195 us
  Pallas kernels  80.1 us (41%)
  starting transfers between devices  46.9 us (24%)
  waiting for transfers between devices  42.9 us (22%)
  other arithmetic  18.3 us (9%)
  local copies, waits for them, and re-layouts  4.04 us (2%)
  between operations  2.62 us (1%)
    ppermute x39, starting transfers between devices, swap_with(): lax.ppermute(array, AXES, [(source, source ^ offset) for source in range(...  46.9 us
    ppermute x39, waiting for transfers between devices, swap_with(): lax.ppermute(array, AXES, [(source, source ^ offset) for source in range(...  42.9 us
    pallas_call x1, Pallas kernels, ffn(): pl.pallas_call(functools.partial(ffn_kernel, direct, len(parts), tables,...  30.7 us
    pallas_call x1, Pallas kernels, attend_back(): pl.pallas_call(functools.partial(attn_bwd_kernel, offsets), grid=(width /...  29.5 us
    pallas_call x1, Pallas kernels, attend(): pl.pallas_call(functools.partial(attn_fwd_kernel, direct, tables, layout)...  17 us
    convert_element_type x2, other arithmetic, plane_sums(): total(offset).astype(jnp.bfloat16)  4.42 us
  transfers between devices with their start and end apart: 39, of which 16 were waited for; matrix products, arithmetic and copies ran while one was open for 6% of the time, Pallas kernels for 24%

profile of v4, /device:TPU:0, one launch (start us, length us, event | category | flops | bytes accessed | tf_op | source)
XLA Modules:
  0.0 195.0 jit_solution(345975191872430485)
XLA Ops:
  0.7 0.9 convert.28
  1.6 0.7 tile.8
  2.4 0.7 tile.19
  3.3 3.1 %collective-permute-start = (bf16[4,16,512]{2,1,0:T(8,128)(2,1)S(1)}, bf16[4,16,512]{2,1,0:T(8,128)(2,1)S(1)}, u32[]{:S(2)}, u32[]{:S(2)}) collective-permute-start(bf16[4,16,512]{2,1,0:T(8,128)(2,1)S(1)} %get-tuple-element.208), channel_id=1, source_target_pairs={{0,8},{1,9},{2,10},{3,11},{4,12},{5,13},{6,14},{7,15},{8,0},{9,1},... | collective-permute-start | bytes 196616 | tf_op jit(solution)/shard_map/ppermute | solution.py:54
  6.5 2.6 %collective-permute-start.1 = (bf16[4,16,512]{2,1,0:T(8,128)(2,1)S(1)}, bf16[4,16,512]{2,1,0:T(8,128)(2,1)S(1)}, u32[]{:S(2)}, u32[]{:S(2)}) collective-permute-start(bf16[4,16,512]{2,1,0:T(8,128)(2,1)S(1)} %get-tuple-element.208), channel_id=1, source_target_pairs={{0,16},{1,17},{2,18},{3,19},{4,20},{5,21},{6,22},{7,23},{8,24},{9,... | collective-permute-start | bytes 196616 | tf_op jit(solution)/shard_map/ppermute | solution.py:54
  9.0 0.9 convert_element_type.207
  10.0 0.8 convert_dynamic-update-slice_fusion
  10.8 0.9 convert_element_type.208
  11.8 1.0 collective-permute-start.3
  12.7 3.5 %collective-permute-start.4 = (bf16[11,16,512]{2,1,0:T(8,128)(2,1)S(1)}, bf16[11,16,512]{2,1,0:T(8,128)(2,1)S(1)}, u32[]{:S(2)}, u32[]{:S(2)}) collective-permute-start(bf16[11,16,512]{2,1,0:T(8,128)(2,1)S(1)} %constant_dynamic-update-slice_fusion), channel_id=1, source_target_pairs={{0,16},{1,17},{2,18},{3,19},{4,20},{5,21},{6,22},{7,23},{8,24},{9,... | collective-permute-start | bytes 540680 | tf_op jit(solution)/shard_map/ppermute | solution.py:54
  16.3 1.8 collective-permute-start.6
  18.1 1.5 collective-permute-start.7
  19.6 1.4 collective-permute-done.3
  21.0 2.4 %collective-permute-start.8 = (bf16[4,4,16,512]{3,2,1,0:T(8,128)(2,1)S(1)}, bf16[4,4,16,512]{3,2,1,0:T(8,128)(2,1)S(1)}, u32[]{:S(2)}, u32[]{:S(2)}) collective-permute-start(bf16[4,4,16,512]{3,2,1,0:T(8,128)(2,1)S(1)} %pad_maximum_fusion.3.refs_0_), channel_id=1, source_target_pairs={{0,6},{1,7},{2,4},{3,5},{4,2},{5,3},{6,0},{7,1},{8,14},{9,15},{10,... | collective-permute-start | bytes 786440 | tf_op jit(solution)/shard_map/ppermute | solution.py:54
  23.5 5.8 %collective-permute-done.4 = bf16[11,16,512]{2,1,0:T(8,128)(2,1)S(1)} collective-permute-done((bf16[11,16,512]{2,1,0:T(8,128)(2,1)S(1)}, bf16[11,16,512]{2,1,0:T(8,128)(2,1)S(1)}, u32[]{:S(2)}, u32[]{:S(2)}) %collective-permute-start.4) | collective-permute-done | bytes 180256 | tf_op jit(solution)/shard_map/ppermute | solution.py:54
  29.5 0.5 collective-permute-done.7.refs_2_
  30.3 0.4 copy-done
  31.0 1.7 collective-permute-start.10
  32.7 0.5 fusion.1
  33.3 1.6 collective-permute-start.11
  34.9 7.2 %collective-permute-done.11 = bf16[4,5,16,512]{3,2,1,0:T(8,128)(2,1)S(1)} collective-permute-done((bf16[4,5,16,512]{3,2,1,0:T(8,128)(2,1)S(1)}, bf16[4,5,16,512]{3,2,1,0:T(8,128)(2,1)S(1)}, u32[]{:S(2)}, u32[]{:S(2)}) %collective-permute-start.11) | collective-permute-done | bytes 327712 | tf_op jit(solution)/shard_map/ppermute | solution.py:54
  42.2 1.6 collective-permute-start.14
  44.1 1.0 collective-permute-start.15
  45.1 17.0 %attn_fwd.1 = (bf16[1024,512]{1,0:T(8,128)(2,1)}, bf16[1024,512]{1,0:T(8,128)(2,1)}, bf16[1024,512]{1,0:T(8,128)(2,1)}, bf16[1024,512]{1,0:T(8,128)(2,1)}, bf16[...) custom-call(s32[1]{0:T(128)} %bitcast.own_ref, ...), custom_call_target="tpu_custom_call" | custom-call | tf_op jit(solution)/shard_map/attn_fwd/pallas_call | solution.py:365
  62.1 0.7 slice.197
  63.0 0.4 collective-permute-start.17
  63.5 2.9 %collective-permute-done.17.refs_7_ = bf16[8,5,16,512]{3,2,1,0:T(8,128)(2,1)S(1)} collective-permute-done((bf16[8,5,16,512]{3,2,1,0:T(8,128)(2,1)}, bf16[8,5,16,512]{3,2,1,0:T(8,128)(2,1)S(1)}, u32[]{:S(2)}, u32[]{:S(2)}) %collective-permute-start.17) | collective-permute-done | bytes 655392 | tf_op jit(solution)/shard_map/ppermute | solution.py:54
  66.4 0.8 copy-done.14
  67.5 30.7 %ffn.1 = (bf16[1024,512]{1,0:T(8,128)(2,1)}, bf16[1024,512]{1,0:T(8,128)(2,1)}, f32[1024,512]{1,0:T(8,128)}, f32[1024,512]{1,0:T(8,128)}, f32[12,512]{1,0:T(8,12...) custom-call(s32[1]{0:T(128)} %bitcast.own_ref, bf16[1024,512]{1,0:T(8,128)(2,1)} %x_ref.3, ...), custom_call_target="tpu_custom_call" | custom-call | tf_op jit(solution)/shard_map/ffn/pallas_call | solution.py:595
  98.4 5.4 %collective-permute-done.18 = bf16[16,11,16,512]{3,2,1,0:T(8,128)(2,1)S(1)} collective-permute-done((bf16[16,11,16,512]{3,2,1,0:T(8,128)(2,1)}, bf16[16,11,16,512]{3,2,1,0:T(8,128)(2,1)S(1)}, u32[]{:S(2)}, u32[]{:S(2)}) %collective-permute-start.18) | collective-permute-done | bytes 2883616 | tf_op jit(solution)/shard_map/ppermute | solution.py:54
  103.8 4.1 %add_convert_fusion = (bf16[4,11,16,512]{3,2,1,0:T(8,128)(2,1)}, bf16[4,11,16,512]{3,2,1,0:T(8,128)(2,1)}, bf16[4,11,16,512]{3,2,1,0:T(8,128)(2,1)}, f32[4,11,16,512]{3,2,1,0:T(8,128)S(1)}) fusion(bf16[16,11,16,512]{3,2,1,0:T(8,128)(2,1)S(1)} %collective-permute-done.18, bf16[16,11,16,512]{3,2,1,0:T(8,128)(2,1)} %get-tuple-element.132), kind=kLoop, calls=%fused_computation.16 | loop fusion | flops 5406720 | bytes 9371648 | tf_op jit(solution)/shard_map/convert_element_type | solution.py:160
  107.9 1.0 collective-permute-start.19
  108.9 0.8 collective-permute-start.20
  109.7 1.7 collective-permute-start.21
  111.4 29.5 %attn_bwd.1 = (bf16[16,3,16,512]{3,2,1,0:T(8,128)(2,1)}, bf16[16,3,16,512]{3,2,1,0:T(8,128)(2,1)}, f32[1024,512]{1,0:T(8,128)}) custom-call(s32[1]{0:T(128)} %bitcast.own_ref, s32[1,1024]{1,0:T(1,128)} %bitcast.78, s32[1,1024]{1,0:T(1,128)} %bitcast.80, bf16[1024,512]{1,0:T(8,128)(2,1)} %get-tuple-element.125.q_ref, ...), custom_call_target="tpu_custom_call" | custom-call | tf_op jit(solution)/shard_map/attn_bwd/pallas_call | solution.py:400
  140.9 1.6 collective-permute-done.20
  142.5 1.6 fusion.12
  144.2 3.7 %collective-permute-start.26 = (bf16[11,16,512]{2,1,0:T(8,128)(2,1)S(1)}, bf16[11,16,512]{2,1,0:T(8,128)(2,1)S(1)}, u32[]{:S(2)}, u32[]{:S(2)}) collective-permute-start(bf16[11,16,512]{2,1,0:T(8,128)(2,1)S(1)} %get-tuple-element.197), channel_id=1, source_target_pairs={{0,24},{1,25},{2,26},{3,27},{4,28},{5,29},{6,30},{7,31},{8,16},{9,... | collective-permute-start | bytes 540680 | tf_op jit(solution)/shard_map/ppermute | solution.py:54
  148.5 1.2 fusion.11
  149.8 1.1 collective-permute-start.23
  150.9 0.9 collective-permute-start.24
  151.8 1.6 collective-permute-start.25
  153.3 1.7 fusion.10
  155.0 2.6 %collective-permute-done.23 = bf16[4,3,16,512]{3,2,1,0:T(8,128)(2,1)S(1)} collective-permute-done((bf16[4,3,16,512]{3,2,1,0:T(8,128)(2,1)S(1)}, bf16[4,3,16,512]{3,2,1,0:T(8,128)(2,1)S(1)}, u32[]{:S(2)}, u32[]{:S(2)}) %collective-permute-start.23) | collective-permute-done | bytes 196640 | tf_op jit(solution)/shard_map/ppermute | solution.py:54
  157.6 0.4 collective-permute-start.28
  158.0 3.5 %collective-permute-done.24 = bf16[4,3,16,512]{3,2,1,0:T(8,128)(2,1)S(1)} collective-permute-done((bf16[4,3,16,512]{3,2,1,0:T(8,128)(2,1)S(1)}, bf16[4,3,16,512]{3,2,1,0:T(8,128)(2,1)S(1)}, u32[]{:S(2)}, u32[]{:S(2)}) %collective-permute-start.24) | collective-permute-done | bytes 196640 | tf_op jit(solution)/shard_map/ppermute | solution.py:54
  161.7 2.5 %collective-permute-start.29 = (bf16[3,16,512]{2,1,0:T(8,128)(2,1)S(1)}, bf16[3,16,512]{2,1,0:T(8,128)(2,1)S(1)}, u32[]{:S(2)}, u32[]{:S(2)}) collective-permute-start(bf16[3,16,512]{2,1,0:T(8,128)(2,1)S(1)} %get-tuple-element.204), channel_id=1, source_target_pairs={{0,24},{1,25},{2,26},{3,27},{4,28},{5,29},{6,30},{7,31},{8,16},{9,... | collective-permute-start | bytes 147464 | tf_op jit(solution)/shard_map/ppermute | solution.py:54
  164.3 1.8 collective-permute-start.31
  166.1 2.6 %collective-permute-done.28 = bf16[11,16,512]{2,1,0:T(8,128)(2,1)S(1)} collective-permute-done((bf16[11,16,512]{2,1,0:T(8,128)(2,1)S(1)}, bf16[11,16,512]{2,1,0:T(8,128)(2,1)S(1)}, u32[]{:S(2)}, u32[]{:S(2)}) %collective-permute-start.28) | collective-permute-done | bytes 180256 | tf_op jit(solution)/shard_map/ppermute | solution.py:54
  168.7 2.4 %multiply_reduce_fusion.1 = (f32[]{:T(128)}, f32[11,16,512]{2,1,0:T(8,128)}) fusion(bf16[11,16,512]{2,1,0:T(8,128)(2,1)S(1)} %collective-permute-done.28, bf16[11,16,512]{2,1,0:T(8,128)(2,1)S(1)} %collective-permute-done.27, bf16[11,16,512]{2,1,0:T(8,128)(2,1)S(1)} %collective-permute-done.26, bf16[4,11,16,512]{3,2,1,0:T(8,128)(2,1)} %collective-permute-done.21, ...), kind=kLoop, calls=%fused_computation.27 | loop fusion | flops 1261567 | bytes 1802244 | tf_op jit(solution)/shard_map/reduce_sum | solution.py:806
  171.1 1.3 multiply_reduce_fusion.2
  173.8 1.2 collective-permute-done.32
  175.1 1.0 collective-permute-start.33
  176.1 0.9 collective-permute-start.34
  177.1 1.6 collective-permute-start.35
  178.6 0.4 collective-permute-done.33
  179.1 1.0 collective-permute-done.34
  180.0 1.8 collective-permute-done.35
  182.0 3.5 %collective-permute-start.37 = (f32[12,512]{1,0:T(8,128)S(1)}, f32[12,512]{1,0:T(8,128)S(1)}, u32[]{:S(2)}, u32[]{:S(2)}) collective-permute-start(f32[12,512]{1,0:T(8,128)S(1)} %add_add_fusion.1), channel_id=1, source_target_pairs={{0,16},{1,17},{2,18},{3,19},{4,20},{5,21},{6,22},{7,23},{8,24},{9,... | collective-permute-start | bytes 73736 | tf_op jit(solution)/shard_map/ppermute | solution.py:54
  185.5 0.9 collective-permute-start.38
  186.4 1.0 collective-permute-done.37
  187.4 3.8 %collective-permute-done.38 = f32[12,512]{1,0:T(8,128)S(1)} collective-permute-done((f32[12,512]{1,0:T(8,128)S(1)}, f32[12,512]{1,0:T(8,128)S(1)}, u32[]{:S(2)}, u32[]{:S(2)}) %collective-permute-start.38) | collective-permute-done | bytes 24608 | tf_op jit(solution)/shard_map/ppermute | solution.py:54
  191.2 0.6 add_add_fusion.payload_ref
  191.8 3.0 %update.1 = (f32[1,1]{1,0:T(1,128)}, f32[4,16,512]{2,1,0:T(8,128)}, f32[4,16,512]{2,1,0:T(8,128)}, f32[4,16,512]{2,1,0:T(8,128)}, f32[2,16,512]{2,1,0:T(8,128)},...) custom-call(s32[1]{0:T(128)} %bitcast.own_ref, ...), custom_call_target="tpu_custom_call" | custom-call | tf_op jit(solution)/shard_map/update/pallas_call | solution.py:671
  (102 shorter events, 3.3 us)
Async XLA Ops:
  3.3 12.9 %collective-permute-start = (bf16[4,16,512]{2,1,0:T(8,128)(2,1)S(1)}, bf16[4,16,512]{2,1,0:T(8,128)(2,1)S(1)}, u32[]{:S(2)}, u32[]{:S(2)}) collective-permute-start(bf16[4,16,512]{2,1,0:T(8,128)(2,1)S(1)} %get-tuple-element.208), channel_id=1, source_target_pairs={{0,8},{1,9},{2,10},{3,11},{4,12},{5,13},{6,14},{7,15},{8,0},{9,1},... | collective-permute-start | bytes 196616 | tf_op jit(solution)/shard_map/ppermute | solution.py:54
  6.5 9.8 %collective-permute-start.1 = (bf16[4,16,512]{2,1,0:T(8,128)(2,1)S(1)}, bf16[4,16,512]{2,1,0:T(8,128)(2,1)S(1)}, u32[]{:S(2)}, u32[]{:S(2)}) collective-permute-start(bf16[4,16,512]{2,1,0:T(8,128)(2,1)S(1)} %get-tuple-element.208), channel_id=1, source_target_pairs={{0,16},{1,17},{2,18},{3,19},{4,20},{5,21},{6,22},{7,23},{8,24},{9,... | collective-permute-start | bytes 196616 | tf_op jit(solution)/shard_map/ppermute | solution.py:54
  9.0 7.2 %collective-permute-start.2 = (bf16[4,16,512]{2,1,0:T(8,128)(2,1)S(1)}, bf16[4,16,512]{2,1,0:T(8,128)(2,1)S(1)}, u32[]{:S(2)}, u32[]{:S(2)}) collective-permute-start(bf16[4,16,512]{2,1,0:T(8,128)(2,1)S(1)} %get-tuple-element.208), channel_id=1, source_target_pairs={{0,24},{1,25},{2,26},{3,27},{4,28},{5,29},{6,30},{7,31},{8,16},{9,... | collective-permute-start | bytes 196616 | tf_op jit(solution)/shard_map/ppermute | solution.py:54
  11.8 9.2 %collective-permute-start.3 = (bf16[11,16,512]{2,1,0:T(8,128)(2,1)S(1)}, bf16[11,16,512]{2,1,0:T(8,128)(2,1)S(1)}, u32[]{:S(2)}, u32[]{:S(2)}) collective-permute-start(bf16[11,16,512]{2,1,0:T(8,128)(2,1)S(1)} %constant_dynamic-update-slice_fusion), channel_id=1, source_target_pairs={{0,8},{1,9},{2,10},{3,11},{4,12},{5,13},{6,14},{7,15},{8,0},{9,1},... | collective-permute-start | bytes 540680 | tf_op jit(solution)/shard_map/ppermute | solution.py:54
  12.7 16.6 %collective-permute-start.4 = (bf16[11,16,512]{2,1,0:T(8,128)(2,1)S(1)}, bf16[11,16,512]{2,1,0:T(8,128)(2,1)S(1)}, u32[]{:S(2)}, u32[]{:S(2)}) collective-permute-start(bf16[11,16,512]{2,1,0:T(8,128)(2,1)S(1)} %constant_dynamic-update-slice_fusion), channel_id=1, source_target_pairs={{0,16},{1,17},{2,18},{3,19},{4,20},{5,21},{6,22},{7,23},{8,24},{9,... | collective-permute-start | bytes 540680 | tf_op jit(solution)/shard_map/ppermute | solution.py:54
  16.2 13.1 %collective-permute-start.5 = (bf16[11,16,512]{2,1,0:T(8,128)(2,1)S(1)}, bf16[11,16,512]{2,1,0:T(8,128)(2,1)S(1)}, u32[]{:S(2)}, u32[]{:S(2)}) collective-permute-start(bf16[11,16,512]{2,1,0:T(8,128)(2,1)S(1)} %constant_dynamic-update-slice_fusion), channel_id=1, source_target_pairs={{0,24},{1,25},{2,26},{3,27},{4,28},{5,29},{6,30},{7,31},{8,16},{9,... | collective-permute-start | bytes 540680 | tf_op jit(solution)/shard_map/ppermute | solution.py:54
  16.3 13.9 %copy-start.3 = (bf16[4,4,16,512]{3,2,1,0:T(8,128)(2,1)}, bf16[4,4,16,512]{3,2,1,0:T(8,128)(2,1)S(1)}, u32[]{:S(2)}) copy-start(bf16[4,4,16,512]{3,2,1,0:T(8,128)(2,1)S(1)} %pad_maximum_fusion.3.refs_0_) | copy-start | bytes 786436
  16.3 13.2 %collective-permute-start.6 = (bf16[4,4,16,512]{3,2,1,0:T(8,128)(2,1)S(1)}, bf16[4,4,16,512]{3,2,1,0:T(8,128)(2,1)S(1)}, u32[]{:S(2)}, u32[]{:S(2)}) collective-permute-start(bf16[4,4,16,512]{3,2,1,0:T(8,128)(2,1)S(1)} %pad_maximum_fusion.3.refs_0_), channel_id=1, source_target_pairs={{0,2},{1,3},{2,0},{3,1},{4,6},{5,7},{6,4},{7,5},{8,10},{9,11},{10,... | collective-permute-start | bytes 786440 | tf_op jit(solution)/shard_map/ppermute | solution.py:54
  18.1 12.0 %collective-permute-start.7 = (bf16[4,4,16,512]{3,2,1,0:T(8,128)(2,1)S(1)}, bf16[4,4,16,512]{3,2,1,0:T(8,128)(2,1)S(1)}, u32[]{:S(2)}, u32[]{:S(2)}) collective-permute-start(bf16[4,4,16,512]{3,2,1,0:T(8,128)(2,1)S(1)} %pad_maximum_fusion.3.refs_0_), channel_id=1, source_target_pairs={{0,4},{1,5},{2,6},{3,7},{4,0},{5,1},{6,2},{7,3},{8,12},{9,13},{10,... | collective-permute-start | bytes 786440 | tf_op jit(solution)/shard_map/ppermute | solution.py:54
  21.0 9.0 %collective-permute-start.8 = (bf16[4,4,16,512]{3,2,1,0:T(8,128)(2,1)S(1)}, bf16[4,4,16,512]{3,2,1,0:T(8,128)(2,1)S(1)}, u32[]{:S(2)}, u32[]{:S(2)}) collective-permute-start(bf16[4,4,16,512]{3,2,1,0:T(8,128)(2,1)S(1)} %pad_maximum_fusion.3.refs_0_), channel_id=1, source_target_pairs={{0,6},{1,7},{2,4},{3,5},{4,2},{5,3},{6,0},{7,1},{8,14},{9,15},{10,... | collective-permute-start | bytes 786440 | tf_op jit(solution)/shard_map/ppermute | solution.py:54
  29.4 1.3 copy-start
  29.5 3.7 %copy-start.8 = (bf16[4,4,16,512]{3,2,1,0:T(8,128)(2,1)}, bf16[4,4,16,512]{3,2,1,0:T(8,128)(2,1)S(1)}, u32[]{:S(2)}) copy-start(bf16[4,4,16,512]{3,2,1,0:T(8,128)(2,1)S(1)} %collective-permute-done.6.refs_1_) | copy-start | bytes 786436
  30.1 3.2 %copy-start.9 = (bf16[4,4,16,512]{3,2,1,0:T(8,128)(2,1)}, bf16[4,4,16,512]{3,2,1,0:T(8,128)(2,1)S(1)}, u32[]{:S(2)}) copy-start(bf16[4,4,16,512]{3,2,1,0:T(8,128)(2,1)S(1)} %collective-permute-done.7.refs_2_) | copy-start | bytes 786436
  30.1 3.2 %copy-start.10 = (bf16[4,4,16,512]{3,2,1,0:T(8,128)(2,1)}, bf16[4,4,16,512]{3,2,1,0:T(8,128)(2,1)S(1)}, u32[]{:S(2)}) copy-start(bf16[4,4,16,512]{3,2,1,0:T(8,128)(2,1)S(1)} %collective-permute-done.8.refs_3_) | copy-start | bytes 786436
  30.2 11.9 %collective-permute-start.9 = (bf16[16,4,16,512]{3,2,1,0:T(8,128)(2,1)S(1)}, bf16[16,4,16,512]{3,2,1,0:T(8,128)(2,1)S(1)}, u32[]{:S(2)}, u32[]{:S(2)}) collective-permute-start(bf16[16,4,16,512]{3,2,1,0:T(8,128)(2,1)S(1)} %pad_maximum_fusion), channel_id=1, source_target_pairs={{0,1},{1,0},{2,3},{3,2},{4,5},{5,4},{6,7},{7,6},{8,9},{9,8},{10,11... | collective-permute-start | bytes 3145736 | tf_op jit(solution)/shard_map/ppermute | solution.py:54
  31.0 11.1 %collective-permute-start.10 = (bf16[4,6,16,512]{3,2,1,0:T(8,128)(2,1)S(1)}, bf16[4,6,16,512]{3,2,1,0:T(8,128)(2,1)S(1)}, u32[]{:S(2)}, u32[]{:S(2)}) collective-permute-start(bf16[4,6,16,512]{3,2,1,0:T(8,128)(2,1)S(1)} %slice.252), channel_id=1, source_target_pairs={{0,2},{1,3},{2,0},{3,1},{4,6},{5,7},{6,4},{7,5},{8,10},{9,11},{10,... | collective-permute-start | bytes 1179656 | tf_op jit(solution)/shard_map/ppermute | solution.py:54
  33.3 8.8 %collective-permute-start.11 = (bf16[4,5,16,512]{3,2,1,0:T(8,128)(2,1)S(1)}, bf16[4,5,16,512]{3,2,1,0:T(8,128)(2,1)S(1)}, u32[]{:S(2)}, u32[]{:S(2)}) collective-permute-start(bf16[4,5,16,512]{3,2,1,0:T(8,128)(2,1)S(1)} %pad_maximum_fusion.2), channel_id=1, source_target_pairs={{0,4},{1,5},{2,6},{3,7},{4,0},{5,1},{6,2},{7,3},{8,12},{9,13},{10,... | collective-permute-start | bytes 983048 | tf_op jit(solution)/shard_map/ppermute | solution.py:54
  42.1 3.0 %copy-start.7 = (bf16[16,4,16,512]{3,2,1,0:T(8,128)(2,1)}, bf16[16,4,16,512]{3,2,1,0:T(8,128)(2,1)S(1)}, u32[]{:S(2)}) copy-start(bf16[16,4,16,512]{3,2,1,0:T(8,128)(2,1)S(1)} %collective-permute-done.9.refs_4_) | copy-start | bytes 3145732
  42.1 20.0 %copy-start.5 = (bf16[8,6,16,512]{3,2,1,0:T(8,128)(2,1)}, bf16[8,6,16,512]{3,2,1,0:T(8,128)(2,1)S(1)}, u32[]{:S(2)}) copy-start(bf16[8,6,16,512]{3,2,1,0:T(8,128)(2,1)S(1)} %constant_dynamic-update-slice_fusion.6.refs_0_) | copy-start | bytes 2359300
  42.2 20.7 %collective-permute-start.12 = (bf16[8,6,16,512]{3,2,1,0:T(8,128)(2,1)S(1)}, bf16[8,6,16,512]{3,2,1,0:T(8,128)(2,1)S(1)}, u32[]{:S(2)}, u32[]{:S(2)}) collective-permute-start(bf16[8,6,16,512]{3,2,1,0:T(8,128)(2,1)S(1)} %constant_dynamic-update-slice_fusion.6.refs_0_), channel_id=1, source_target_pairs={{0,1},{1,0},{2,3},{3,2},{4,5},{5,4},{6,7},{7,6},{8,9},{9,8},{10,11... | collective-permute-start | bytes 2359304 | tf_op jit(solution)/shard_map/ppermute | solution.py:54
  42.2 20.7 %collective-permute-start.14 = (bf16[8,6,16,512]{3,2,1,0:T(8,128)(2,1)S(1)}, bf16[8,6,16,512]{3,2,1,0:T(8,128)(2,1)}, u32[]{:S(2)}, u32[]{:S(2)}) collective-permute-start(bf16[8,6,16,512]{3,2,1,0:T(8,128)(2,1)S(1)} %constant_dynamic-update-slice_fusion.6.refs_0_), channel_id=1, source_target_pairs={{0,4},{1,5},{2,6},{3,7},{4,0},{5,1},{6,2},{7,3},{8,12},{9,13},{10,... | collective-permute-start | bytes 2359304 | tf_op jit(solution)/shard_map/ppermute | solution.py:54
  43.9 22.5 %copy-start.6 = (bf16[8,5,16,512]{3,2,1,0:T(8,128)(2,1)}, bf16[8,5,16,512]{3,2,1,0:T(8,128)(2,1)S(1)}, u32[]{:S(2)}) copy-start(bf16[8,5,16,512]{3,2,1,0:T(8,128)(2,1)S(1)} %constant_dynamic-update-slice_fusion.8.refs_1_) | copy-start | bytes 1966084
  43.9 19.0 %collective-permute-start.13 = (bf16[8,5,16,512]{3,2,1,0:T(8,128)(2,1)S(1)}, bf16[8,5,16,512]{3,2,1,0:T(8,128)(2,1)}, u32[]{:S(2)}, u32[]{:S(2)}) collective-permute-start(bf16[8,5,16,512]{3,2,1,0:T(8,128)(2,1)S(1)} %constant_dynamic-update-slice_fusion.8.refs_1_), channel_id=1, source_target_pairs={{0,1},{1,0},{2,3},{3,2},{4,5},{5,4},{6,7},{7,6},{8,9},{9,8},{10,11... | collective-permute-start | bytes 1966088 | tf_op jit(solution)/shard_map/ppermute | solution.py:54
  44.1 18.8 %collective-permute-start.15 = (bf16[8,5,16,512]{3,2,1,0:T(8,128)(2,1)S(1)}, bf16[8,5,16,512]{3,2,1,0:T(8,128)(2,1)}, u32[]{:S(2)}, u32[]{:S(2)}) collective-permute-start(bf16[8,5,16,512]{3,2,1,0:T(8,128)(2,1)S(1)} %constant_dynamic-update-slice_fusion.8.refs_1_), channel_id=1, source_target_pairs={{0,2},{1,3},{2,0},{3,1},{4,6},{5,7},{6,4},{7,5},{8,10},{9,11},{10,... | collective-permute-start | bytes 1966088 | tf_op jit(solution)/shard_map/ppermute | solution.py:54
  62.9 3.5 %copy-start.11 = (bf16[8,6,16,512]{3,2,1,0:T(8,128)(2,1)}, bf16[8,6,16,512]{3,2,1,0:T(8,128)(2,1)S(1)}, u32[]{:S(2)}) copy-start(bf16[8,6,16,512]{3,2,1,0:T(8,128)(2,1)S(1)} %collective-permute-done.12.refs_4_) | copy-start | bytes 2359300
  62.9 3.5 %collective-permute-start.16 = (bf16[8,6,16,512]{3,2,1,0:T(8,128)(2,1)}, bf16[8,6,16,512]{3,2,1,0:T(8,128)(2,1)S(1)}, u32[]{:S(2)}, u32[]{:S(2)}) collective-permute-start(bf16[8,6,16,512]{3,2,1,0:T(8,128)(2,1)} %collective-permute-done.14.refs_2_), channel_id=1, source_target_pairs={{0,1},{1,0},{2,3},{3,2},{4,5},{5,4},{6,7},{7,6},{8,9},{9,8},{10,11... | collective-permute-start | bytes 2359304 | tf_op jit(solution)/shard_map/ppermute | solution.py:54
  63.0 3.4 %collective-permute-start.17 = (bf16[8,5,16,512]{3,2,1,0:T(8,128)(2,1)}, bf16[8,5,16,512]{3,2,1,0:T(8,128)(2,1)S(1)}, u32[]{:S(2)}, u32[]{:S(2)}) collective-permute-start(bf16[8,5,16,512]{3,2,1,0:T(8,128)(2,1)} %collective-permute-done.15.refs_3_), channel_id=1, source_target_pairs={{0,1},{1,0},{2,3},{3,2},{4,5},{5,4},{6,7},{7,6},{8,9},{9,8},{10,11... | collective-permute-start | bytes 1966088 | tf_op jit(solution)/shard_map/ppermute | solution.py:54
  66.4 0.8 copy-start.14
  66.4 1.1 copy-start.12
  98.2 5.6 %collective-permute-start.18 = (bf16[16,11,16,512]{3,2,1,0:T(8,128)(2,1)}, bf16[16,11,16,512]{3,2,1,0:T(8,128)(2,1)S(1)}, u32[]{:S(2)}, u32[]{:S(2)}) collective-permute-start(bf16[16,11,16,512]{3,2,1,0:T(8,128)(2,1)} %get-tuple-element.128), channel_id=1, source_target_pairs={{0,1},{1,0},{2,3},{3,2},{4,5},{5,4},{6,7},{7,6},{8,9},{9,8},{10,11... | collective-permute-start | bytes 8650760 | tf_op jit(solution)/shard_map/ppermute | solution.py:54
  107.9 33.0 %collective-permute-start.19 = (bf16[4,11,16,512]{3,2,1,0:T(8,128)(2,1)}, bf16[4,11,16,512]{3,2,1,0:T(8,128)(2,1)S(1)}, u32[]{:S(2)}, u32[]{:S(2)}) collective-permute-start(bf16[4,11,16,512]{3,2,1,0:T(8,128)(2,1)} %get-tuple-element.142), channel_id=1, source_target_pairs={{0,2},{1,3},{2,0},{3,1},{4,6},{5,7},{6,4},{7,5},{8,10},{9,11},{10,... | collective-permute-start | bytes 2162696 | tf_op jit(solution)/shard_map/ppermute | solution.py:54
  108.9 33.6 %collective-permute-start.20 = (bf16[4,11,16,512]{3,2,1,0:T(8,128)(2,1)}, bf16[4,11,16,512]{3,2,1,0:T(8,128)(2,1)S(1)}, u32[]{:S(2)}, u32[]{:S(2)}) collective-permute-start(bf16[4,11,16,512]{3,2,1,0:T(8,128)(2,1)} %get-tuple-element.143), channel_id=1, source_target_pairs={{0,4},{1,5},{2,6},{3,7},{4,0},{5,1},{6,2},{7,3},{8,12},{9,13},{10,... | collective-permute-start | bytes 2162696 | tf_op jit(solution)/shard_map/ppermute | solution.py:54
  109.7 32.7 %collective-permute-start.21 = (bf16[4,11,16,512]{3,2,1,0:T(8,128)(2,1)}, bf16[4,11,16,512]{3,2,1,0:T(8,128)(2,1)}, u32[]{:S(2)}, u32[]{:S(2)}) collective-permute-start(bf16[4,11,16,512]{3,2,1,0:T(8,128)(2,1)} %get-tuple-element.144), channel_id=1, source_target_pairs={{0,6},{1,7},{2,4},{3,5},{4,2},{5,3},{6,0},{7,1},{8,14},{9,15},{10,... | collective-permute-start | bytes 2162696 | tf_op jit(solution)/shard_map/ppermute | solution.py:54
  140.9 7.3 %copy-start.13 = (bf16[16,3,16,512]{3,2,1,0:T(8,128)(2,1)S(1)}, bf16[16,3,16,512]{3,2,1,0:T(8,128)(2,1)}, u32[]{:S(2)}) copy-start(bf16[16,3,16,512]{3,2,1,0:T(8,128)(2,1)} %get-tuple-element.146) | copy-start | bytes 2359300
  142.5 5.7 %collective-permute-start.22 = (bf16[16,3,16,512]{3,2,1,0:T(8,128)(2,1)}, bf16[16,3,16,512]{3,2,1,0:T(8,128)(2,1)S(1)}, u32[]{:S(2)}, u32[]{:S(2)}) collective-permute-start(bf16[16,3,16,512]{3,2,1,0:T(8,128)(2,1)} %get-tuple-element.147), channel_id=1, source_target_pairs={{0,1},{1,0},{2,3},{3,2},{4,5},{5,4},{6,7},{7,6},{8,9},{9,8},{10,11... | collective-permute-start | bytes 2359304 | tf_op jit(solution)/shard_map/ppermute | solution.py:54
  142.5 6.0 %copy-start.1 = (bf16[1024,512]{1,0:T(8,128)(2,1)S(1)}, bf16[1024,512]{1,0:T(8,128)(2,1)}, u32[]{:S(2)}) copy-start(bf16[1024,512]{1,0:T(8,128)(2,1)} %x_ref.3) | copy-start | bytes 3145732
  142.5 6.0 %copy-start.2 = (f32[1024,512]{1,0:T(8,128)S(1)}, f32[1024,512]{1,0:T(8,128)}, u32[]{:S(2)}) copy-start(f32[1024,512]{1,0:T(8,128)} %get-tuple-element.148) | copy-start | bytes 6291460
  144.2 20.2 %collective-permute-start.26 = (bf16[11,16,512]{2,1,0:T(8,128)(2,1)S(1)}, bf16[11,16,512]{2,1,0:T(8,128)(2,1)S(1)}, u32[]{:S(2)}, u32[]{:S(2)}) collective-permute-start(bf16[11,16,512]{2,1,0:T(8,128)(2,1)S(1)} %get-tuple-element.197), channel_id=1, source_target_pairs={{0,24},{1,25},{2,26},{3,27},{4,28},{5,29},{6,30},{7,31},{8,16},{9,... | collective-permute-start | bytes 540680 | tf_op jit(solution)/shard_map/ppermute | solution.py:54
  147.8 18.3 %collective-permute-start.27 = (bf16[11,16,512]{2,1,0:T(8,128)(2,1)S(1)}, bf16[11,16,512]{2,1,0:T(8,128)(2,1)S(1)}, u32[]{:S(2)}, u32[]{:S(2)}) collective-permute-start(bf16[11,16,512]{2,1,0:T(8,128)(2,1)S(1)} %get-tuple-element.199), channel_id=1, source_target_pairs={{0,16},{1,17},{2,18},{3,19},{4,20},{5,21},{6,22},{7,23},{8,24},{9,... | collective-permute-start | bytes 540680 | tf_op jit(solution)/shard_map/ppermute | solution.py:54
  148.5 4.8 %copy-start.4 = (f32[1024,512]{1,0:T(8,128)S(1)}, f32[1024,512]{1,0:T(8,128)}, u32[]{:S(2)}) copy-start(f32[1024,512]{1,0:T(8,128)} %get-tuple-element.123) | copy-start | bytes 6291460
  149.8 7.8 %collective-permute-start.23 = (bf16[4,3,16,512]{3,2,1,0:T(8,128)(2,1)S(1)}, bf16[4,3,16,512]{3,2,1,0:T(8,128)(2,1)S(1)}, u32[]{:S(2)}, u32[]{:S(2)}) collective-permute-start(bf16[4,3,16,512]{3,2,1,0:T(8,128)(2,1)S(1)} %get-tuple-element.151), channel_id=1, source_target_pairs={{0,2},{1,3},{2,0},{3,1},{4,6},{5,7},{6,4},{7,5},{8,10},{9,11},{10,... | collective-permute-start | bytes 589832 | tf_op jit(solution)/shard_map/ppermute | solution.py:54
  150.9 10.7 %collective-permute-start.24 = (bf16[4,3,16,512]{3,2,1,0:T(8,128)(2,1)S(1)}, bf16[4,3,16,512]{3,2,1,0:T(8,128)(2,1)S(1)}, u32[]{:S(2)}, u32[]{:S(2)}) collective-permute-start(bf16[4,3,16,512]{3,2,1,0:T(8,128)(2,1)S(1)} %get-tuple-element.152), channel_id=1, source_target_pairs={{0,4},{1,5},{2,6},{3,7},{4,0},{5,1},{6,2},{7,3},{8,12},{9,13},{10,... | collective-permute-start | bytes 589832 | tf_op jit(solution)/shard_map/ppermute | solution.py:54
  151.8 9.8 %collective-permute-start.25 = (bf16[4,3,16,512]{3,2,1,0:T(8,128)(2,1)S(1)}, bf16[4,3,16,512]{3,2,1,0:T(8,128)(2,1)S(1)}, u32[]{:S(2)}, u32[]{:S(2)}) collective-permute-start(bf16[4,3,16,512]{3,2,1,0:T(8,128)(2,1)S(1)} %get-tuple-element.153), channel_id=1, source_target_pairs={{0,6},{1,7},{2,4},{3,5},{4,2},{5,3},{6,0},{7,1},{8,14},{9,15},{10,... | collective-permute-start | bytes 589832 | tf_op jit(solution)/shard_map/ppermute | solution.py:54
  155.0 18.7 %copy-start.15 = (f32[12,512]{1,0:T(8,128)S(1)}, f32[12,512]{1,0:T(8,128)}, u32[]{:S(2)}) copy-start(f32[12,512]{1,0:T(8,128)} %get-tuple-element.165) | copy-start | bytes 73732
  157.6 11.1 %collective-permute-start.28 = (bf16[11,16,512]{2,1,0:T(8,128)(2,1)S(1)}, bf16[11,16,512]{2,1,0:T(8,128)(2,1)S(1)}, u32[]{:S(2)}, u32[]{:S(2)}) collective-permute-start(bf16[11,16,512]{2,1,0:T(8,128)(2,1)S(1)} %get-tuple-element.198), channel_id=1, source_target_pairs={{0,8},{1,9},{2,10},{3,11},{4,12},{5,13},{6,14},{7,15},{8,0},{9,1},... | collective-permute-start | bytes 540680 | tf_op jit(solution)/shard_map/ppermute | solution.py:54
  161.7 9.5 %collective-permute-start.29 = (bf16[3,16,512]{2,1,0:T(8,128)(2,1)S(1)}, bf16[3,16,512]{2,1,0:T(8,128)(2,1)S(1)}, u32[]{:S(2)}, u32[]{:S(2)}) collective-permute-start(bf16[3,16,512]{2,1,0:T(8,128)(2,1)S(1)} %get-tuple-element.204), channel_id=1, source_target_pairs={{0,24},{1,25},{2,26},{3,27},{4,28},{5,29},{6,30},{7,31},{8,16},{9,... | collective-permute-start | bytes 147464 | tf_op jit(solution)/shard_map/ppermute | solution.py:54
  164.2 6.9 %collective-permute-start.30 = (bf16[3,16,512]{2,1,0:T(8,128)(2,1)S(1)}, bf16[3,16,512]{2,1,0:T(8,128)(2,1)S(1)}, u32[]{:S(2)}, u32[]{:S(2)}) collective-permute-start(bf16[3,16,512]{2,1,0:T(8,128)(2,1)S(1)} %get-tuple-element.206), channel_id=1, source_target_pairs={{0,16},{1,17},{2,18},{3,19},{4,20},{5,21},{6,22},{7,23},{8,24},{9,... | collective-permute-start | bytes 147464 | tf_op jit(solution)/shard_map/ppermute | solution.py:54
  164.3 6.8 %collective-permute-start.31 = (bf16[3,16,512]{2,1,0:T(8,128)(2,1)S(1)}, bf16[3,16,512]{2,1,0:T(8,128)(2,1)S(1)}, u32[]{:S(2)}, u32[]{:S(2)}) collective-permute-start(bf16[3,16,512]{2,1,0:T(8,128)(2,1)S(1)} %get-tuple-element.205), channel_id=1, source_target_pairs={{0,8},{1,9},{2,10},{3,11},{4,12},{5,13},{6,14},{7,15},{8,0},{9,1},... | collective-permute-start | bytes 147464 | tf_op jit(solution)/shard_map/ppermute | solution.py:54
  173.8 1.2 collective-permute-start.32
  175.1 4.0 %collective-permute-start.33 = (f32[12,512]{1,0:T(8,128)S(1)}, f32[12,512]{1,0:T(8,128)S(1)}, u32[]{:S(2)}, u32[]{:S(2)}) collective-permute-start(f32[12,512]{1,0:T(8,128)S(1)} %fusion.30), channel_id=1, source_target_pairs={{0,2},{1,3},{2,0},{3,1},{4,6},{5,7},{6,4},{7,5},{8,10},{9,11},{10,... | collective-permute-start | bytes 73736 | tf_op jit(solution)/shard_map/ppermute | solution.py:54
  176.1 3.9 %collective-permute-start.34 = (f32[12,512]{1,0:T(8,128)S(1)}, f32[12,512]{1,0:T(8,128)S(1)}, u32[]{:S(2)}, u32[]{:S(2)}) collective-permute-start(f32[12,512]{1,0:T(8,128)S(1)} %fusion.30), channel_id=1, source_target_pairs={{0,4},{1,5},{2,6},{3,7},{4,0},{5,1},{6,2},{7,3},{8,12},{9,13},{10,... | collective-permute-start | bytes 73736 | tf_op jit(solution)/shard_map/ppermute | solution.py:54
  177.1 4.8 %collective-permute-start.35 = (f32[12,512]{1,0:T(8,128)S(1)}, f32[12,512]{1,0:T(8,128)S(1)}, u32[]{:S(2)}, u32[]{:S(2)}) collective-permute-start(f32[12,512]{1,0:T(8,128)S(1)} %fusion.30), channel_id=1, source_target_pairs={{0,6},{1,7},{2,4},{3,5},{4,2},{5,3},{6,0},{7,1},{8,14},{9,15},{10,... | collective-permute-start | bytes 73736 | tf_op jit(solution)/shard_map/ppermute | solution.py:54
  181.9 4.5 %collective-permute-start.36 = (f32[12,512]{1,0:T(8,128)S(1)}, f32[12,512]{1,0:T(8,128)S(1)}, u32[]{:S(2)}, u32[]{:S(2)}) collective-permute-start(f32[12,512]{1,0:T(8,128)S(1)} %add_add_fusion.1), channel_id=1, source_target_pairs={{0,8},{1,9},{2,10},{3,11},{4,12},{5,13},{6,14},{7,15},{8,0},{9,1},... | collective-permute-start | bytes 73736 | tf_op jit(solution)/shard_map/ppermute | solution.py:54
  182.0 5.4 %collective-permute-start.37 = (f32[12,512]{1,0:T(8,128)S(1)}, f32[12,512]{1,0:T(8,128)S(1)}, u32[]{:S(2)}, u32[]{:S(2)}) collective-permute-start(f32[12,512]{1,0:T(8,128)S(1)} %add_add_fusion.1), channel_id=1, source_target_pairs={{0,16},{1,17},{2,18},{3,19},{4,20},{5,21},{6,22},{7,23},{8,24},{9,... | collective-permute-start | bytes 73736 | tf_op jit(solution)/shard_map/ppermute | solution.py:54
  185.5 5.7 %collective-permute-start.38 = (f32[12,512]{1,0:T(8,128)S(1)}, f32[12,512]{1,0:T(8,128)S(1)}, u32[]{:S(2)}, u32[]{:S(2)}) collective-permute-start(f32[12,512]{1,0:T(8,128)S(1)} %add_add_fusion.1), channel_id=1, source_target_pairs={{0,24},{1,25},{2,26},{3,27},{4,28},{5,29},{6,30},{7,31},{8,16},{9,... | collective-permute-start | bytes 73736 | tf_op jit(solution)/shard_map/ppermute | solution.py:54

commit v5 on v4

--- a/solution.py
+++ b/solution.py
@@ -174,18 +174,47 @@
     ]
 
 
-def reduce_end(own_part, arrived):
-    return own_part + sum(part.astype(jnp.float32) for part in arrived)
+def finish_kernel(sums_ref, gain_ref, shift_ref, *refs):
+    *ins, total_a_ref, total_b_ref, payload_ref = refs
+    half = len(ins) // 2
+    squares = 0.0
+    for group, target in ((ins[:half], total_a_ref), (ins[half:], total_b_ref)):
+        for piece in range(target.shape[0]):
+            total = group[0][piece]
+            for arrived in group[1:]:
+                total = total + arrived[piece].astype(jnp.float32)
+            target[piece] = total
+            squares = squares + total * total
+    payload_ref[...] = sums_ref[...]
+    payload_ref[0:1, :] = gain_ref[...]
+    payload_ref[1:2, :] = shift_ref[...]
+    payload_ref[11:12, :] = jnp.sum(squares, 0, keepdims=True)
+
+
+def finish(sums, gain, shift, own_a, z_a, own_b, z_b):
+    ins = [sums, gain[None], shift[None], own_a, *z_a, own_b, *z_b]
+    return pl.pallas_call(
+        finish_kernel,
+        in_specs=[vmem_spec() for _ in ins],
+        out_specs=[vmem_spec() for _ in range(3)],
+        out_shape=[jax.ShapeDtypeStruct(value.shape, jnp.float32) for value in (own_a, own_b, sums)],
+        name="finish",
+    )(*ins)
+
+
+def tree_sum(values):
+    while len(values) > 1:
+        values = [one + two for one, two in zip(values[::2], values[1::2])]
+    return values[0]
 
 
 def sum_all(value, groups):
     count = 2 ** sum(groups)
+    values = [value]
     for first_bit, bits in stage_bits(groups):
+        value = tree_sum(values)
         values = [value] + [swap_with(value, offset << first_bit, count) for offset in range(1, 2**bits)]
-        while len(values) > 1:
-            values = [one + two for one, two in zip(values[::2], values[1::2])]
-        value = values[0]
-    return value
+    return values
 
 
 def tie(*values):
@@ -627,13 +656,15 @@
     return pltpu.roll(rows, (width - first) % width, 1)[:, :lanes]
 
 
-def update_kernel(own_ref, payload_ref, a_ref, b_ref, *refs):
+def update_kernel(terms, own_ref, a_ref, b_ref, *refs):
+    payload = tree_sum([ref[...] for ref in refs[:terms]])
+    refs = refs[terms:]
     states = [refs[3 * index : 3 * index + 3] for index in range(6)]
     norm_ref = refs[18]
     news = [refs[19 + 3 * index : 22 + 3 * index] for index in range(6)]
-    squares = payload_ref[:11, :] * payload_ref[:11, :]
-    total = jnp.sum(jnp.sum(squares, 1, keepdims=True), 0, keepdims=True)
-    norm = jnp.sqrt(total + payload_ref[11:12, 0:1])
+    line = lax.broadcasted_iota(jnp.int32, payload.shape, 0)
+    squares = jnp.where(line == 11, payload, payload * payload)
+    norm = jnp.sqrt(jnp.sum(jnp.sum(squares, 1, keepdims=True), 0, keepdims=True))
     norm_ref[...] = norm
     factor = jnp.minimum(1.0, clip_norm / (norm + 1e-06))
 
@@ -656,11 +687,10 @@
         update(3, slice(chunk * step, (chunk + 1) * step), b_ref[3 + chunks + chunk])
     own = own_ref[0]
     vec_lanes = states[4][0].shape[1]
-    update(4, Ellipsis, own_lanes(payload_ref[0:8, :], own * vec_lanes, vec_lanes)[:7])
+    update(4, Ellipsis, own_lanes(payload[0:8], own * vec_lanes, vec_lanes)[:7])
     bias_lanes = states[5][0].shape[1]
     first = own * bias_lanes
-    line = lax.broadcasted_iota(jnp.int32, (5, width), 0)
-    picked = jnp.sum(jnp.where(line == first // width, payload_ref[7:12, :], 0.0), 0, keepdims=True)
+    picked = jnp.sum(jnp.where(line == 7 + first // width, payload, 0.0), 0, keepdims=True)
     picked = own_lanes(jnp.broadcast_to(picked, (8, width)), first % width, bias_lanes)
     update(5, Ellipsis, picked[0:1])
 
@@ -669,12 +699,12 @@
     flat = [value for state in states for value in state]
     shapes = [jax.ShapeDtypeStruct(value.shape, jnp.float32) for value in flat]
     norm, *news = pl.pallas_call(
-        update_kernel,
-        in_specs=[smem_spec()] + [vmem_spec() for _ in range(3 + len(flat))],
+        functools.partial(update_kernel, len(payload)),
+        in_specs=[smem_spec()] + [vmem_spec() for _ in range(2 + len(payload) + len(flat))],
         out_specs=[vmem_spec() for _ in range(1 + len(flat))],
         out_shape=[jax.ShapeDtypeStruct((1, 1), jnp.float32)] + shapes,
         name="update",
-    )(own[None].astype(jnp.int32), payload, total_a, total_b, *flat)
+    )(own[None].astype(jnp.int32), total_a, total_b, *payload, *flat)
     return norm[0, 0], [news[3 * index : 3 * index + 3] for index in range(len(states))]
 
 
@@ -758,7 +788,7 @@
     )
     w_qkv = w_qkv.reshape(3, count * step, width)
     core_near = [swap_with(half, 1, count) for half in halves]
-    mixed_heads, gain_one, *tied = tie(mixed_heads, vectors[0], *core_near, *received)
+    mixed_heads, *tied = tie(mixed_heads, *core_near, *received)
     core_near, received = tied[:2], tied[2:]
     core_far = [swap_with(half, 1, count) for half in received]
     unit_one = (inputs - mean_one) * scale_one
@@ -780,7 +810,7 @@
         groups,
     )
     core_b = swap_with(sent_b, 1, count)
-    core_b, kept_b, grad_mixed = tie(core_b, kept_b, grad_mixed)
+    core_b, kept_b, grad_mixed, gain_one = tie(core_b, kept_b, grad_mixed, vectors[0])
     own_b, parts_b = plane_sums(kept_b, core_b, groups)
     own_b, log_total, *parts_b = tie(own_b, log_total, *parts_b)
     plane_b = plane_send(parts_b, groups)
@@ -801,12 +831,7 @@
         input_grad, grad_gain_one, grad_shift_one, *plane_a
     )
     own_a, z_a = reduce_z(own_a, plane_a, groups)
-    total_b = reduce_end(own_b, z_b)
-    total_a = reduce_end(own_a, z_a)
-    local_squares = jnp.sum(total_b * total_b) + jnp.sum(total_a * total_a)
-    line = lax.broadcasted_iota(jnp.int32, sums.shape, 0)
-    payload = jnp.where(line == 0, grad_gain_one, jnp.where(line == 1, grad_shift_one, sums))
-    payload = jnp.where(line == 11, local_squares, payload)
+    total_a, total_b, payload = finish(sums, grad_gain_one, grad_shift_one, own_a, z_a, own_b, z_b)
     payload = sum_all(payload, groups)
     states = (
         (attn_weight, attn_m, attn_v),

time: 195 us -> 196 us (level)
  Pallas kernels: 80.1 us -> 82.3 us
    reduce_sum x2 -> x0, other arithmetic: 3.7 us -> none  [body(): local_squares = jnp.sum(total_b * total_b) + jnp.sum(total_a * total_a)]
    pallas_call x1 -> x2, Pallas kernels: 2.97 us -> 5.04 us  [the longest x1 2.85 us: update_all(): pl.pallas_call(functools.partial(update_kernel, len(payload)), in_specs=[...]
  transfers between devices with their start and end apart: 39 -> 39, of which waited for: 16 -> 21; matrix products, arithmetic and copies ran while one was open for 6% -> 6% of each run, Pallas kernels for 24% -> 24%
where the time goes in v5:
time: 196 us; the launch traced here: 195 us
  Pallas kernels  82.3 us (42%)
  starting transfers between devices  46.6 us (24%)
  waiting for transfers between devices  43 us (22%)
  other arithmetic  16.8 us (9%)
  local copies, waits for them, and re-layouts  5.25 us (3%)
    ppermute x39, starting transfers between devices, swap_with(): lax.ppermute(array, AXES, [(source, source ^ offset) for source in range(...  46.6 us
    ppermute x39, waiting for transfers between devices, swap_with(): lax.ppermute(array, AXES, [(source, source ^ offset) for source in range(...  43 us
    pallas_call x1, Pallas kernels, ffn(): pl.pallas_call(functools.partial(ffn_kernel, direct, len(parts), tables,...  30.7 us
    pallas_call x1, Pallas kernels, attend_back(): pl.pallas_call(functools.partial(attn_bwd_kernel, offsets), grid=(width /...  29.5 us
    pallas_call x1, Pallas kernels, attend(): pl.pallas_call(functools.partial(attn_fwd_kernel, direct, tables, layout)...  17 us
    convert_element_type x2, other arithmetic, plane_sums(): total(offset).astype(jnp.bfloat16)  4.4 us
  transfers between devices with their start and end apart: 39, of which 21 were waited for; matrix products, arithmetic and copies ran while one was open for 6% of the time, Pallas kernels for 24%

profile of v5, /device:TPU:0, one launch (start us, length us, event | category | flops | bytes accessed | tf_op | source)
XLA Modules:
  0.0 195.2 jit_solution(2822403808240816658)
XLA Ops:
  0.7 0.9 convert.28
  1.6 0.7 tile.8
  2.4 0.7 tile.19
  3.3 3.1 %collective-permute-start = (bf16[4,16,512]{2,1,0:T(8,128)(2,1)S(1)}, bf16[4,16,512]{2,1,0:T(8,128)(2,1)S(1)}, u32[]{:S(2)}, u32[]{:S(2)}) collective-permute-start(bf16[4,16,512]{2,1,0:T(8,128)(2,1)S(1)} %get-tuple-element.212), channel_id=1, source_target_pairs={{0,8},{1,9},{2,10},{3,11},{4,12},{5,13},{6,14},{7,15},{8,0},{9,1},... | collective-permute-start | bytes 196616 | tf_op jit(solution)/shard_map/ppermute | solution.py:54
  6.5 2.6 %collective-permute-start.1 = (bf16[4,16,512]{2,1,0:T(8,128)(2,1)S(1)}, bf16[4,16,512]{2,1,0:T(8,128)(2,1)S(1)}, u32[]{:S(2)}, u32[]{:S(2)}) collective-permute-start(bf16[4,16,512]{2,1,0:T(8,128)(2,1)S(1)} %get-tuple-element.212), channel_id=1, source_target_pairs={{0,16},{1,17},{2,18},{3,19},{4,20},{5,21},{6,22},{7,23},{8,24},{9,... | collective-permute-start | bytes 196616 | tf_op jit(solution)/shard_map/ppermute | solution.py:54
  9.0 0.9 convert_element_type.189
  10.0 0.8 convert_dynamic-update-slice_fusion
  10.8 0.9 convert_element_type.190
  11.8 1.0 collective-permute-start.3
  12.7 3.5 %collective-permute-start.4 = (bf16[11,16,512]{2,1,0:T(8,128)(2,1)S(1)}, bf16[11,16,512]{2,1,0:T(8,128)(2,1)S(1)}, u32[]{:S(2)}, u32[]{:S(2)}) collective-permute-start(bf16[11,16,512]{2,1,0:T(8,128)(2,1)S(1)} %constant_dynamic-update-slice_fusion), channel_id=1, source_target_pairs={{0,16},{1,17},{2,18},{3,19},{4,20},{5,21},{6,22},{7,23},{8,24},{9,... | collective-permute-start | bytes 540680 | tf_op jit(solution)/shard_map/ppermute | solution.py:54
  16.3 1.8 collective-permute-start.6
  18.1 1.5 collective-permute-start.7
  19.6 1.4 collective-permute-done.3
  21.0 2.4 %collective-permute-start.8 = (bf16[4,4,16,512]{3,2,1,0:T(8,128)(2,1)S(1)}, bf16[4,4,16,512]{3,2,1,0:T(8,128)(2,1)S(1)}, u32[]{:S(2)}, u32[]{:S(2)}) collective-permute-start(bf16[4,4,16,512]{3,2,1,0:T(8,128)(2,1)S(1)} %pad_maximum_fusion.3.refs_0_), channel_id=1, source_target_pairs={{0,6},{1,7},{2,4},{3,5},{4,2},{5,3},{6,0},{7,1},{8,14},{9,15},{10,... | collective-permute-start | bytes 786440 | tf_op jit(solution)/shard_map/ppermute | solution.py:54
  23.5 5.8 %collective-permute-done.4 = bf16[11,16,512]{2,1,0:T(8,128)(2,1)S(1)} collective-permute-done((bf16[11,16,512]{2,1,0:T(8,128)(2,1)S(1)}, bf16[11,16,512]{2,1,0:T(8,128)(2,1)S(1)}, u32[]{:S(2)}, u32[]{:S(2)}) %collective-permute-start.4) | collective-permute-done | bytes 180256 | tf_op jit(solution)/shard_map/ppermute | solution.py:54
  31.0 1.7 collective-permute-start.10
  33.3 1.6 collective-permute-start.11
  34.9 7.2 %collective-permute-done.11 = bf16[4,5,16,512]{3,2,1,0:T(8,128)(2,1)S(1)} collective-permute-done((bf16[4,5,16,512]{3,2,1,0:T(8,128)(2,1)S(1)}, bf16[4,5,16,512]{3,2,1,0:T(8,128)(2,1)S(1)}, u32[]{:S(2)}, u32[]{:S(2)}) %collective-permute-start.11) | collective-permute-done | bytes 327712 | tf_op jit(solution)/shard_map/ppermute | solution.py:54
  42.2 1.6 collective-permute-start.14
  44.1 1.0 collective-permute-start.15
  45.1 17.0 %attn_fwd.1 = (bf16[1024,512]{1,0:T(8,128)(2,1)}, bf16[1024,512]{1,0:T(8,128)(2,1)}, bf16[1024,512]{1,0:T(8,128)(2,1)}, bf16[1024,512]{1,0:T(8,128)(2,1)}, bf16[...) custom-call(s32[1]{0:T(128)} %bitcast.own_ref, ...), custom_call_target="tpu_custom_call" | custom-call | tf_op jit(solution)/shard_map/attn_fwd/pallas_call | solution.py:394
  62.8 2.9 %collective-permute-done.17.refs_7_ = bf16[8,5,16,512]{3,2,1,0:T(8,128)(2,1)S(1)} collective-permute-done((bf16[8,5,16,512]{3,2,1,0:T(8,128)(2,1)}, bf16[8,5,16,512]{3,2,1,0:T(8,128)(2,1)S(1)}, u32[]{:S(2)}, u32[]{:S(2)}) %collective-permute-start.17) | collective-permute-done | bytes 655392 | tf_op jit(solution)/shard_map/ppermute | solution.py:54
  65.7 0.8 copy-done.14
  66.8 30.7 %ffn.1 = (bf16[1024,512]{1,0:T(8,128)(2,1)}, bf16[1024,512]{1,0:T(8,128)(2,1)}, f32[1024,512]{1,0:T(8,128)}, f32[1024,512]{1,0:T(8,128)}, f32[12,512]{1,0:T(8,12...) custom-call(s32[1]{0:T(128)} %bitcast.own_ref, bf16[1024,512]{1,0:T(8,128)(2,1)} %x_ref.3, ...), custom_call_target="tpu_custom_call" | custom-call | tf_op jit(solution)/shard_map/ffn/pallas_call | solution.py:624
  97.8 0.7 slice.197
  98.5 4.6 %collective-permute-done.18 = bf16[16,11,16,512]{3,2,1,0:T(8,128)(2,1)S(1)} collective-permute-done((bf16[16,11,16,512]{3,2,1,0:T(8,128)(2,1)}, bf16[16,11,16,512]{3,2,1,0:T(8,128)(2,1)S(1)}, u32[]{:S(2)}, u32[]{:S(2)}) %collective-permute-start.18) | collective-permute-done | bytes 2883616 | tf_op jit(solution)/shard_map/ppermute | solution.py:54
  103.1 4.1 %add_convert_fusion = (bf16[4,11,16,512]{3,2,1,0:T(8,128)(2,1)}, bf16[4,11,16,512]{3,2,1,0:T(8,128)(2,1)}, bf16[4,11,16,512]{3,2,1,0:T(8,128)(2,1)}, f32[4,11,16,512]{3,2,1,0:T(8,128)S(1)}) fusion(bf16[16,11,16,512]{3,2,1,0:T(8,128)(2,1)S(1)} %collective-permute-done.18, bf16[16,11,16,512]{3,2,1,0:T(8,128)(2,1)} %get-tuple-element.135), kind=kLoop, calls=%fused_computation.16 | loop fusion | flops 5406720 | bytes 9371648 | tf_op jit(solution)/shard_map/convert_element_type | solution.py:160
  107.2 1.0 collective-permute-start.19
  108.2 1.5 collective-permute-start.20
  109.7 1.0 collective-permute-start.21
  110.7 29.5 %attn_bwd.1 = (bf16[16,3,16,512]{3,2,1,0:T(8,128)(2,1)}, bf16[16,3,16,512]{3,2,1,0:T(8,128)(2,1)}, f32[1024,512]{1,0:T(8,128)}) custom-call(s32[1]{0:T(128)} %bitcast.own_ref, s32[1,1024]{1,0:T(1,128)} %bitcast.78, s32[1,1024]{1,0:T(1,128)} %bitcast.80, bf16[1024,512]{1,0:T(8,128)(2,1)} %get-tuple-element.128.q_ref, ...), custom_call_target="tpu_custom_call" | custom-call | tf_op jit(solution)/shard_map/attn_bwd/pallas_call | solution.py:429
  140.2 0.7 collective-permute-done.20
  140.9 1.2 collective-permute-done.21
  142.1 2.6 %fusion.14 = (bf16[11,16,512]{2,1,0:T(8,128)(2,1)S(1)}, bf16[11,16,512]{2,1,0:T(8,128)(2,1)S(1)}, bf16[11,16,512]{2,1,0:T(8,128)(2,1)S(1)}, f32[11,16,512]{2,1,0:T(8,128)}) fusion(f32[4,11,16,512]{3,2,1,0:T(8,128)S(1)} %get-tuple-element.165, bf16[4,11,16,512]{3,2,1,0:T(8,128)(2,1)} %collective-permute-done.21, ...), kind=kLoop, calls=%fused_computation.34 | loop fusion | flops 2433024 | bytes 4505600 | tf_op jit(solution)/shard_map/add | solution.py:171
  144.7 3.6 %collective-permute-start.29 = (bf16[11,16,512]{2,1,0:T(8,128)(2,1)S(1)}, bf16[11,16,512]{2,1,0:T(8,128)(2,1)S(1)}, u32[]{:S(2)}, u32[]{:S(2)}) collective-permute-start(bf16[11,16,512]{2,1,0:T(8,128)(2,1)S(1)} %get-tuple-element.201), channel_id=1, source_target_pairs={{0,24},{1,25},{2,26},{3,27},{4,28},{5,29},{6,30},{7,31},{8,16},{9,... | collective-permute-start | bytes 540680 | tf_op jit(solution)/shard_map/ppermute | solution.py:54
  149.0 1.8 fusion.11
  150.8 1.0 collective-permute-start.23
  151.8 1.2 collective-permute-start.24
  153.0 1.3 collective-permute-start.25
  154.3 1.7 fusion.10
  156.0 2.6 %collective-permute-done.23 = bf16[4,3,16,512]{3,2,1,0:T(8,128)(2,1)S(1)} collective-permute-done((bf16[4,3,16,512]{3,2,1,0:T(8,128)(2,1)S(1)}, bf16[4,3,16,512]{3,2,1,0:T(8,128)(2,1)S(1)}, u32[]{:S(2)}, u32[]{:S(2)}) %collective-permute-start.23) | collective-permute-done | bytes 196640 | tf_op jit(solution)/shard_map/ppermute | solution.py:54
  159.0 2.2 %collective-permute-done.24 = bf16[4,3,16,512]{3,2,1,0:T(8,128)(2,1)S(1)} collective-permute-done((bf16[4,3,16,512]{3,2,1,0:T(8,128)(2,1)S(1)}, bf16[4,3,16,512]{3,2,1,0:T(8,128)(2,1)S(1)}, u32[]{:S(2)}, u32[]{:S(2)}) %collective-permute-start.24) | collective-permute-done | bytes 196640 | tf_op jit(solution)/shard_map/ppermute | solution.py:54
  161.2 1.3 collective-permute-done.25
  162.5 0.8 fusion.17
  163.3 2.4 %collective-permute-start.26 = (bf16[3,16,512]{2,1,0:T(8,128)(2,1)S(1)}, bf16[3,16,512]{2,1,0:T(8,128)(2,1)S(1)}, u32[]{:S(2)}, u32[]{:S(2)}) collective-permute-start(bf16[3,16,512]{2,1,0:T(8,128)(2,1)S(1)} %get-tuple-element.209), channel_id=1, source_target_pairs={{0,24},{1,25},{2,26},{3,27},{4,28},{5,29},{6,30},{7,31},{8,16},{9,... | collective-permute-start | bytes 147464 | tf_op jit(solution)/shard_map/ppermute | solution.py:54
  165.8 1.9 collective-permute-start.28
  167.9 1.3 collective-permute-done.26.refs_1_
  169.2 2.0 %collective-permute-done.27.refs_2_ = bf16[3,16,512]{2,1,0:T(8,128)(2,1)S(1)} collective-permute-done((bf16[3,16,512]{2,1,0:T(8,128)(2,1)S(1)}, bf16[3,16,512]{2,1,0:T(8,128)(2,1)S(1)}, u32[]{:S(2)}, u32[]{:S(2)}) %collective-permute-start.27) | collective-permute-done | bytes 49184 | tf_op jit(solution)/shard_map/ppermute | solution.py:54
  171.3 0.6 copy-done.20
  171.9 2.2 %finish.1 = (f32[3,16,512]{2,1,0:T(8,128)}, f32[11,16,512]{2,1,0:T(8,128)}, f32[12,512]{1,0:T(8,128)}) custom-call(f32[12,512]{1,0:T(8,128)} %get-tuple-element.158.sums_ref, f32[1,512]{1,0:T(1,128)} %bitcast.81, f32[1,512]{1,0:T(1,128)} %bitcast.82, f32[3,16,512]{2,1,0:T(8,128)} %get-tuple-element.210.refs_0_, bf16[3,16,512]{2,1,0:T(8,128)(2,1)} %copy-done.19, ...), custom_call_target="tpu_custom_call" | custom-call | tf_op jit(solution)/shard_map/finish/pallas_call | solution.py:196
  174.1 1.4 collective-permute-done.32
  175.5 0.8 add.220
  176.2 1.0 collective-permute-start.33
  177.2 1.2 collective-permute-start.34
  178.5 1.3 collective-permute-start.35
  180.2 1.0 collective-permute-done.34
  181.1 2.1 %collective-permute-done.35 = f32[12,512]{1,0:T(8,128)S(1)} collective-permute-done((f32[12,512]{1,0:T(8,128)S(1)}, f32[12,512]{1,0:T(8,128)S(1)}, u32[]{:S(2)}, u32[]{:S(2)}) %collective-permute-start.35) | collective-permute-done | bytes 24608 | tf_op jit(solution)/shard_map/ppermute | solution.py:54
  183.3 0.6 collective-permute-start.36
  183.9 2.0 %collective-permute-start.37 = (f32[12,512]{1,0:T(8,128)S(1)}, f32[12,512]{1,0:T(8,128)S(1)}, u32[]{:S(2)}, u32[]{:S(2)}) collective-permute-start(f32[12,512]{1,0:T(8,128)S(1)} %add_add_fusion.refs_0_), channel_id=1, source_target_pairs={{0,16},{1,17},{2,18},{3,19},{4,20},{5,21},{6,22},{7,23},{8,24},{9,... | collective-permute-start | bytes 73736 | tf_op jit(solution)/shard_map/ppermute | solution.py:54
  185.9 1.9 collective-permute-start.38
  187.8 1.1 collective-permute-done.37.refs_2_
  188.9 2.7 %collective-permute-done.38.refs_3_ = f32[12,512]{1,0:T(8,128)S(1)} collective-permute-done((f32[12,512]{1,0:T(8,128)S(1)}, f32[12,512]{1,0:T(8,128)S(1)}, u32[]{:S(2)}, u32[]{:S(2)}) %collective-permute-start.38) | collective-permute-done | bytes 24608 | tf_op jit(solution)/shard_map/ppermute | solution.py:54
  191.6 0.6 copy-done.24
  192.2 2.9 %update.1 = (f32[1,1]{1,0:T(1,128)}, f32[4,16,512]{2,1,0:T(8,128)}, f32[4,16,512]{2,1,0:T(8,128)}, f32[4,16,512]{2,1,0:T(8,128)}, f32[2,16,512]{2,1,0:T(8,128)},...) custom-call(s32[1]{0:T(128)} %bitcast.own_ref, ...), custom_call_target="tpu_custom_call" | custom-call | tf_op jit(solution)/shard_map/update/pallas_call | solution.py:701
  (115 shorter events, 5.9 us)
Async XLA Ops:
  3.3 12.9 %collective-permute-start = (bf16[4,16,512]{2,1,0:T(8,128)(2,1)S(1)}, bf16[4,16,512]{2,1,0:T(8,128)(2,1)S(1)}, u32[]{:S(2)}, u32[]{:S(2)}) collective-permute-start(bf16[4,16,512]{2,1,0:T(8,128)(2,1)S(1)} %get-tuple-element.212), channel_id=1, source_target_pairs={{0,8},{1,9},{2,10},{3,11},{4,12},{5,13},{6,14},{7,15},{8,0},{9,1},... | collective-permute-start | bytes 196616 | tf_op jit(solution)/shard_map/ppermute | solution.py:54
  6.5 9.8 %collective-permute-start.1 = (bf16[4,16,512]{2,1,0:T(8,128)(2,1)S(1)}, bf16[4,16,512]{2,1,0:T(8,128)(2,1)S(1)}, u32[]{:S(2)}, u32[]{:S(2)}) collective-permute-start(bf16[4,16,512]{2,1,0:T(8,128)(2,1)S(1)} %get-tuple-element.212), channel_id=1, source_target_pairs={{0,16},{1,17},{2,18},{3,19},{4,20},{5,21},{6,22},{7,23},{8,24},{9,... | collective-permute-start | bytes 196616 | tf_op jit(solution)/shard_map/ppermute | solution.py:54
  9.0 7.2 %collective-permute-start.2 = (bf16[4,16,512]{2,1,0:T(8,128)(2,1)S(1)}, bf16[4,16,512]{2,1,0:T(8,128)(2,1)S(1)}, u32[]{:S(2)}, u32[]{:S(2)}) collective-permute-start(bf16[4,16,512]{2,1,0:T(8,128)(2,1)S(1)} %get-tuple-element.212), channel_id=1, source_target_pairs={{0,24},{1,25},{2,26},{3,27},{4,28},{5,29},{6,30},{7,31},{8,16},{9,... | collective-permute-start | bytes 196616 | tf_op jit(solution)/shard_map/ppermute | solution.py:54
  11.8 9.2 %collective-permute-start.3 = (bf16[11,16,512]{2,1,0:T(8,128)(2,1)S(1)}, bf16[11,16,512]{2,1,0:T(8,128)(2,1)S(1)}, u32[]{:S(2)}, u32[]{:S(2)}) collective-permute-start(bf16[11,16,512]{2,1,0:T(8,128)(2,1)S(1)} %constant_dynamic-update-slice_fusion), channel_id=1, source_target_pairs={{0,8},{1,9},{2,10},{3,11},{4,12},{5,13},{6,14},{7,15},{8,0},{9,1},... | collective-permute-start | bytes 540680 | tf_op jit(solution)/shard_map/ppermute | solution.py:54
  12.7 16.6 %collective-permute-start.4 = (bf16[11,16,512]{2,1,0:T(8,128)(2,1)S(1)}, bf16[11,16,512]{2,1,0:T(8,128)(2,1)S(1)}, u32[]{:S(2)}, u32[]{:S(2)}) collective-permute-start(bf16[11,16,512]{2,1,0:T(8,128)(2,1)S(1)} %constant_dynamic-update-slice_fusion), channel_id=1, source_target_pairs={{0,16},{1,17},{2,18},{3,19},{4,20},{5,21},{6,22},{7,23},{8,24},{9,... | collective-permute-start | bytes 540680 | tf_op jit(solution)/shard_map/ppermute | solution.py:54
  16.2 13.1 %collective-permute-start.5 = (bf16[11,16,512]{2,1,0:T(8,128)(2,1)S(1)}, bf16[11,16,512]{2,1,0:T(8,128)(2,1)S(1)}, u32[]{:S(2)}, u32[]{:S(2)}) collective-permute-start(bf16[11,16,512]{2,1,0:T(8,128)(2,1)S(1)} %constant_dynamic-update-slice_fusion), channel_id=1, source_target_pairs={{0,24},{1,25},{2,26},{3,27},{4,28},{5,29},{6,30},{7,31},{8,16},{9,... | collective-permute-start | bytes 540680 | tf_op jit(solution)/shard_map/ppermute | solution.py:54
  16.3 13.9 %copy-start.3 = (bf16[4,4,16,512]{3,2,1,0:T(8,128)(2,1)}, bf16[4,4,16,512]{3,2,1,0:T(8,128)(2,1)S(1)}, u32[]{:S(2)}) copy-start(bf16[4,4,16,512]{3,2,1,0:T(8,128)(2,1)S(1)} %pad_maximum_fusion.3.refs_0_) | copy-start | bytes 786436
  16.3 13.2 %collective-permute-start.6 = (bf16[4,4,16,512]{3,2,1,0:T(8,128)(2,1)S(1)}, bf16[4,4,16,512]{3,2,1,0:T(8,128)(2,1)S(1)}, u32[]{:S(2)}, u32[]{:S(2)}) collective-permute-start(bf16[4,4,16,512]{3,2,1,0:T(8,128)(2,1)S(1)} %pad_maximum_fusion.3.refs_0_), channel_id=1, source_target_pairs={{0,2},{1,3},{2,0},{3,1},{4,6},{5,7},{6,4},{7,5},{8,10},{9,11},{10,... | collective-permute-start | bytes 786440 | tf_op jit(solution)/shard_map/ppermute | solution.py:54
  18.1 12.0 %collective-permute-start.7 = (bf16[4,4,16,512]{3,2,1,0:T(8,128)(2,1)S(1)}, bf16[4,4,16,512]{3,2,1,0:T(8,128)(2,1)S(1)}, u32[]{:S(2)}, u32[]{:S(2)}) collective-permute-start(bf16[4,4,16,512]{3,2,1,0:T(8,128)(2,1)S(1)} %pad_maximum_fusion.3.refs_0_), channel_id=1, source_target_pairs={{0,4},{1,5},{2,6},{3,7},{4,0},{5,1},{6,2},{7,3},{8,12},{9,13},{10,... | collective-permute-start | bytes 786440 | tf_op jit(solution)/shard_map/ppermute | solution.py:54
  21.0 9.0 %collective-permute-start.8 = (bf16[4,4,16,512]{3,2,1,0:T(8,128)(2,1)S(1)}, bf16[4,4,16,512]{3,2,1,0:T(8,128)(2,1)S(1)}, u32[]{:S(2)}, u32[]{:S(2)}) collective-permute-start(bf16[4,4,16,512]{3,2,1,0:T(8,128)(2,1)S(1)} %pad_maximum_fusion.3.refs_0_), channel_id=1, source_target_pairs={{0,6},{1,7},{2,4},{3,5},{4,2},{5,3},{6,0},{7,1},{8,14},{9,15},{10,... | collective-permute-start | bytes 786440 | tf_op jit(solution)/shard_map/ppermute | solution.py:54
  29.4 1.3 copy-start
  29.5 3.7 %copy-start.8 = (bf16[4,4,16,512]{3,2,1,0:T(8,128)(2,1)}, bf16[4,4,16,512]{3,2,1,0:T(8,128)(2,1)S(1)}, u32[]{:S(2)}) copy-start(bf16[4,4,16,512]{3,2,1,0:T(8,128)(2,1)S(1)} %collective-permute-done.6.refs_1_) | copy-start | bytes 786436
  30.1 3.2 %copy-start.9 = (bf16[4,4,16,512]{3,2,1,0:T(8,128)(2,1)}, bf16[4,4,16,512]{3,2,1,0:T(8,128)(2,1)S(1)}, u32[]{:S(2)}) copy-start(bf16[4,4,16,512]{3,2,1,0:T(8,128)(2,1)S(1)} %collective-permute-done.7.refs_2_) | copy-start | bytes 786436
  30.1 3.2 %copy-start.10 = (bf16[4,4,16,512]{3,2,1,0:T(8,128)(2,1)}, bf16[4,4,16,512]{3,2,1,0:T(8,128)(2,1)S(1)}, u32[]{:S(2)}) copy-start(bf16[4,4,16,512]{3,2,1,0:T(8,128)(2,1)S(1)} %collective-permute-done.8.refs_3_) | copy-start | bytes 786436
  30.2 11.9 %collective-permute-start.9 = (bf16[16,4,16,512]{3,2,1,0:T(8,128)(2,1)S(1)}, bf16[16,4,16,512]{3,2,1,0:T(8,128)(2,1)S(1)}, u32[]{:S(2)}, u32[]{:S(2)}) collective-permute-start(bf16[16,4,16,512]{3,2,1,0:T(8,128)(2,1)S(1)} %pad_maximum_fusion), channel_id=1, source_target_pairs={{0,1},{1,0},{2,3},{3,2},{4,5},{5,4},{6,7},{7,6},{8,9},{9,8},{10,11... | collective-permute-start | bytes 3145736 | tf_op jit(solution)/shard_map/ppermute | solution.py:54
  31.0 11.1 %collective-permute-start.10 = (bf16[4,6,16,512]{3,2,1,0:T(8,128)(2,1)S(1)}, bf16[4,6,16,512]{3,2,1,0:T(8,128)(2,1)S(1)}, u32[]{:S(2)}, u32[]{:S(2)}) collective-permute-start(bf16[4,6,16,512]{3,2,1,0:T(8,128)(2,1)S(1)} %slice.252), channel_id=1, source_target_pairs={{0,2},{1,3},{2,0},{3,1},{4,6},{5,7},{6,4},{7,5},{8,10},{9,11},{10,... | collective-permute-start | bytes 1179656 | tf_op jit(solution)/shard_map/ppermute | solution.py:54
  33.3 8.8 %collective-permute-start.11 = (bf16[4,5,16,512]{3,2,1,0:T(8,128)(2,1)S(1)}, bf16[4,5,16,512]{3,2,1,0:T(8,128)(2,1)S(1)}, u32[]{:S(2)}, u32[]{:S(2)}) collective-permute-start(bf16[4,5,16,512]{3,2,1,0:T(8,128)(2,1)S(1)} %pad_maximum_fusion.2), channel_id=1, source_target_pairs={{0,4},{1,5},{2,6},{3,7},{4,0},{5,1},{6,2},{7,3},{8,12},{9,13},{10,... | collective-permute-start | bytes 983048 | tf_op jit(solution)/shard_map/ppermute | solution.py:54
  42.1 3.0 %copy-start.7 = (bf16[16,4,16,512]{3,2,1,0:T(8,128)(2,1)}, bf16[16,4,16,512]{3,2,1,0:T(8,128)(2,1)S(1)}, u32[]{:S(2)}) copy-start(bf16[16,4,16,512]{3,2,1,0:T(8,128)(2,1)S(1)} %collective-permute-done.9.refs_4_) | copy-start | bytes 3145732
  42.1 20.0 %copy-start.5 = (bf16[8,6,16,512]{3,2,1,0:T(8,128)(2,1)}, bf16[8,6,16,512]{3,2,1,0:T(8,128)(2,1)S(1)}, u32[]{:S(2)}) copy-start(bf16[8,6,16,512]{3,2,1,0:T(8,128)(2,1)S(1)} %constant_dynamic-update-slice_fusion.6.refs_0_) | copy-start | bytes 2359300
  42.2 20.0 %collective-permute-start.12 = (bf16[8,6,16,512]{3,2,1,0:T(8,128)(2,1)S(1)}, bf16[8,6,16,512]{3,2,1,0:T(8,128)(2,1)S(1)}, u32[]{:S(2)}, u32[]{:S(2)}) collective-permute-start(bf16[8,6,16,512]{3,2,1,0:T(8,128)(2,1)S(1)} %constant_dynamic-update-slice_fusion.6.refs_0_), channel_id=1, source_target_pairs={{0,1},{1,0},{2,3},{3,2},{4,5},{5,4},{6,7},{7,6},{8,9},{9,8},{10,11... | collective-permute-start | bytes 2359304 | tf_op jit(solution)/shard_map/ppermute | solution.py:54
  42.2 20.0 %collective-permute-start.14 = (bf16[8,6,16,512]{3,2,1,0:T(8,128)(2,1)S(1)}, bf16[8,6,16,512]{3,2,1,0:T(8,128)(2,1)}, u32[]{:S(2)}, u32[]{:S(2)}) collective-permute-start(bf16[8,6,16,512]{3,2,1,0:T(8,128)(2,1)S(1)} %constant_dynamic-update-slice_fusion.6.refs_0_), channel_id=1, source_target_pairs={{0,4},{1,5},{2,6},{3,7},{4,0},{5,1},{6,2},{7,3},{8,12},{9,13},{10,... | collective-permute-start | bytes 2359304 | tf_op jit(solution)/shard_map/ppermute | solution.py:54
  43.9 21.9 %copy-start.6 = (bf16[8,5,16,512]{3,2,1,0:T(8,128)(2,1)}, bf16[8,5,16,512]{3,2,1,0:T(8,128)(2,1)S(1)}, u32[]{:S(2)}) copy-start(bf16[8,5,16,512]{3,2,1,0:T(8,128)(2,1)S(1)} %constant_dynamic-update-slice_fusion.8.refs_1_) | copy-start | bytes 1966084
  43.9 18.3 %collective-permute-start.13 = (bf16[8,5,16,512]{3,2,1,0:T(8,128)(2,1)S(1)}, bf16[8,5,16,512]{3,2,1,0:T(8,128)(2,1)}, u32[]{:S(2)}, u32[]{:S(2)}) collective-permute-start(bf16[8,5,16,512]{3,2,1,0:T(8,128)(2,1)S(1)} %constant_dynamic-update-slice_fusion.8.refs_1_), channel_id=1, source_target_pairs={{0,1},{1,0},{2,3},{3,2},{4,5},{5,4},{6,7},{7,6},{8,9},{9,8},{10,11... | collective-permute-start | bytes 1966088 | tf_op jit(solution)/shard_map/ppermute | solution.py:54
  44.1 18.0 %collective-permute-start.15 = (bf16[8,5,16,512]{3,2,1,0:T(8,128)(2,1)S(1)}, bf16[8,5,16,512]{3,2,1,0:T(8,128)(2,1)}, u32[]{:S(2)}, u32[]{:S(2)}) collective-permute-start(bf16[8,5,16,512]{3,2,1,0:T(8,128)(2,1)S(1)} %constant_dynamic-update-slice_fusion.8.refs_1_), channel_id=1, source_target_pairs={{0,2},{1,3},{2,0},{3,1},{4,6},{5,7},{6,4},{7,5},{8,10},{9,11},{10,... | collective-permute-start | bytes 1966088 | tf_op jit(solution)/shard_map/ppermute | solution.py:54
  62.2 3.6 %copy-start.11 = (bf16[8,6,16,512]{3,2,1,0:T(8,128)(2,1)}, bf16[8,6,16,512]{3,2,1,0:T(8,128)(2,1)S(1)}, u32[]{:S(2)}) copy-start(bf16[8,6,16,512]{3,2,1,0:T(8,128)(2,1)S(1)} %collective-permute-done.12.refs_4_) | copy-start | bytes 2359300
  62.3 3.4 %collective-permute-start.16 = (bf16[8,6,16,512]{3,2,1,0:T(8,128)(2,1)}, bf16[8,6,16,512]{3,2,1,0:T(8,128)(2,1)S(1)}, u32[]{:S(2)}, u32[]{:S(2)}) collective-permute-start(bf16[8,6,16,512]{3,2,1,0:T(8,128)(2,1)} %collective-permute-done.14.refs_2_), channel_id=1, source_target_pairs={{0,1},{1,0},{2,3},{3,2},{4,5},{5,4},{6,7},{7,6},{8,9},{9,8},{10,11... | collective-permute-start | bytes 2359304 | tf_op jit(solution)/shard_map/ppermute | solution.py:54
  62.3 3.4 %collective-permute-start.17 = (bf16[8,5,16,512]{3,2,1,0:T(8,128)(2,1)}, bf16[8,5,16,512]{3,2,1,0:T(8,128)(2,1)S(1)}, u32[]{:S(2)}, u32[]{:S(2)}) collective-permute-start(bf16[8,5,16,512]{3,2,1,0:T(8,128)(2,1)} %collective-permute-done.15.refs_3_), channel_id=1, source_target_pairs={{0,1},{1,0},{2,3},{3,2},{4,5},{5,4},{6,7},{7,6},{8,9},{9,8},{10,11... | collective-permute-start | bytes 1966088 | tf_op jit(solution)/shard_map/ppermute | solution.py:54
  65.7 0.9 copy-start.14
  65.7 1.1 copy-start.12
  97.6 5.6 %collective-permute-start.18 = (bf16[16,11,16,512]{3,2,1,0:T(8,128)(2,1)}, bf16[16,11,16,512]{3,2,1,0:T(8,128)(2,1)S(1)}, u32[]{:S(2)}, u32[]{:S(2)}) collective-permute-start(bf16[16,11,16,512]{3,2,1,0:T(8,128)(2,1)} %get-tuple-element.131), channel_id=1, source_target_pairs={{0,1},{1,0},{2,3},{3,2},{4,5},{5,4},{6,7},{7,6},{8,9},{9,8},{10,11... | collective-permute-start | bytes 8650760 | tf_op jit(solution)/shard_map/ppermute | solution.py:54
  107.2 33.0 %collective-permute-start.19 = (bf16[4,11,16,512]{3,2,1,0:T(8,128)(2,1)}, bf16[4,11,16,512]{3,2,1,0:T(8,128)(2,1)S(1)}, u32[]{:S(2)}, u32[]{:S(2)}) collective-permute-start(bf16[4,11,16,512]{3,2,1,0:T(8,128)(2,1)} %get-tuple-element.145), channel_id=1, source_target_pairs={{0,2},{1,3},{2,0},{3,1},{4,6},{5,7},{6,4},{7,5},{8,10},{9,11},{10,... | collective-permute-start | bytes 2162696 | tf_op jit(solution)/shard_map/ppermute | solution.py:54
  108.2 32.7 %collective-permute-start.20 = (bf16[4,11,16,512]{3,2,1,0:T(8,128)(2,1)}, bf16[4,11,16,512]{3,2,1,0:T(8,128)(2,1)S(1)}, u32[]{:S(2)}, u32[]{:S(2)}) collective-permute-start(bf16[4,11,16,512]{3,2,1,0:T(8,128)(2,1)} %get-tuple-element.146), channel_id=1, source_target_pairs={{0,4},{1,5},{2,6},{3,7},{4,0},{5,1},{6,2},{7,3},{8,12},{9,13},{10,... | collective-permute-start | bytes 2162696 | tf_op jit(solution)/shard_map/ppermute | solution.py:54
  109.7 32.4 %collective-permute-start.21 = (bf16[4,11,16,512]{3,2,1,0:T(8,128)(2,1)}, bf16[4,11,16,512]{3,2,1,0:T(8,128)(2,1)}, u32[]{:S(2)}, u32[]{:S(2)}) collective-permute-start(bf16[4,11,16,512]{3,2,1,0:T(8,128)(2,1)} %get-tuple-element.147), channel_id=1, source_target_pairs={{0,6},{1,7},{2,4},{3,5},{4,2},{5,3},{6,0},{7,1},{8,14},{9,15},{10,... | collective-permute-start | bytes 2162696 | tf_op jit(solution)/shard_map/ppermute | solution.py:54
  142.1 6.6 %copy-start.13 = (bf16[16,3,16,512]{3,2,1,0:T(8,128)(2,1)S(1)}, bf16[16,3,16,512]{3,2,1,0:T(8,128)(2,1)}, u32[]{:S(2)}) copy-start(bf16[16,3,16,512]{3,2,1,0:T(8,128)(2,1)} %get-tuple-element.149) | copy-start | bytes 2359300
  142.1 6.6 %collective-permute-start.22 = (bf16[16,3,16,512]{3,2,1,0:T(8,128)(2,1)}, bf16[16,3,16,512]{3,2,1,0:T(8,128)(2,1)S(1)}, u32[]{:S(2)}, u32[]{:S(2)}) collective-permute-start(bf16[16,3,16,512]{3,2,1,0:T(8,128)(2,1)} %get-tuple-element.150), channel_id=1, source_target_pairs={{0,1},{1,0},{2,3},{3,2},{4,5},{5,4},{6,7},{7,6},{8,9},{9,8},{10,11... | collective-permute-start | bytes 2359304 | tf_op jit(solution)/shard_map/ppermute | solution.py:54
  142.1 6.9 %copy-start.2 = (f32[1024,512]{1,0:T(8,128)S(1)}, f32[1024,512]{1,0:T(8,128)}, u32[]{:S(2)}) copy-start(f32[1024,512]{1,0:T(8,128)} %get-tuple-element.151) | copy-start | bytes 6291460
  144.7 4.3 %copy-start.1 = (bf16[1024,512]{1,0:T(8,128)(2,1)S(1)}, bf16[1024,512]{1,0:T(8,128)(2,1)}, u32[]{:S(2)}) copy-start(bf16[1024,512]{1,0:T(8,128)(2,1)} %x_ref.3) | copy-start | bytes 3145732
  144.7 21.1 %collective-permute-start.29 = (bf16[11,16,512]{2,1,0:T(8,128)(2,1)S(1)}, bf16[11,16,512]{2,1,0:T(8,128)(2,1)S(1)}, u32[]{:S(2)}, u32[]{:S(2)}) collective-permute-start(bf16[11,16,512]{2,1,0:T(8,128)(2,1)S(1)} %get-tuple-element.201), channel_id=1, source_target_pairs={{0,24},{1,25},{2,26},{3,27},{4,28},{5,29},{6,30},{7,31},{8,16},{9,... | collective-permute-start | bytes 540680 | tf_op jit(solution)/shard_map/ppermute | solution.py:54
  148.3 19.3 %collective-permute-start.30 = (bf16[11,16,512]{2,1,0:T(8,128)(2,1)S(1)}, bf16[11,16,512]{2,1,0:T(8,128)(2,1)S(1)}, u32[]{:S(2)}, u32[]{:S(2)}) collective-permute-start(bf16[11,16,512]{2,1,0:T(8,128)(2,1)S(1)} %get-tuple-element.200), channel_id=1, source_target_pairs={{0,16},{1,17},{2,18},{3,19},{4,20},{5,21},{6,22},{7,23},{8,24},{9,... | collective-permute-start | bytes 540680 | tf_op jit(solution)/shard_map/ppermute | solution.py:54
  149.0 5.3 %copy-start.4 = (f32[1024,512]{1,0:T(8,128)S(1)}, f32[1024,512]{1,0:T(8,128)}, u32[]{:S(2)}) copy-start(f32[1024,512]{1,0:T(8,128)} %get-tuple-element.126) | copy-start | bytes 6291460
  150.8 7.8 %collective-permute-start.23 = (bf16[4,3,16,512]{3,2,1,0:T(8,128)(2,1)S(1)}, bf16[4,3,16,512]{3,2,1,0:T(8,128)(2,1)S(1)}, u32[]{:S(2)}, u32[]{:S(2)}) collective-permute-start(bf16[4,3,16,512]{3,2,1,0:T(8,128)(2,1)S(1)} %get-tuple-element.154), channel_id=1, source_target_pairs={{0,2},{1,3},{2,0},{3,1},{4,6},{5,7},{6,4},{7,5},{8,10},{9,11},{10,... | collective-permute-start | bytes 589832 | tf_op jit(solution)/shard_map/ppermute | solution.py:54
  151.8 9.4 %collective-permute-start.24 = (bf16[4,3,16,512]{3,2,1,0:T(8,128)(2,1)S(1)}, bf16[4,3,16,512]{3,2,1,0:T(8,128)(2,1)S(1)}, u32[]{:S(2)}, u32[]{:S(2)}) collective-permute-start(bf16[4,3,16,512]{3,2,1,0:T(8,128)(2,1)S(1)} %get-tuple-element.155), channel_id=1, source_target_pairs={{0,4},{1,5},{2,6},{3,7},{4,0},{5,1},{6,2},{7,3},{8,12},{9,13},{10,... | collective-permute-start | bytes 589832 | tf_op jit(solution)/shard_map/ppermute | solution.py:54
  153.0 9.5 %collective-permute-start.25 = (bf16[4,3,16,512]{3,2,1,0:T(8,128)(2,1)S(1)}, bf16[4,3,16,512]{3,2,1,0:T(8,128)(2,1)S(1)}, u32[]{:S(2)}, u32[]{:S(2)}) collective-permute-start(bf16[4,3,16,512]{3,2,1,0:T(8,128)(2,1)S(1)} %get-tuple-element.156), channel_id=1, source_target_pairs={{0,6},{1,7},{2,4},{3,5},{4,2},{5,3},{6,0},{7,1},{8,14},{9,15},{10,... | collective-permute-start | bytes 589832 | tf_op jit(solution)/shard_map/ppermute | solution.py:54
  158.6 9.3 %collective-permute-start.31 = (bf16[11,16,512]{2,1,0:T(8,128)(2,1)S(1)}, bf16[11,16,512]{2,1,0:T(8,128)(2,1)S(1)}, u32[]{:S(2)}, u32[]{:S(2)}) collective-permute-start(bf16[11,16,512]{2,1,0:T(8,128)(2,1)S(1)} %get-tuple-element.199), channel_id=1, source_target_pairs={{0,8},{1,9},{2,10},{3,11},{4,12},{5,13},{6,14},{7,15},{8,0},{9,1},... | collective-permute-start | bytes 540680 | tf_op jit(solution)/shard_map/ppermute | solution.py:54
  163.3 5.9 %collective-permute-start.26 = (bf16[3,16,512]{2,1,0:T(8,128)(2,1)S(1)}, bf16[3,16,512]{2,1,0:T(8,128)(2,1)S(1)}, u32[]{:S(2)}, u32[]{:S(2)}) collective-permute-start(bf16[3,16,512]{2,1,0:T(8,128)(2,1)S(1)} %get-tuple-element.209), channel_id=1, source_target_pairs={{0,24},{1,25},{2,26},{3,27},{4,28},{5,29},{6,30},{7,31},{8,16},{9,... | collective-permute-start | bytes 147464 | tf_op jit(solution)/shard_map/ppermute | solution.py:54
  165.7 5.5 %collective-permute-start.27 = (bf16[3,16,512]{2,1,0:T(8,128)(2,1)S(1)}, bf16[3,16,512]{2,1,0:T(8,128)(2,1)S(1)}, u32[]{:S(2)}, u32[]{:S(2)}) collective-permute-start(bf16[3,16,512]{2,1,0:T(8,128)(2,1)S(1)} %get-tuple-element.208), channel_id=1, source_target_pairs={{0,16},{1,17},{2,18},{3,19},{4,20},{5,21},{6,22},{7,23},{8,24},{9,... | collective-permute-start | bytes 147464 | tf_op jit(solution)/shard_map/ppermute | solution.py:54
  165.8 5.4 %copy-start.15 = (bf16[11,16,512]{2,1,0:T(8,128)(2,1)}, bf16[11,16,512]{2,1,0:T(8,128)(2,1)S(1)}, u32[]{:S(2)}) copy-start(bf16[11,16,512]{2,1,0:T(8,128)(2,1)S(1)} %collective-permute-done.29.refs_5_) | copy-start | bytes 540676
  165.8 5.4 %collective-permute-start.28 = (bf16[3,16,512]{2,1,0:T(8,128)(2,1)S(1)}, bf16[3,16,512]{2,1,0:T(8,128)(2,1)S(1)}, u32[]{:S(2)}, u32[]{:S(2)}) collective-permute-start(bf16[3,16,512]{2,1,0:T(8,128)(2,1)S(1)} %get-tuple-element.207), channel_id=1, source_target_pairs={{0,8},{1,9},{2,10},{3,11},{4,12},{5,13},{6,14},{7,15},{8,0},{9,1},... | collective-permute-start | bytes 147464 | tf_op jit(solution)/shard_map/ppermute | solution.py:54
  167.7 3.6 %copy-start.16 = (bf16[11,16,512]{2,1,0:T(8,128)(2,1)}, bf16[11,16,512]{2,1,0:T(8,128)(2,1)S(1)}, u32[]{:S(2)}) copy-start(bf16[11,16,512]{2,1,0:T(8,128)(2,1)S(1)} %collective-permute-done.30.refs_6_) | copy-start | bytes 540676
  167.9 3.4 %copy-start.17 = (bf16[11,16,512]{2,1,0:T(8,128)(2,1)}, bf16[11,16,512]{2,1,0:T(8,128)(2,1)S(1)}, u32[]{:S(2)}) copy-start(bf16[11,16,512]{2,1,0:T(8,128)(2,1)S(1)} %collective-permute-done.31.refs_7_) | copy-start | bytes 540676
  169.2 2.1 %copy-start.19 = (bf16[3,16,512]{2,1,0:T(8,128)(2,1)}, bf16[3,16,512]{2,1,0:T(8,128)(2,1)S(1)}, u32[]{:S(2)}) copy-start(bf16[3,16,512]{2,1,0:T(8,128)(2,1)S(1)} %collective-permute-done.26.refs_1_) | copy-start | bytes 147460
  171.2 0.6 copy-start.20
  171.2 0.6 copy-start.21
  174.1 1.4 collective-permute-start.32
  176.2 3.9 %collective-permute-start.33 = (f32[12,512]{1,0:T(8,128)S(1)}, f32[12,512]{1,0:T(8,128)S(1)}, u32[]{:S(2)}, u32[]{:S(2)}) collective-permute-start(f32[12,512]{1,0:T(8,128)S(1)} %add.220), channel_id=1, source_target_pairs={{0,2},{1,3},{2,0},{3,1},{4,6},{5,7},{6,4},{7,5},{8,10},{9,11},{10,... | collective-permute-start | bytes 73736 | tf_op jit(solution)/shard_map/ppermute | solution.py:54
  177.2 3.9 %collective-permute-start.34 = (f32[12,512]{1,0:T(8,128)S(1)}, f32[12,512]{1,0:T(8,128)S(1)}, u32[]{:S(2)}, u32[]{:S(2)}) collective-permute-start(f32[12,512]{1,0:T(8,128)S(1)} %add.220), channel_id=1, source_target_pairs={{0,4},{1,5},{2,6},{3,7},{4,0},{5,1},{6,2},{7,3},{8,12},{9,13},{10,... | collective-permute-start | bytes 73736 | tf_op jit(solution)/shard_map/ppermute | solution.py:54
  178.5 4.8 %collective-permute-start.35 = (f32[12,512]{1,0:T(8,128)S(1)}, f32[12,512]{1,0:T(8,128)S(1)}, u32[]{:S(2)}, u32[]{:S(2)}) collective-permute-start(f32[12,512]{1,0:T(8,128)S(1)} %add.220), channel_id=1, source_target_pairs={{0,6},{1,7},{2,4},{3,5},{4,2},{5,3},{6,0},{7,1},{8,14},{9,15},{10,... | collective-permute-start | bytes 73736 | tf_op jit(solution)/shard_map/ppermute | solution.py:54
  183.3 8.3 %copy-start.18 = (f32[12,512]{1,0:T(8,128)}, f32[12,512]{1,0:T(8,128)S(1)}, u32[]{:S(2)}) copy-start(f32[12,512]{1,0:T(8,128)S(1)} %add_add_fusion.refs_0_) | copy-start | bytes 73732
  183.3 4.5 %collective-permute-start.36 = (f32[12,512]{1,0:T(8,128)S(1)}, f32[12,512]{1,0:T(8,128)S(1)}, u32[]{:S(2)}, u32[]{:S(2)}) collective-permute-start(f32[12,512]{1,0:T(8,128)S(1)} %add_add_fusion.refs_0_), channel_id=1, source_target_pairs={{0,8},{1,9},{2,10},{3,11},{4,12},{5,13},{6,14},{7,15},{8,0},{9,1},... | collective-permute-start | bytes 73736 | tf_op jit(solution)/shard_map/ppermute | solution.py:54
  183.9 5.0 %collective-permute-start.37 = (f32[12,512]{1,0:T(8,128)S(1)}, f32[12,512]{1,0:T(8,128)S(1)}, u32[]{:S(2)}, u32[]{:S(2)}) collective-permute-start(f32[12,512]{1,0:T(8,128)S(1)} %add_add_fusion.refs_0_), channel_id=1, source_target_pairs={{0,16},{1,17},{2,18},{3,19},{4,20},{5,21},{6,22},{7,23},{8,24},{9,... | collective-permute-start | bytes 73736 | tf_op jit(solution)/shard_map/ppermute | solution.py:54
  185.9 5.7 %collective-permute-start.38 = (f32[12,512]{1,0:T(8,128)S(1)}, f32[12,512]{1,0:T(8,128)S(1)}, u32[]{:S(2)}, u32[]{:S(2)}) collective-permute-start(f32[12,512]{1,0:T(8,128)S(1)} %add_add_fusion.refs_0_), channel_id=1, source_target_pairs={{0,24},{1,25},{2,26},{3,27},{4,28},{5,29},{6,30},{7,31},{8,16},{9,... | collective-permute-start | bytes 73736 | tf_op jit(solution)/shard_map/ppermute | solution.py:54
  187.8 3.8 %copy-start.22 = (f32[12,512]{1,0:T(8,128)}, f32[12,512]{1,0:T(8,128)S(1)}, u32[]{:S(2)}) copy-start(f32[12,512]{1,0:T(8,128)S(1)} %collective-permute-done.36.refs_1_) | copy-start | bytes 73732
  188.9 2.7 %copy-start.23 = (f32[12,512]{1,0:T(8,128)}, f32[12,512]{1,0:T(8,128)S(1)}, u32[]{:S(2)}) copy-start(f32[12,512]{1,0:T(8,128)S(1)} %collective-permute-done.37.refs_2_) | copy-start | bytes 73732
  191.6 0.6 copy-start.24
